TPU v7x, 32 devices: a whole 2x2x4 slice. The times are simulated.
32 devices in a mesh: dp: 2 (over y), ep: 4 (over x, core), tp: 4 (over z).
Axes of the slice: x: 2, y: 2, z: 4, core: 2. Of those that a mesh axis runs over, the one named last changes fastest.
Arguments:
- layer_input: bfloat16 [4096, 2048], P(('dp', 'ep', 'tp')), may hold values from -6 to 6
- cotangent: bfloat16 [4096, 2048], P(('dp', 'ep', 'tp')), may hold values from -6 to 6
- lengths: int32 [8], replicated, may hold values from 256 to 512, as said below
- seq_order: int32 [8], replicated, may hold values from 0 to 7, each once
- routes: int32 [4096, 4], P(('dp', 'ep')), may hold values from 0 to 7, all different within a row; in each aligned block of 512 rows (0 to 511, 512 to 1023, ...) at most 384 rows name the same one
- query_weight: bfloat16 [2048, 2048], P(('dp', 'ep'), 'tp'), may hold values from -0.125 to 0.125
- key_weight: bfloat16 [2048, 2048], P(('dp', 'ep'), 'tp'), may hold values from -0.125 to 0.125
- value_weight: bfloat16 [2048, 2048], P(('dp', 'ep'), 'tp'), may hold values from -0.125 to 0.125
- mixing_weight: bfloat16 [2048, 2048], P('tp', ('dp', 'ep')), may hold values from -0.5 to 0.5
- heads_bias: bfloat16 [3, 16, 128], P(None, 'tp', ('dp', 'ep')), may hold values from -3 to 3
- entry_gain: bfloat16 [2048], P(('dp', 'ep')), may hold values from 0.099609375 to 1.8984375
- middle_gain: bfloat16 [2048], P(('dp', 'ep')), may hold values from 0.099609375 to 1.8984375
- router_weight: bfloat16 [2048, 8], P(('dp', 'ep')), may hold values from -0.0625 to 0.0625
- shared_switch: bfloat16 [2048], P(('dp', 'ep')), may hold values from -0.125 to 0.125
- shared_gate: bfloat16 [2048, 5632], P(('dp', 'ep'), 'tp'), may hold values from -0.125 to 0.125
- shared_up: bfloat16 [2048, 5632], P(('dp', 'ep'), 'tp'), may hold values from -0.125 to 0.125
- shared_down: bfloat16 [5632, 2048], P('tp', ('dp', 'ep')), may hold values from -0.15625 to 0.15625
- expert_gate: bfloat16 [8, 2048, 1408], P('ep', None, 'tp'), may hold values from -0.125 to 0.125
- expert_up: bfloat16 [8, 2048, 1408], P('ep', None, 'tp'), may hold values from -0.125 to 0.125
- expert_down: bfloat16 [8, 1408, 2048], P('ep', 'tp'), may hold values from -1.25 to 1.25
Outputs:
- layer_output: bfloat16 [4096, 2048], P(('dp', 'ep', 'tp'))
- input_gradient: float32 [4096, 2048], P(('dp', 'ep', 'tp'))
- query_gradient: float32 [2048, 2048], P(('dp', 'ep'), 'tp')
- key_gradient: float32 [2048, 2048], P(('dp', 'ep'), 'tp')
- value_gradient: float32 [2048, 2048], P(('dp', 'ep'), 'tp')
- mixing_gradient: float32 [2048, 2048], P('tp', ('dp', 'ep'))
- bias_gradient: float32 [3, 16, 128], P(None, 'tp', ('dp', 'ep'))
- entry_gradient: float32 [2048], P(('dp', 'ep'))
- middle_gradient: float32 [2048], P(('dp', 'ep'))
- router_gradient: float32 [2048, 8], P(('dp', 'ep'))
- switch_gradient: float32 [2048], P(('dp', 'ep'))
- shared_gate_gradient: float32 [2048, 5632], P(('dp', 'ep'), 'tp')
- shared_up_gradient: float32 [2048, 5632], P(('dp', 'ep'), 'tp')
- shared_down_gradient: float32 [5632, 2048], P('tp', ('dp', 'ep'))
- expert_gate_gradient: float32 [8, 2048, 1408], P('ep', None, 'tp')
- expert_up_gradient: float32 [8, 2048, 1408], P('ep', None, 'tp')
- expert_down_gradient: float32 [8, 1408, 2048], P('ep', 'tp')
Inputs may be any that keep to these rules, and one draw needn't show every extreme that they name: `lengths`: some sequence has exactly 512 tokens. `seq_order`: each group receives exactly one sequence. `routes`: the 4 experts of a row differ. In the rows of each group (aligned blocks of 512 rows) no expert is named more than 384 times, a bound that some block reaches.
All inputs are finite; a program needn't handle non-finite values.
Results may differ from a plain program's by a relative error of at most 0.04.
Values may be sent and summed in bfloat16 or wider, within the bound.
No kernel may reach another device: no remote copies, remote signals or barrier semaphores. Data moves between devices by JAX's collectives and lax.ppermute only.
A program may use at most 320 MiB of HBM per device.

v0:
```python
import jax
import jax.numpy as jnp
from jax import lax
from jax.sharding import PartitionSpec as P

HD = 128
TOP = 4


EPS = 1e-06
THETA = 1000000.0


def norm_parts(values):
    inverse = lax.rsqrt(jnp.mean(values * values, axis=-1, keepdims=True) + EPS)
    return (values * inverse, inverse)


def norm_back(grad_normed, gain_vector, unit_rows, inverse):
    scaled = grad_normed * gain_vector
    return inverse * (scaled - unit_rows * jnp.mean(scaled * unit_rows, axis=-1, keepdims=True))


def rotate(values):
    middle = values.shape[-1] // 2
    return jnp.concatenate([-values[..., middle:], values[..., :middle]], axis=-1)


def unrotate(values):
    middle = values.shape[-1] // 2
    return jnp.concatenate([values[..., middle:], -values[..., :middle]], axis=-1)


def rope_tables(row_total):
    position = jnp.arange(row_total).astype(jnp.float32)
    freqs = THETA ** (-(jnp.arange(HD // 2).astype(jnp.float32) * 2.0) / HD)
    angles = position[:, None] * freqs[None, :]
    angles = jnp.concatenate([angles, angles], axis=-1)
    return (jnp.cos(angles)[:, None, :], jnp.sin(angles)[:, None, :])


def silu_parts(values):
    sigmoid = jax.nn.sigmoid(values)
    return (values * sigmoid, sigmoid * (1.0 + values * (1.0 - sigmoid)))


def body(
    layer_input,
    cotangent,
    lengths,
    seq_order,
    routes,
    query_weight,
    key_weight,
    value_weight,
    mixing_weight,
    heads_bias,
    entry_gain,
    middle_gain,
    router_weight,
    shared_switch,
    shared_gate,
    shared_up,
    shared_down,
    expert_gate,
    expert_up,
    expert_down,
):
    slab_count = lax.axis_size("tp")
    owner_count = lax.axis_size("ep")
    own_rows = layer_input.shape[0]
    group_rows = own_rows * slab_count
    slab_index = lax.axis_index("tp")
    group_index = lax.axis_index(("dp", "ep"))
    length = jnp.take(lengths, jnp.take(seq_order, group_index))
    row_keep = (jnp.arange(group_rows) < length).astype(jnp.float32)
    keep_column = row_keep[:, None]
    dense_full = (
        lax.all_gather(query_weight, ("dp", "ep"), axis=0, tiled=True),
        lax.all_gather(key_weight, ("dp", "ep"), axis=0, tiled=True),
        lax.all_gather(value_weight, ("dp", "ep"), axis=0, tiled=True),
        lax.all_gather(mixing_weight, ("dp", "ep"), axis=1, tiled=True),
        lax.all_gather(heads_bias, ("dp", "ep"), axis=2, tiled=True),
        lax.all_gather(entry_gain, ("dp", "ep"), axis=0, tiled=True),
        lax.all_gather(middle_gain, ("dp", "ep"), axis=0, tiled=True),
        lax.all_gather(router_weight, ("dp", "ep"), axis=0, tiled=True),
        lax.all_gather(shared_switch, ("dp", "ep"), axis=0, tiled=True),
        lax.all_gather(shared_gate, ("dp", "ep"), axis=0, tiled=True),
        lax.all_gather(shared_up, ("dp", "ep"), axis=0, tiled=True),
        lax.all_gather(shared_down, ("dp", "ep"), axis=1, tiled=True),
    )
    query_full = dense_full[0]
    key_full = dense_full[1]
    value_full = dense_full[2]
    mixing_full = dense_full[3]
    bias_full = dense_full[4]
    entry_full = dense_full[5].astype(jnp.float32)
    middle_full = dense_full[6].astype(jnp.float32)
    router_full = dense_full[7]
    switch_full = dense_full[8]
    gate_full = dense_full[9]
    up_full = dense_full[10]
    down_full = dense_full[11]
    head_cols = query_full.shape[1]
    head_count = head_cols // HD
    bias_flat = bias_full.reshape(3, head_cols).astype(jnp.float32)
    gathered = lax.all_gather(layer_input, "tp", axis=0, tiled=True)
    input_values = gathered.astype(jnp.float32)
    entry_unit, entry_inverse = norm_parts(input_values)
    entry_normed = (entry_unit * entry_full).astype(jnp.bfloat16)
    query_lin = jnp.dot(entry_normed, query_full, preferred_element_type=jnp.float32) + bias_flat[0]
    key_lin = jnp.dot(entry_normed, key_full, preferred_element_type=jnp.float32) + bias_flat[1]
    value_lin = jnp.dot(entry_normed, value_full, preferred_element_type=jnp.float32) + bias_flat[2]
    cosine, sine = rope_tables(group_rows)
    query_heads = query_lin.reshape(group_rows, head_count, HD)
    key_heads = key_lin.reshape(group_rows, head_count, HD)
    query_rot = (query_heads * cosine + rotate(query_heads) * sine).astype(jnp.bfloat16)
    key_rot = (key_heads * cosine + rotate(key_heads) * sine).astype(jnp.bfloat16)
    value_heads = value_lin.astype(jnp.bfloat16).reshape(group_rows, head_count, HD)
    score_scale = HD ** (-0.5)
    causal = jnp.arange(group_rows)[:, None] >= jnp.arange(group_rows)[None, :]

    def score_matrix():
        raw_scores = jnp.einsum(
            "qhd,khd->hqk", query_rot, key_rot, preferred_element_type=jnp.float32
        )
        return jnp.where(causal[None], raw_scores * score_scale, -1e30)

    scores = score_matrix()
    top_score = jnp.max(scores, axis=-1, keepdims=True)
    log_total = top_score + jnp.log(jnp.sum(jnp.exp(scores - top_score), axis=-1, keepdims=True))
    attn_probs = jnp.exp(scores - log_total).astype(jnp.bfloat16)
    context = jnp.einsum(
        "hqk,khd->qhd", attn_probs, value_heads, preferred_element_type=jnp.float32
    )
    context_low = context.astype(jnp.bfloat16).reshape(group_rows, head_cols)
    head_terms = jnp.dot(context_low, mixing_full, preferred_element_type=jnp.float32)
    attention = lax.psum(head_terms.astype(jnp.bfloat16), "tp").astype(jnp.float32)
    hidden_state = input_values + keep_column * attention
    middle_unit, middle_inverse = norm_parts(hidden_state)
    middle_normed = (middle_unit * middle_full).astype(jnp.bfloat16)
    logits = jnp.dot(middle_normed, router_full, preferred_element_type=jnp.float32)
    expert_probs = jax.nn.softmax(logits, axis=-1)
    expert_count = router_full.shape[1]
    route_picks = (routes[:, :, None] == jnp.arange(expert_count)[None, None, :]).astype(
        jnp.float32
    )
    route_gates = keep_column * jnp.sum(expert_probs[:, None, :] * route_picks, axis=-1)
    switch_value = jax.nn.sigmoid(
        jnp.dot(middle_normed, switch_full, preferred_element_type=jnp.float32)
    )
    shared_pre_gate = jnp.dot(middle_normed, gate_full, preferred_element_type=jnp.float32)
    shared_pre_up = jnp.dot(middle_normed, up_full, preferred_element_type=jnp.float32)
    shared_act, shared_slope = silu_parts(shared_pre_gate)
    shared_hidden = (shared_act * shared_pre_up).astype(jnp.bfloat16)
    shared_terms = jnp.dot(shared_hidden, down_full, preferred_element_type=jnp.float32)
    capacity = group_rows * TOP * 3 // (2 * expert_count)
    local_experts = expert_gate.shape[0]
    width = middle_normed.shape[1]
    flat_route = routes.reshape(-1)
    route_hot = (flat_route[:, None] == jnp.arange(expert_count)[None, :]).astype(jnp.int32)
    earlier = jnp.cumsum(route_hot, axis=0) - route_hot
    slot_rank = jnp.sum(earlier * route_hot, axis=1)
    slot_of = flat_route * capacity + slot_rank
    pair_ids = jnp.arange(group_rows * TOP, dtype=jnp.int32)
    slot_pair = jnp.zeros((expert_count * capacity,), jnp.int32).at[slot_of].set(pair_ids)
    slot_used = jnp.zeros((expert_count * capacity,), jnp.int32).at[slot_of].set(1)
    slot_rows = jnp.take(middle_normed, slot_pair // TOP, axis=0)
    outgoing = jnp.where(slot_used[:, None] > 0, slot_rows, jnp.zeros_like(slot_rows))
    outgoing = outgoing.reshape(owner_count, local_experts, capacity, width)
    arrived = lax.all_to_all(outgoing, "ep", split_axis=0, concat_axis=0, tiled=True)
    expert_pre_gate = jnp.einsum(
        "sjcd,jdf->sjcf", arrived, expert_gate, preferred_element_type=jnp.float32
    )
    expert_pre_up = jnp.einsum(
        "sjcd,jdf->sjcf", arrived, expert_up, preferred_element_type=jnp.float32
    )
    expert_act, expert_slope = silu_parts(expert_pre_gate)
    expert_hidden = (expert_act * expert_pre_up).astype(jnp.bfloat16)
    expert_terms = jnp.einsum(
        "sjcf,jfd->sjcd", expert_hidden, expert_down, preferred_element_type=jnp.float32
    ).astype(jnp.bfloat16)
    returned = lax.all_to_all(expert_terms, "ep", split_axis=0, concat_axis=0, tiled=True)
    returned = returned.reshape(expert_count * capacity, width).astype(jnp.float32)
    route_values = jnp.take(returned, slot_of, axis=0).reshape(group_rows, TOP, width)
    routed_terms = jnp.sum(route_gates[:, :, None] * route_values, axis=1)
    branch_terms = (row_keep * switch_value)[:, None] * shared_terms + routed_terms
    branch_own = lax.psum_scatter(
        branch_terms.astype(jnp.bfloat16), "tp", scatter_dimension=0, tiled=True
    ).astype(jnp.float32)
    state_own = lax.dynamic_slice_in_dim(hidden_state, slab_index * own_rows, own_rows, 0)
    layer_output = (state_own + branch_own).astype(jnp.bfloat16)
    dense_back = (
        lax.all_gather(query_weight, ("dp", "ep"), axis=0, tiled=True),
        lax.all_gather(key_weight, ("dp", "ep"), axis=0, tiled=True),
        lax.all_gather(value_weight, ("dp", "ep"), axis=0, tiled=True),
        lax.all_gather(mixing_weight, ("dp", "ep"), axis=1, tiled=True),
        lax.all_gather(heads_bias, ("dp", "ep"), axis=2, tiled=True),
        lax.all_gather(entry_gain, ("dp", "ep"), axis=0, tiled=True),
        lax.all_gather(middle_gain, ("dp", "ep"), axis=0, tiled=True),
        lax.all_gather(router_weight, ("dp", "ep"), axis=0, tiled=True),
        lax.all_gather(shared_switch, ("dp", "ep"), axis=0, tiled=True),
        lax.all_gather(shared_gate, ("dp", "ep"), axis=0, tiled=True),
        lax.all_gather(shared_up, ("dp", "ep"), axis=0, tiled=True),
        lax.all_gather(shared_down, ("dp", "ep"), axis=1, tiled=True),
    )
    query_back = dense_back[0]
    key_back = dense_back[1]
    value_back = dense_back[2]
    mixing_back = dense_back[3]
    entry_back = dense_back[5].astype(jnp.float32)
    middle_back = dense_back[6].astype(jnp.float32)
    router_back = dense_back[7].astype(jnp.float32)
    switch_back = dense_back[8].astype(jnp.float32)
    gate_back = dense_back[9]
    up_back = dense_back[10]
    down_back = dense_back[11]
    upstream = lax.all_gather(cotangent, "tp", axis=0, tiled=True).astype(jnp.float32)
    shared_grad_out = (keep_column * switch_value[:, None] * upstream).astype(jnp.bfloat16)
    shared_down_grad = jnp.dot(shared_hidden.T, shared_grad_out, preferred_element_type=jnp.float32)
    shared_hidden_grad = jnp.dot(shared_grad_out, down_back.T, preferred_element_type=jnp.float32)
    shared_gate_low = (shared_hidden_grad * shared_pre_up * shared_slope).astype(jnp.bfloat16)
    shared_up_low = (shared_hidden_grad * shared_act).astype(jnp.bfloat16)
    shared_gate_grad = jnp.dot(middle_normed.T, shared_gate_low, preferred_element_type=jnp.float32)
    shared_up_grad = jnp.dot(middle_normed.T, shared_up_low, preferred_element_type=jnp.float32)
    normed_grad = jnp.dot(shared_gate_low, gate_back.T, preferred_element_type=jnp.float32)
    normed_grad = normed_grad + jnp.dot(
        shared_up_low, up_back.T, preferred_element_type=jnp.float32
    )
    switch_part = row_keep * jnp.sum(upstream * shared_terms, axis=-1)
    gate_part = jnp.sum(upstream[:, None, :] * route_values, axis=-1)
    route_grads = (route_gates[:, :, None] * upstream[:, None, :]).astype(jnp.bfloat16)
    route_grads = route_grads.reshape(group_rows * TOP, width)
    slot_grads_in = jnp.take(route_grads, slot_pair, axis=0)
    outgoing_grads = jnp.where(slot_used[:, None] > 0, slot_grads_in, jnp.zeros_like(slot_grads_in))
    outgoing_grads = outgoing_grads.reshape(owner_count, local_experts, capacity, width)
    arrived_grads = lax.all_to_all(outgoing_grads, "ep", split_axis=0, concat_axis=0, tiled=True)
    expert_down_grad = jnp.einsum(
        "sjcf,sjcd->jfd", expert_hidden, arrived_grads, preferred_element_type=jnp.float32
    )
    expert_hidden_grad = jnp.einsum(
        "sjcd,jfd->sjcf", arrived_grads, expert_down, preferred_element_type=jnp.float32
    )
    expert_gate_low = (expert_hidden_grad * expert_pre_up * expert_slope).astype(jnp.bfloat16)
    expert_up_low = (expert_hidden_grad * expert_act).astype(jnp.bfloat16)
    expert_gate_grad = jnp.einsum(
        "sjcd,sjcf->jdf", arrived, expert_gate_low, preferred_element_type=jnp.float32
    )
    expert_up_grad = jnp.einsum(
        "sjcd,sjcf->jdf", arrived, expert_up_low, preferred_element_type=jnp.float32
    )
    expert_sums = (
        lax.psum(expert_gate_grad.astype(jnp.bfloat16), "dp").astype(jnp.float32),
        lax.psum(expert_up_grad.astype(jnp.bfloat16), "dp").astype(jnp.float32),
        lax.psum(expert_down_grad.astype(jnp.bfloat16), "dp").astype(jnp.float32),
    )
    slot_back = jnp.einsum(
        "sjcf,jdf->sjcd", expert_gate_low, expert_gate, preferred_element_type=jnp.float32
    )
    slot_back = slot_back + jnp.einsum(
        "sjcf,jdf->sjcd", expert_up_low, expert_up, preferred_element_type=jnp.float32
    )
    slot_back_low = slot_back.astype(jnp.bfloat16)
    returned_grads = lax.all_to_all(slot_back_low, "ep", split_axis=0, concat_axis=0, tiled=True)
    returned_grads = returned_grads.reshape(expert_count * capacity, width).astype(jnp.float32)
    route_back = jnp.take(returned_grads, slot_of, axis=0).reshape(group_rows, TOP, width)
    normed_grad = normed_grad + jnp.sum(route_back, axis=1)
    summed = (
        lax.psum(normed_grad.astype(jnp.bfloat16), "tp").astype(jnp.float32),
        lax.psum(gate_part.astype(jnp.bfloat16), "tp").astype(jnp.float32),
        lax.psum(switch_part.astype(jnp.bfloat16), "tp").astype(jnp.float32),
    )
    normed_total = summed[0]
    gate_total = summed[1]
    switch_total = summed[2]
    prob_grad = jnp.sum((keep_column * gate_total)[:, :, None] * route_picks, axis=1)
    logit_grad = expert_probs * (
        prob_grad - jnp.sum(expert_probs * prob_grad, axis=-1, keepdims=True)
    )
    switch_grad = switch_total * switch_value * (1.0 - switch_value)
    normed_values = middle_normed.astype(jnp.float32)
    router_grad = jnp.dot(normed_values.T, logit_grad, precision=lax.Precision.HIGHEST)
    switch_weight_grad = jnp.dot(switch_grad, normed_values, precision=lax.Precision.HIGHEST)
    normed_total = normed_total + jnp.dot(
        logit_grad, router_back.T, precision=lax.Precision.HIGHEST
    )
    normed_total = normed_total + switch_grad[:, None] * switch_back[None, :]
    middle_gain_grad = jnp.sum(normed_total * middle_unit, axis=0)
    state_grad = upstream + norm_back(normed_total, middle_back, middle_unit, middle_inverse)
    attention_grad = (keep_column * state_grad).astype(jnp.bfloat16)
    mixing_grad = jnp.dot(context_low.T, attention_grad, preferred_element_type=jnp.float32)
    context_grad = jnp.dot(attention_grad, mixing_back.T, preferred_element_type=jnp.float32)
    context_grad = context_grad.astype(jnp.bfloat16).reshape(group_rows, head_count, HD)
    probs_again = jnp.exp(score_matrix() - log_total)
    probs_low = probs_again.astype(jnp.bfloat16)
    value_grad = jnp.einsum(
        "hqk,qhd->khd", probs_low, context_grad, preferred_element_type=jnp.float32
    )
    value_grad = value_grad.astype(jnp.bfloat16).reshape(group_rows, head_cols)
    prob_grads = jnp.einsum(
        "qhd,khd->hqk", context_grad, value_heads, preferred_element_type=jnp.float32
    )
    row_delta = jnp.sum(probs_again * prob_grads, axis=-1, keepdims=True)
    score_grads = (probs_again * (prob_grads - row_delta)).astype(jnp.bfloat16)
    query_rot_grad = (
        jnp.einsum("hqk,khd->qhd", score_grads, key_rot, preferred_element_type=jnp.float32)
        * score_scale
    )
    key_rot_grad = (
        jnp.einsum("hqk,qhd->khd", score_grads, query_rot, preferred_element_type=jnp.float32)
        * score_scale
    )
    query_grad = (query_rot_grad * cosine + unrotate(query_rot_grad * sine)).astype(jnp.bfloat16)
    key_grad = (key_rot_grad * cosine + unrotate(key_rot_grad * sine)).astype(jnp.bfloat16)
    query_grad = query_grad.reshape(group_rows, head_cols)
    key_grad = key_grad.reshape(group_rows, head_cols)
    bias_grad = jnp.stack(
        [
            jnp.sum(query_grad.astype(jnp.float32), axis=0),
            jnp.sum(key_grad.astype(jnp.float32), axis=0),
            jnp.sum(value_grad.astype(jnp.float32), axis=0),
        ]
    ).reshape(3, head_count, HD)
    query_weight_grad = jnp.dot(entry_normed.T, query_grad, preferred_element_type=jnp.float32)
    key_weight_grad = jnp.dot(entry_normed.T, key_grad, preferred_element_type=jnp.float32)
    value_weight_grad = jnp.dot(entry_normed.T, value_grad, preferred_element_type=jnp.float32)
    entry_part = jnp.dot(query_grad, query_back.T, preferred_element_type=jnp.float32)
    entry_part = entry_part + jnp.dot(key_grad, key_back.T, preferred_element_type=jnp.float32)
    entry_part = entry_part + jnp.dot(value_grad, value_back.T, preferred_element_type=jnp.float32)
    entry_total = lax.psum(entry_part.astype(jnp.bfloat16), "tp").astype(jnp.float32)
    entry_gain_grad = jnp.sum(entry_total * entry_unit, axis=0)
    input_full_grad = state_grad + norm_back(entry_total, entry_back, entry_unit, entry_inverse)
    input_gradient = lax.dynamic_slice_in_dim(input_full_grad, slab_index * own_rows, own_rows, 0)
    weight_sums = (
        lax.psum_scatter(
            query_weight_grad.astype(jnp.bfloat16), ("dp", "ep"), scatter_dimension=0, tiled=True
        ).astype(jnp.float32),
        lax.psum_scatter(
            key_weight_grad.astype(jnp.bfloat16), ("dp", "ep"), scatter_dimension=0, tiled=True
        ).astype(jnp.float32),
        lax.psum_scatter(
            value_weight_grad.astype(jnp.bfloat16), ("dp", "ep"), scatter_dimension=0, tiled=True
        ).astype(jnp.float32),
        lax.psum_scatter(
            mixing_grad.astype(jnp.bfloat16), ("dp", "ep"), scatter_dimension=1, tiled=True
        ).astype(jnp.float32),
        lax.psum_scatter(
            bias_grad.astype(jnp.bfloat16), ("dp", "ep"), scatter_dimension=2, tiled=True
        ).astype(jnp.float32),
        lax.psum_scatter(
            entry_gain_grad.astype(jnp.bfloat16), ("dp", "ep"), scatter_dimension=0, tiled=True
        ).astype(jnp.float32),
        lax.psum_scatter(
            middle_gain_grad.astype(jnp.bfloat16), ("dp", "ep"), scatter_dimension=0, tiled=True
        ).astype(jnp.float32),
        lax.psum_scatter(
            router_grad.astype(jnp.bfloat16), ("dp", "ep"), scatter_dimension=0, tiled=True
        ).astype(jnp.float32),
        lax.psum_scatter(
            switch_weight_grad.astype(jnp.bfloat16), ("dp", "ep"), scatter_dimension=0, tiled=True
        ).astype(jnp.float32),
        lax.psum_scatter(
            shared_gate_grad.astype(jnp.bfloat16), ("dp", "ep"), scatter_dimension=0, tiled=True
        ).astype(jnp.float32),
        lax.psum_scatter(
            shared_up_grad.astype(jnp.bfloat16), ("dp", "ep"), scatter_dimension=0, tiled=True
        ).astype(jnp.float32),
        lax.psum_scatter(
            shared_down_grad.astype(jnp.bfloat16), ("dp", "ep"), scatter_dimension=1, tiled=True
        ).astype(jnp.float32),
    )
    return (
        layer_output,
        input_gradient,
        weight_sums[0],
        weight_sums[1],
        weight_sums[2],
        weight_sums[3],
        weight_sums[4],
        weight_sums[5],
        weight_sums[6],
        weight_sums[7],
        weight_sums[8],
        weight_sums[9],
        weight_sums[10],
        weight_sums[11],
        expert_sums[0],
        expert_sums[1],
        expert_sums[2],
    )


def solution(mesh):
    return jax.shard_map(
        body,
        mesh=mesh,
        in_specs=(
            P(("dp", "ep", "tp"), None),
            P(("dp", "ep", "tp"), None),
            P(),
            P(),
            P(("dp", "ep"), None),
            P(("dp", "ep"), "tp"),
            P(("dp", "ep"), "tp"),
            P(("dp", "ep"), "tp"),
            P("tp", ("dp", "ep")),
            P(None, "tp", ("dp", "ep")),
            P(("dp", "ep")),
            P(("dp", "ep")),
            P(("dp", "ep"), None),
            P(("dp", "ep")),
            P(("dp", "ep"), "tp"),
            P(("dp", "ep"), "tp"),
            P("tp", ("dp", "ep")),
            P("ep", None, "tp"),
            P("ep", None, "tp"),
            P("ep", "tp", None),
        ),
        out_specs=(
            P(("dp", "ep", "tp"), None),
            P(("dp", "ep", "tp"), None),
            P(("dp", "ep"), "tp"),
            P(("dp", "ep"), "tp"),
            P(("dp", "ep"), "tp"),
            P("tp", ("dp", "ep")),
            P(None, "tp", ("dp", "ep")),
            P(("dp", "ep")),
            P(("dp", "ep")),
            P(("dp", "ep"), None),
            P(("dp", "ep")),
            P(("dp", "ep"), "tp"),
            P(("dp", "ep"), "tp"),
            P("tp", ("dp", "ep")),
            P("ep", None, "tp"),
            P("ep", None, "tp"),
            P("ep", "tp", None),
        ),
        check_vma=False,
    )
```

profile of v0, /device:TPU:0, one launch (start us, length us, event | category | flops | bytes accessed | tf_op | source)
XLA Modules:
  0.0 2194.8 jit_solution(12488172921909447957)
XLA Ops:
  11.6 10.7 all_gather.56
  33.9 24.3 %all-gather.13.cloned.1.call-done = bf16[512,2048]{1,0:T(8,128)(2,1)} async-done(((bf16[128,2048]{1,0:T(8,128)(2,1)}), bf16[512,2048]{1,0:T(8,128)(2,1)}) %all-gather.13.cloned.1.call-update) | async-done | bytes 2097168 | tf_op jit(solution)/shard_map/all_gather | solution.py:107
  60.4 26.4 %all-gather.19.cloned.1.call-done = bf16[2048,512]{1,0:T(8,128)(2,1)} async-done(((bf16[256,512]{1,0:T(8,128)(2,1)}), bf16[2048,512]{1,0:T(8,128)(2,1)}) %all-gather.19.cloned.1.call-update) | async-done | bytes 2097168 | tf_op jit(solution)/shard_map/all_gather | solution.py:80
  92.5 24.2 %all-gather.17.cloned.1.call-done = bf16[2048,512]{1,0:T(8,128)(2,1)} async-done(((bf16[256,512]{1,0:T(8,128)(2,1)}), bf16[2048,512]{1,0:T(8,128)(2,1)}) %all-gather.17.cloned.1.call-update) | async-done | bytes 2097168 | tf_op jit(solution)/shard_map/all_gather | solution.py:79
  125.1 21.2 all-gather.15.cloned.1.call-done
  153.0 23.2 %all-gather.21.cloned.1.call-done = bf16[512,2048]{1,0:T(8,128)(2,1)} async-done(((bf16[512,256]{1,0:T(8,128)(2,1)}), bf16[512,2048]{1,0:T(8,128)(2,1)}) %all-gather.21.cloned.1.call-update) | async-done | bytes 2097168 | tf_op jit(solution)/shard_map/all_gather | solution.py:82
  215.0 52.3 %all-reduce.11.cloned.1.call-done = bf16[512,2048]{1,0:T(8,128)(2,1)} async-done(((bf16[512,2048]{1,0:T(8,128)(2,1)}), bf16[512,2048]{1,0:T(8,128)(2,1)}) %all-reduce.11.cloned.1.call-update) | async-done | bytes 2097168 | tf_op jit(solution)/shard_map/psum | solution.py:138
  274.2 25.9 %gather_fusion = bf16[3072,2048]{1,0:T(8,128)(2,1)} fusion(bf16[512,2048]{1,0:T(8,128)(2,1)} %multiply_convert_fusion.4, s32[3072]{0:T(1024)S(1)} %get-tuple-element.93), kind=kCustom, calls=%fused_computation.2 | custom fusion | bytes 25178112 | tf_op jit(solution)/shard_map/jit(_take)/gather | solution.py:168
  300.1 10.9 select_select_fusion.1
  317.9 207.0 %all-to-all-done = bf16[4,2,384,2048]{3,2,1,0:T(8,128)(2,1)} async-done(((bf16[4,2,384,2048]{3,2,1,0:T(8,128)(2,1)}), bf16[4,2,384,2048]{3,2,1,0:T(8,128)(2,1)}, u32[]{:S(2)}, u32[]{:S(2)}) %all-to-all-start) | async-done | bytes 12582944 | tf_op jit(solution)/shard_map/all_to_all | solution.py:171
  533.6 11.2 fusion.12
  564.3 140.3 %all-gather.2 = bf16[8,1,256]{2,1,0:T(2,128)(2,1)S(1)} all-gather(bf16[1,1,256]{2,1,0:T(2,128)(2,1)S(1)} %reshape.463), channel_id=1, replica_groups=mesh['dp'=2,'ep'=4,'tp'=4] {'dp','ep'}, dimensions={0}, use_global_device_ids=true | all-gather | bytes 4608 | tf_op jit(solution)/shard_map/all_gather | solution.py:87
  713.9 9.9 mul.458
  723.8 19.4 mul.459
  764.4 11.0 multiply_convert_fusion.6
  780.6 14.4 bitcast_convert_fusion.1
  795.0 24.7 %gather_fusion.2 = f32[2048,2048]{1,0:T(8,128)} fusion(f32[3072,2048]{1,0:T(8,128)} %bitcast_convert_fusion.1, s32[2048]{0:T(1024)S(1)} %broadcast_clamp_fusion.1), kind=kCustom, calls=%fused_computation.clone | custom fusion | bytes 33562624 | tf_op jit(solution)/shard_map/jit(_take)/gather | solution.py:185
  819.6 18.4 multiply_reduce_fusion
  838.4 10.3 all-reduce.4
  849.7 9.3 multiply_convert_fusion
  859.0 28.3 %gather_fusion.1 = bf16[3072,2048]{1,0:T(8,128)(2,1)} fusion(bf16[2048,2048]{1,0:T(8,128)(2,1)} %multiply_convert_fusion, s32[3072]{0:T(1024)S(1)} %copy-done.56), kind=kCustom, calls=%fused_computation.3 | custom fusion | bytes 25178112 | tf_op jit(solution)/shard_map/jit(_take)/gather | solution.py:234
  894.1 142.1 %all_to_all.20 = bf16[4,2,384,2048]{3,2,1,0:T(8,128)(2,1)} all-to-all(bf16[4,2,384,2048]{3,2,1,0:T(8,128)(2,1)S(1)} %select_select_fusion), channel_id=1, replica_groups=mesh['dp'=2,'ep'=4,'tp'=4] {'ep'}, dimensions={0} | all-to-all | bytes 25165824 | tf_op jit(solution)/shard_map/all_to_all | solution.py:237
  1036.2 11.3 fusion.11
  1047.5 11.8 fusion.25
  1059.3 15.1 fusion
  1074.4 10.7 copy.130
  1099.4 130.3 %all-to-all-done.3 = bf16[4,2,384,2048]{3,2,1,0:T(8,128)(2,1)} async-done(((bf16[4,2,384,2048]{3,2,1,0:T(8,128)(2,1)}), bf16[4,2,384,2048]{3,2,1,0:T(8,128)(2,1)}, u32[]{:S(2)}, u32[]{:S(2)}) %all-to-all-start.3) | async-done | bytes 12582944 | tf_op jit(solution)/shard_map/all_to_all | solution.py:264
  1229.7 14.4 bitcast_convert_fusion
  1244.1 24.6 %gather_fusion.3 = f32[2048,2048]{1,0:T(8,128)} fusion(f32[3072,2048]{1,0:T(8,128)} %bitcast_convert_fusion, s32[2048]{0:T(1024)S(1)} %broadcast_clamp_fusion.1), kind=kCustom, calls=%fused_computation.1.clone | custom fusion | bytes 33562624 | tf_op jit(solution)/shard_map/jit(_take)/gather | solution.py:266
  1268.7 11.7 broadcast_select_fusion
  1280.4 19.0 reshape.342
  1299.4 15.1 reduce_sum.190
  1314.5 10.4 add_convert_fusion.2
  1347.0 19.0 reshape.341
  1367.6 16.4 multiply_reduce_fusion.1
  1389.5 11.1 bitcast_convert_fusion.4
  1400.6 11.0 bitcast_convert_fusion.3
  1473.3 61.2 %reduce-scatter.27.cloned.1.call-done = bf16[256,1408]{1,0:T(8,128)(2,1)} async-done(((bf16[2048,1408]{1,0:T(8,128)(2,1)}), bf16[256,1408]{1,0:T(8,128)(2,1)}) %reduce-scatter.27.cloned.1.call-update) | async-done | bytes 720912 | tf_op jit(solution)/shard_map/reduce_scatter | solution.py:365
  1536.8 60.7 %reduce-scatter.29.cloned.1.call-done = bf16[1408,256]{1,0:T(8,128)(2,1)} async-done(((bf16[1408,2048]{1,0:T(8,128)(2,1)}), bf16[1408,256]{1,0:T(8,128)(2,1)}) %reduce-scatter.29.cloned.1.call-update) | async-done | bytes 720912 | tf_op jit(solution)/shard_map/reduce_scatter | solution.py:368
  1600.7 31.1 %reduce-scatter.23.cloned.1.call-done = bf16[256,8]{0,1:T(8,128)(2,1)} async-done(((bf16[2048,8]{0,1:T(8,128)(2,1)}), bf16[256,8]{0,1:T(8,128)(2,1)}) %reduce-scatter.23.cloned.1.call-update) | async-done | bytes 4112 | tf_op jit(solution)/shard_map/reduce_scatter | solution.py:356
  1633.1 44.8 %reduce-scatter.13.cloned.1.call-done = bf16[128,2048]{1,0:T(8,128)(2,1)} async-done(((bf16[512,2048]{1,0:T(8,128)(2,1)}), bf16[128,2048]{1,0:T(8,128)(2,1)}) %reduce-scatter.13.cloned.1.call-update) | async-done | bytes 524304 | tf_op jit(solution)/shard_map/reduce_scatter | solution.py:188
  1680.1 204.4 %all-reduce.17.cloned.1.call-done = (bf16[2,2048,352]{1,2,0:T(8,128)(2,1)}, bf16[2,2048,352]{1,2,0:T(8,128)(2,1)}, bf16[2,352,2048]{2,1,0:T(8,128)(2,1)}) async-done(((bf16[2,2048,352]{1,2,0:T(8,128)(2,1)}, bf16[2,2048,352]{1,2,0:T(8,128)(2,1)}, bf16[2,352,2048]{2,1,0:T(8,128)(2,1)}), (bf16[2,2048,352]{1,2,0:T(8,128)(2,1)}, bf16[2,2048,352]{1,2,0:T(8,128)(2,1)}, ...) | async-done | bytes 8650768 | tf_op jit(solution)/shard_map/psum | solution.py:253
  1896.5 23.1 %reduce-scatter.31.cloned.1.call-done = bf16[16,12]{1,0:T(8,128)(2,1)} async-done(((bf16[128,12]{1,0:T(8,128)(2,1)}), bf16[16,12]{1,0:T(8,128)(2,1)}) %reduce-scatter.31.cloned.1.call-update) | async-done | bytes 400
  1921.0 87.5 %all-reduce.15.cloned.1.call-done = bf16[512,2048]{1,0:T(8,128)(2,1)} async-done(((bf16[512,2048]{1,0:T(8,128)(2,1)}), bf16[512,2048]{1,0:T(8,128)(2,1)}) %all-reduce.15.cloned.1.call-update) | async-done | bytes 2097168 | tf_op jit(solution)/shard_map/psum | solution.py:330
  2015.4 24.3 %all-reduce.3 = (bf16[2048]{0:T(1024)(128)(2,1)S(1)}, bf16[2048]{0:T(1024)(128)(2,1)S(1)}, bf16[2048]{0:T(1024)(128)(2,1)S(1)}) all-reduce(bf16[2048]{0:T(1024)(128)(2,1)S(1)} %get-tuple-element.42, bf16[2048]{0:T(1024)(128)(2,1)S(1)} %get-tuple-element.40, ...), channel_id=8, replica_groups=mesh['dp'=2,'ep'=4,'tp'=4] {'dp','ep'}, use_global_device_ids=true, to_apply=%region_36.38.clone | all-reduce | flops 6144 | bytes 24576
  2054.1 42.7 %reduce-scatter.17.cloned.1.call-done = bf16[256,512]{1,0:T(8,128)(2,1)} async-done(((bf16[2048,512]{1,0:T(8,128)(2,1)}), bf16[256,512]{1,0:T(8,128)(2,1)}) %reduce-scatter.17.cloned.1.call-update) | async-done | bytes 262160 | tf_op jit(solution)/shard_map/reduce_scatter | solution.py:338
  2098.6 43.1 %reduce-scatter.19.cloned.1.call-done = bf16[256,512]{1,0:T(8,128)(2,1)} async-done(((bf16[2048,512]{1,0:T(8,128)(2,1)}), bf16[256,512]{1,0:T(8,128)(2,1)}) %reduce-scatter.19.cloned.1.call-update) | async-done | bytes 262160 | tf_op jit(solution)/shard_map/reduce_scatter | solution.py:341
  2143.5 42.8 %reduce-scatter.21.cloned.1.call-done = bf16[512,256]{1,0:T(8,128)(2,1)} async-done(((bf16[512,2048]{1,0:T(8,128)(2,1)}), bf16[512,256]{1,0:T(8,128)(2,1)}) %reduce-scatter.21.cloned.1.call-update) | async-done | bytes 262160 | tf_op jit(solution)/shard_map/reduce_scatter | solution.py:344
  (389 shorter events, 314.2 us)
Async XLA Ops:
  7.2 537.7 %copy-start = (bf16[2,352,2048]{2,1,0:T(8,128)(2,1)S(1)}, bf16[2,352,2048]{2,1,0:T(8,128)(2,1)}, u32[]{:S(2)}) copy-start(bf16[2,352,2048]{2,1,0:T(8,128)(2,1)} %param.41) | copy-start | bytes 8650756
  7.2 51.1 %all-gather.13.cloned.1.call-start = ((), (), s32[]{:S(2)}) async-start(), calls=%async_computation.14 | async-start | bytes 2621440 | tf_op jit(solution)/shard_map/all_gather | solution.py:107
  7.9 78.9 %all-gather.19.cloned.1.call-start = ((), (), s32[]{:S(2)}) async-start(), calls=%async_computation.17 | async-start | bytes 2359296 | tf_op jit(solution)/shard_map/all_gather | solution.py:80
  8.7 107.9 %all-gather.17.cloned.1.call-start = ((), (), s32[]{:S(2)}) async-start(), calls=%async_computation.16 | async-start | bytes 2359296 | tf_op jit(solution)/shard_map/all_gather | solution.py:79
  9.4 136.9 %all-gather.15.cloned.1.call-start = ((), (), s32[]{:S(2)}) async-start(), calls=%async_computation.15 | async-start | bytes 2359296 | tf_op jit(solution)/shard_map/all_gather | solution.py:81
  10.0 166.3 %all-gather.21.cloned.1.call-start = ((), (), s32[]{:S(2)}) async-start(), calls=%async_computation.18 | async-start | bytes 2359296 | tf_op jit(solution)/shard_map/all_gather | solution.py:82
  10.6 256.7 %all-reduce.11.cloned.1.call-start = ((), (), s32[]{:S(2)}) async-start(), calls=%async_computation.19 | async-start | bytes 4194304 | tf_op jit(solution)/shard_map/psum | solution.py:138
  10.7 139.4 %copy-start.11 = (pred[512,512]{0,1:T(8,128)(4,1)}, pred[512,512]{0,1:T(8,128)(4,1)S(1)}, u32[]{:S(2)}) copy-start(pred[512,512]{0,1:T(8,128)(4,1)S(1)} %iota_compare_fusion) | copy-start | bytes 786436
  32.0 114.3 %copy-start.57 = (f32[8,1,256]{2,1,0:T(1,128)}, f32[8,1,256]{2,1,0:T(1,128)S(1)}, u32[]{:S(2)}) copy-start(f32[8,1,256]{2,1,0:T(1,128)S(1)} %convert_element_type.383) | copy-start | bytes 24580
  60.4 85.9 %copy-start.73 = (f32[512]{0:T(512)}, f32[512]{0:T(512)S(1)}, u32[]{:S(2)}) copy-start(f32[512]{0:T(512)S(1)} %add_rsqrt_fusion.1) | copy-start | bytes 6148
  125.1 27.9 %copy-start.52 = (f32[4,512]{1,0:T(4,128)}, f32[4,512]{1,0:T(4,128)S(1)}, u32[]{:S(2)}) copy-start(f32[4,512]{1,0:T(4,128)S(1)} %log_add_fusion) | copy-start | bytes 24580
  180.7 533.2 %all-gather.29.cloned.1.call-start = ((), (), s32[]{:S(2)}) async-start(), calls=%async_computation.24 | async-start | bytes 2621440 | tf_op jit(solution)/shard_map/all_gather | solution.py:218
  181.4 566.4 %all-gather.23.cloned.1.call-start = ((), (), s32[]{:S(2)}) async-start(), calls=%async_computation.20 | async-start | bytes 6488064 | tf_op jit(solution)/shard_map/all_gather | solution.py:88
  182.2 574.0 %all-gather.25.cloned.1.call-start = ((), (), s32[]{:S(2)}) async-start(), calls=%async_computation.21 | async-start | bytes 6488064 | tf_op jit(solution)/shard_map/all_gather | solution.py:89
  197.9 72.5 %copy-start.61 = (f32[512]{0:T(512)}, f32[512]{0:T(512)S(1)}, u32[]{:S(2)}) copy-start(f32[512]{0:T(512)S(1)} %fusion.59) | copy-start | bytes 6148
  206.8 63.7 %copy-start.46 = (f32[8,1,256]{2,1,0:T(1,128)}, f32[8,1,256]{2,1,0:T(1,128)S(1)}, u32[]{:S(2)}) copy-start(f32[8,1,256]{2,1,0:T(1,128)S(1)} %convert_element_type.384) | copy-start | bytes 24580
  215.0 85.1 %copy-start.54 = (pred[4,2,384]{2,1,0:T(4,128)(4,1)}, pred[4,2,384]{2,1,0:T(4,128)(4,1)S(1)}, u32[]{:S(2)}) copy-start(pred[4,2,384]{2,1,0:T(4,128)(4,1)S(1)} %broadcast_in_dim.119) | copy-start | bytes 9220
  270.5 29.6 %copy-start.64 = (f32[512]{0:T(512)}, f32[512]{0:T(512)S(1)}, u32[]{:S(2)}) copy-start(f32[512]{0:T(512)S(1)} %add_rsqrt_fusion) | copy-start | bytes 6148
  311.0 213.9 %all-to-all-start = ((bf16[4,2,384,2048]{3,2,1,0:T(8,128)(2,1)}), bf16[4,2,384,2048]{3,2,1,0:T(8,128)(2,1)}, u32[]{:S(2)}, u32[]{:S(2)}) async-start(bf16[4,2,384,2048]{3,2,1,0:T(8,128)(2,1)} %select_select_fusion.1), calls=%async_computation | async-start | bytes 25165824 | tf_op jit(solution)/shard_map/all_to_all | solution.py:171
  317.3 447.0 %all-gather.27.cloned.1.call-start = ((), (), s32[]{:S(2)}) async-start(), calls=%async_computation.22 | async-start | bytes 6488064 | tf_op jit(solution)/shard_map/all_gather | solution.py:90
  557.3 147.3 %copy-start.77 = (bf16[256,8]{0,1:T(8,128)(2,1)S(1)}, bf16[256,8]{0,1:T(8,128)(2,1)}, u32[]{:S(2)}) copy-start(bf16[256,8]{0,1:T(8,128)(2,1)} %param.34) | copy-start | bytes 12292
  557.3 223.3 %all-to-all-start.1 = ((bf16[4,2,384,2048]{3,2,1,0:T(8,128)(2,1)}), bf16[4,2,384,2048]{3,2,1,0:T(8,128)(2,1)}, u32[]{:S(2)}, u32[]{:S(2)}) async-start(bf16[4,2,384,2048]{3,2,1,0:T(8,128)(2,1)} %copy.127), calls=%async_computation.1 | async-start | bytes 25165824 | tf_op jit(solution)/shard_map/all_to_all | solution.py:183
  704.6 40.9 %copy-start.48 = (bf16[8,1,256]{2,1,0:T(2,128)(2,1)}, bf16[8,1,256]{2,1,0:T(2,128)(2,1)S(1)}, u32[]{:S(2)}) copy-start(bf16[8,1,256]{2,1,0:T(2,128)(2,1)S(1)} %all-gather.2) | copy-start | bytes 12292
  713.8 29.4 %copy-start.39 = (bf16[2048,8]{0,1:T(8,128)(2,1)}, bf16[2048,8]{0,1:T(8,128)(2,1)S(1)}, u32[]{:S(2)}) copy-start(bf16[2048,8]{0,1:T(8,128)(2,1)S(1)} %all_gather.65) | copy-start | bytes 98308
  713.8 105.8 %copy-start.67 = (pred[2048]{0:T(1024)(128)(4,1)}, pred[2048]{0:T(1024)(128)(4,1)S(1)}, u32[]{:S(2)}) copy-start(pred[2048]{0:T(1024)(128)(4,1)S(1)} %compare_and_fusion.2) | copy-start | bytes 6148
  747.8 100.9 %copy-start.41 = (f32[512,8]{0,1:T(8,128)}, f32[512,8]{0,1:T(8,128)S(1)}, u32[]{:S(2)}) copy-start(f32[512,8]{0,1:T(8,128)S(1)} %fusion.49) | copy-start | bytes 49156
  819.6 29.1 %copy-start.62 = (f32[512]{0:T(512)S(1)}, f32[512]{0:T(512)}, u32[]{:S(2)}) copy-start(f32[512]{0:T(512)} %copy-done.61) | copy-start | bytes 6148
  819.6 29.1 %copy-start.51 = (s32[512,4]{0,1:T(4,128)S(1)}, s32[512,4]{0,1:T(4,128)}, u32[]{:S(2)}) copy-start(s32[512,4]{0,1:T(4,128)} %param.26) | copy-start | bytes 24580
  859.0 28.3 %copy-start.55 = (pred[4,2,384]{2,1,0:T(4,128)(4,1)S(1)}, pred[4,2,384]{2,1,0:T(4,128)(4,1)}, u32[]{:S(2)}) copy-start(pred[4,2,384]{2,1,0:T(4,128)(4,1)} %copy-done.54) | copy-start | bytes 9220
  859.0 28.3 %copy-start.66 = (pred[4,2,384]{2,1,0:T(4,128)(4,1)S(1)}, pred[4,2,384]{2,1,0:T(4,128)(4,1)}, u32[]{:S(2)}) copy-start(pred[4,2,384]{2,1,0:T(4,128)(4,1)} %broadcast_in_dim.125) | copy-start | bytes 9220
  1085.1 144.6 %all-to-all-start.3 = ((bf16[4,2,384,2048]{3,2,1,0:T(8,128)(2,1)}), bf16[4,2,384,2048]{3,2,1,0:T(8,128)(2,1)}, u32[]{:S(2)}, u32[]{:S(2)}) async-start(bf16[4,2,384,2048]{3,2,1,0:T(8,128)(2,1)} %copy.130), calls=%async_computation.4 | async-start | bytes 25165824 | tf_op jit(solution)/shard_map/all_to_all | solution.py:264
  1091.6 326.8 %all-reduce.13.cloned.1.call-start = ((), (), s32[]{:S(2)}) async-start(), calls=%async_computation.25 | async-start | bytes 4194304 | tf_op jit(solution)/shard_map/psum | solution.py:269
  1244.0 24.6 %copy-start.68 = (pred[2048]{0:T(1024)(128)(4,1)S(1)}, pred[2048]{0:T(1024)(128)(4,1)}, u32[]{:S(2)}) copy-start(pred[2048]{0:T(1024)(128)(4,1)} %copy-done.67) | copy-start | bytes 6148
  1324.9 146.1 %reduce-scatter.25.cloned.1.call-start = ((), (), s32[]{:S(2)}) async-start(), calls=%async_computation.32 | async-start | bytes 6488064 | tf_op jit(solution)/shard_map/reduce_scatter | solution.py:362
  1331.6 202.8 %reduce-scatter.27.cloned.1.call-start = ((), (), s32[]{:S(2)}) async-start(), calls=%async_computation.33 | async-start | bytes 6488064 | tf_op jit(solution)/shard_map/reduce_scatter | solution.py:365
  1338.4 259.1 %reduce-scatter.29.cloned.1.call-start = ((), (), s32[]{:S(2)}) async-start(), calls=%async_computation.34 | async-start | bytes 6488064 | tf_op jit(solution)/shard_map/reduce_scatter | solution.py:368
  1346.9 284.9 %reduce-scatter.23.cloned.1.call-start = ((), (), s32[]{:S(2)}) async-start(), calls=%async_computation.31 | async-start | bytes 36864 | tf_op jit(solution)/shard_map/reduce_scatter | solution.py:356
  1384.1 293.8 %reduce-scatter.13.cloned.1.call-start = ((), (), s32[]{:S(2)}) async-start(), calls=%async_computation.23 | async-start | bytes 2621440 | tf_op jit(solution)/shard_map/reduce_scatter | solution.py:188
  1389.4 495.2 %all-reduce.17.cloned.1.call-start = ((), (), s32[]{:S(2)}) async-start(), calls=%async_computation.36 | async-start | bytes 17301504 | tf_op jit(solution)/shard_map/psum | solution.py:253
  1389.5 22.1 %slice-start = ((s8[12582912]{0:T(1024)(128)(4,1)}), s8[4194304]{0:T(1024)(128)(4,1)S(1)}, s32[]{:S(2)}) async-start(s8[12582912]{0:T(1024)(128)(4,1)} %bitcast.199), calls=%async_computation.37 | async-start | bytes 8388608
  1389.5 22.1 %slice-start.1 = ((s8[12582912]{0:T(1024)(128)(4,1)}), s8[4194304]{0:T(1024)(128)(4,1)S(1)}, s32[]{:S(2)}) async-start(s8[12582912]{0:T(1024)(128)(4,1)} %bitcast.199), calls=%async_computation.38 | async-start | bytes 8388608
  1417.7 501.9 %reduce-scatter.31.cloned.1.call-start = ((), (), s32[]{:S(2)}) async-start(), calls=%async_computation.35 | async-start | bytes 36864
  1439.2 569.2 %all-reduce.15.cloned.1.call-start = ((), (), s32[]{:S(2)}) async-start(), calls=%async_computation.26 | async-start | bytes 4194304 | tf_op jit(solution)/shard_map/psum | solution.py:330
  1446.9 605.3 %reduce-scatter.15.cloned.1.call-start = ((), (), s32[]{:S(2)}) async-start(), calls=%async_computation.27 | async-start | bytes 2359296 | tf_op jit(solution)/shard_map/reduce_scatter | solution.py:335
  1451.4 645.4 %reduce-scatter.17.cloned.1.call-start = ((), (), s32[]{:S(2)}) async-start(), calls=%async_computation.28 | async-start | bytes 2359296 | tf_op jit(solution)/shard_map/reduce_scatter | solution.py:338
  1455.9 685.7 %reduce-scatter.19.cloned.1.call-start = ((), (), s32[]{:S(2)}) async-start(), calls=%async_computation.29 | async-start | bytes 2359296 | tf_op jit(solution)/shard_map/reduce_scatter | solution.py:341
  1460.5 725.8 %reduce-scatter.21.cloned.1.call-start = ((), (), s32[]{:S(2)}) async-start(), calls=%async_computation.30 | async-start | bytes 2359296 | tf_op jit(solution)/shard_map/reduce_scatter | solution.py:344
  2008.5 179.5 %copy-start.1 = (bf16[2,352,2048]{2,1,0:T(8,128)(2,1)S(1)}, bf16[2,352,2048]{2,1,0:T(8,128)(2,1)}, u32[]{:S(2)}) copy-start(bf16[2,352,2048]{2,1,0:T(8,128)(2,1)} %param.41) | copy-start | bytes 8650756
  (73 other events, 499.9 us)
Sparse Core Ops, SparseCore 0:
  9.6 48.6 all-gather.12
  60.2 26.5 all-gather.18
  88.7 27.8 all-gather.16
  118.4 27.8 all-gather.14
  148.0 28.1 all-gather.20
  180.8 86.4 all-reduce.10
  269.0 44.8 all-gather.28
  315.9 64.8 all-gather.22
  382.9 66.1 all-gather.24
  451.0 66.4 all-gather.26
  1325.0 83.9 all-reduce.12
  1412.9 58.0 reduce-scatter.24
  1475.4 59.0 reduce-scatter.26
  1538.4 59.0 reduce-scatter.28
  1600.6 31.1 reduce-scatter.22
  1633.9 43.8 reduce-scatter.12
  1680.5 204.0 all-reduce.16
  1888.3 31.2 reduce-scatter.30
  1921.9 86.5 all-reduce.14
  2012.0 40.2 reduce-scatter.14
  2055.5 41.1 reduce-scatter.16
  2100.4 41.2 reduce-scatter.18
  2145.0 41.2 reduce-scatter.20
where the time goes:
time: 2210 us; the launch traced here: 2190 us
  waiting for transfers between devices  1170 us (53%)
  blocking collectives  355 us (16%)
  matrix products  229 us (10%)
  local copies, waits for them, and re-layouts  221 us (10%)
  other arithmetic  183 us (8%)
    all_to_all x1, waiting for transfers between devices, body(): lax.all_to_all(outgoing, 'ep', split_axis=0, concat_axis=0, tiled=True)  207 us
    psum x1, waiting for transfers between devices, body(): lax.psum(expert_gate_grad.astype(jnp.bfloat16), 'dp').astype(jnp.float32)  204 us
    all_to_all x1, blocking collectives, body(): lax.all_to_all(outgoing_grads, 'ep', split_axis=0, concat_axis=0, tiled=T...  142 us
    all_gather x1, blocking collectives, body(): lax.all_gather(shared_switch, ('dp', 'ep'), axis=0, tiled=True)  140 us
    all_to_all x1, waiting for transfers between devices, body(): lax.all_to_all(slot_back_low, 'ep', split_axis=0, concat_axis=0, tiled=True)  130 us
    psum x1, waiting for transfers between devices, body(): lax.psum(entry_part.astype(jnp.bfloat16), 'tp').astype(jnp.float32)  87.5 us
    reduce_scatter x1, waiting for transfers between devices, body(): lax.psum_scatter(shared_up_grad.astype(jnp.bfloat16), ('dp', 'ep'), scatt...  61.2 us
    reduce_scatter x1, waiting for transfers between devices, body(): lax.psum_scatter(shared_down_grad.astype(jnp.bfloat16), ('dp', 'ep'), sca...  60.7 us
  transfers between devices with their start and end apart: 26, of which 20 were waited for; matrix products, arithmetic and copies ran while one was open for 17% of the time, Pallas kernels for 0%

commit v1 on v0

v1 whole, which is shorter than its diff:
```python
import jax
import jax.numpy as jnp
from jax import lax
from jax.sharding import PartitionSpec as P

HD = 128
TOP = 4
EPS = 1e-06
THETA = 1000000.0
LANES = 128
F32 = jnp.float32
BF16 = jnp.bfloat16


def dot_nn(left, right):
    return lax.dot_general(left, right, (((1,), (0,)), ((), ())), preferred_element_type=F32)


def dot_nt(left, right):
    return lax.dot_general(left, right, (((1,), (1,)), ((), ())), preferred_element_type=F32)


def dot_tn(left, right):
    return lax.dot_general(left, right, (((0,), (0,)), ((), ())), preferred_element_type=F32)


def dot_exact(left, right, dims):
    return lax.dot_general(
        left, right, (dims, ((), ())), precision=lax.Precision.HIGHEST, preferred_element_type=F32
    )


def norm_parts(values):
    inverse = lax.rsqrt(jnp.mean(values * values, axis=-1, keepdims=True) + EPS)
    return (values * inverse, inverse)


def norm_back(grad_normed, gain_vector, unit_rows, inverse):
    scaled = grad_normed * gain_vector
    return inverse * (scaled - unit_rows * jnp.mean(scaled * unit_rows, axis=-1, keepdims=True))


def rotate(values):
    middle = values.shape[-1] // 2
    return jnp.concatenate([-values[..., middle:], values[..., :middle]], axis=-1)


def unrotate(values):
    middle = values.shape[-1] // 2
    return jnp.concatenate([values[..., middle:], -values[..., :middle]], axis=-1)


def split_pair(values):
    high = values.astype(BF16)
    rest = values - lax.reduce_precision(values, exponent_bits=8, mantissa_bits=7)
    return high, rest.astype(BF16)


def shifted(block, axis, step):
    count = lax.axis_size(axis)
    return lax.ppermute(block, axis, [(i, (i + step) % count) for i in range(count)])


def gather_blocks(block, axis):
    count = lax.axis_size(axis)
    return [block] + [shifted(block, axis, step) for step in range(1, count)]


def scatter_blocks(blocks, axis):
    total = blocks[0]
    for step in range(1, len(blocks)):
        total = total + shifted(blocks[step].astype(BF16), axis, -step).astype(F32)
    return total


def exchange_sum(values, axis):
    count = lax.axis_size(axis)
    if count & (count - 1):
        return lax.psum(values, axis)
    bit = 1
    while bit < count:
        values = values + lax.ppermute(values, axis, [(i, i ^ bit) for i in range(count)])
        bit *= 2
    return values


def whole_sum(values, axis):
    if lax.axis_size(axis) == 2:
        other = lax.ppermute(values, axis, [(0, 1), (1, 0)])
        return values.astype(F32) + other.astype(F32)
    return lax.psum(values, axis).astype(F32)


def shard_sum(values, axis):
    if lax.axis_size(axis) == 2:
        place = lax.axis_index(axis)
        other = lax.ppermute(
            lax.dynamic_index_in_dim(values, 1 - place, 0, False), axis, [(0, 1), (1, 0)]
        )
        return lax.dynamic_index_in_dim(values, place, 0, False).astype(F32) + other.astype(F32)
    return lax.psum_scatter(values, axis, scatter_dimension=0, tiled=False).astype(F32)


def pair_gather(values, axis):
    if lax.axis_size(axis) == 2:
        place = lax.axis_index(axis)
        other = lax.ppermute(values, axis, [(0, 1), (1, 0)])
        first = jnp.where(place == 0, values, other)
        second = jnp.where(place == 0, other, values)
        return jnp.stack([first, second])
    return lax.all_gather(values, axis)


def body(
    layer_input,
    cotangent,
    lengths,
    seq_order,
    routes,
    query_weight,
    key_weight,
    value_weight,
    mixing_weight,
    heads_bias,
    entry_gain,
    middle_gain,
    router_weight,
    shared_switch,
    shared_gate,
    shared_up,
    shared_down,
    expert_gate,
    expert_up,
    expert_down,
):
    tp_count = lax.axis_size("tp")
    ep_count = lax.axis_size("ep")
    dp_count = lax.axis_size("dp")
    part_count = dp_count * ep_count
    tp_index = lax.axis_index("tp")
    ep_index = lax.axis_index("ep")
    own_rows, width = layer_input.shape
    group_rows = own_rows * tp_count
    span_rows = group_rows * ep_count
    slice_rows = query_weight.shape[0]
    head_cols = query_weight.shape[1]
    head_count = head_cols // HD
    local_experts = expert_gate.shape[0]
    expert_count = router_weight.shape[1]
    hidden = expert_gate.shape[2]
    shared_hidden = shared_gate.shape[1] // ep_count
    segments = local_experts + 1
    seg = -(-max(hidden, shared_hidden) // LANES) * LANES

    group_index = lax.axis_index(("dp", "ep"))
    length = jnp.take(lengths, jnp.take(seq_order, group_index))
    own_keep = ((tp_index * own_rows + jnp.arange(own_rows)) < length).astype(F32)[:, None]
    block_of = jnp.arange(group_rows) // own_rows
    position = ((tp_index - block_of) % tp_count) * own_rows + jnp.arange(group_rows) % own_rows

    bias_rows = heads_bias.size
    small = jnp.concatenate(
        [
            router_weight,
            shared_switch[:, None],
            entry_gain[:, None],
            middle_gain[:, None],
        ],
        axis=1,
    )
    bias_depth = -(-bias_rows // slice_rows)
    bias_cols = jnp.pad(heads_bias.reshape(-1), (0, bias_depth * slice_rows - bias_rows))
    bias_cols = bias_cols.reshape(bias_depth, slice_rows).T
    small = jnp.concatenate([small, bias_cols], axis=1)
    small = jnp.pad(small, ((0, 0), (0, LANES - small.shape[1])))
    dense_own = jnp.concatenate(
        [query_weight, key_weight, value_weight, mixing_weight.T, small], axis=1
    )
    dense_full = lax.all_gather(dense_own, ("dp", "ep"), axis=0, tiled=True)
    in_weight = dense_full[:, : 3 * head_cols]
    out_weight = dense_full[:, 3 * head_cols : 4 * head_cols]
    small_full = dense_full[:, 4 * head_cols :]
    small_rows = small_full[:, : expert_count + 3].astype(F32).T
    entry_full = small_rows[expert_count + 1][None]
    middle_full = small_rows[expert_count + 2][None]
    bias_full = small_full[:, expert_count + 3 : expert_count + 3 + bias_depth]
    bias_full = bias_full.reshape(part_count, slice_rows, bias_depth).transpose(0, 2, 1)
    bias_full = bias_full.reshape(part_count, -1)[:, :bias_rows]
    bias_full = bias_full.reshape((part_count,) + heads_bias.shape).transpose(1, 2, 0, 3)
    bias_full = bias_full.reshape(1, 3 * head_cols).astype(F32)

    input_values = jnp.concatenate(gather_blocks(layer_input, "tp"), axis=0).astype(F32)
    entry_unit, entry_inverse = norm_parts(input_values)
    entry_normed = (entry_unit * entry_full).astype(BF16)

    def to_owners(matrix):
        return matrix.reshape(ep_count, shared_hidden, slice_rows)

    shared_own = jnp.concatenate(
        [to_owners(shared_gate.T), to_owners(shared_up.T), to_owners(shared_down)], axis=1
    )
    shared_span = lax.all_to_all(shared_own, "ep", split_axis=0, concat_axis=0, tiled=True)
    shared_parts = pair_gather(shared_span, "dp").reshape(
        part_count, 3, shared_hidden, slice_rows
    )
    shared_parts = shared_parts.transpose(1, 2, 0, 3).reshape(3, shared_hidden, width)

    def stack_hidden(expert_rows, shared_rows):
        padded = [jnp.pad(rows, ((0, seg - rows.shape[0]), (0, 0))) for rows in expert_rows]
        padded.append(jnp.pad(shared_rows, ((0, seg - shared_hidden), (0, 0))))
        return padded

    gate_rows = stack_hidden([expert_gate[j].T for j in range(local_experts)], shared_parts[0])
    up_rows = stack_hidden([expert_up[j].T for j in range(local_experts)], shared_parts[1])
    down_rows = stack_hidden([expert_down[j] for j in range(local_experts)], shared_parts[2])
    first_weight = jnp.concatenate(gate_rows + up_rows, axis=0)
    down_weight = jnp.concatenate(down_rows, axis=0)

    in_lin = dot_nn(entry_normed, in_weight) + bias_full
    freqs = THETA ** (-(jnp.arange(HD // 2).astype(F32) * 2.0) / HD)
    angles = position.astype(F32)[:, None] * freqs[None, :]
    angles = jnp.concatenate([angles, angles], axis=-1)
    cosine = jnp.cos(angles)[:, None, :]
    sine = jnp.sin(angles)[:, None, :]
    query_heads = in_lin[:, :head_cols].reshape(group_rows, head_count, HD)
    key_heads = in_lin[:, head_cols : 2 * head_cols].reshape(group_rows, head_count, HD)
    query_rot = (query_heads * cosine + rotate(query_heads) * sine).astype(BF16)
    key_rot = (key_heads * cosine + rotate(key_heads) * sine).astype(BF16)
    value_heads = in_lin[:, 2 * head_cols :].astype(BF16).reshape(group_rows, head_count, HD)
    score_scale = HD ** (-0.5)
    causal = position[:, None] >= position[None, :]

    def score_matrix():
        raw_scores = jnp.einsum("qhd,khd->hqk", query_rot, key_rot, preferred_element_type=F32)
        return jnp.where(causal[None], raw_scores * score_scale, -1e30)

    scores = score_matrix()
    top_score = jnp.max(scores, axis=-1, keepdims=True)
    log_total = top_score + jnp.log(jnp.sum(jnp.exp(scores - top_score), axis=-1, keepdims=True))
    attn_probs = jnp.exp(scores - log_total).astype(BF16)
    context = jnp.einsum("hqk,khd->qhd", attn_probs, value_heads, preferred_element_type=F32)
    context_low = context.astype(BF16).reshape(group_rows, head_cols)
    head_terms = dot_nt(context_low, out_weight)
    attention_own = scatter_blocks(
        [head_terms[j * own_rows : (j + 1) * own_rows] for j in range(tp_count)], "tp"
    )

    hidden_state = input_values[:own_rows] + own_keep * attention_own
    middle_unit, middle_inverse = norm_parts(hidden_state)
    middle_normed = (middle_unit * middle_full).astype(BF16)
    own_logits = dot_nn(middle_normed, small_full)
    expert_probs = jax.nn.softmax(own_logits[:, :expert_count], axis=-1)
    switch_value = jax.nn.sigmoid(own_logits[:, expert_count : expert_count + 1])
    own_routes = lax.dynamic_slice_in_dim(routes, tp_index * own_rows, own_rows, 0)
    route_mask = jnp.any(
        own_routes[:, :, None] == jnp.arange(expert_count)[None, None, :], axis=1
    ).astype(F32)
    row_gates = jnp.concatenate([own_keep * route_mask * expert_probs, own_keep * switch_value], axis=1)
    gate_high, gate_low = split_pair(row_gates)
    gate_cols = expert_count + 1
    half = LANES // 2
    extra = jnp.concatenate(
        [
            jnp.pad(gate_high, ((0, 0), (0, half - gate_cols))),
            jnp.pad(gate_low, ((0, 0), (0, half - gate_cols))),
        ],
        axis=1,
    )

    upstream = lax.all_gather(cotangent, ("ep", "tp"), axis=0, tiled=True)
    sent_rows = jnp.concatenate([middle_normed, extra], axis=1)
    span_all = lax.all_gather(sent_rows, ("ep", "tp"), axis=0, tiled=True)
    span_normed = span_all[:, :width]
    span_extra = span_all[:, width:].astype(F32)
    span_gates = span_extra[:, :half] + span_extra[:, half:]
    lane = jnp.arange(half)[None, :]
    gate_of = [
        jnp.sum(jnp.where(lane == ep_index * local_experts + j, span_gates, 0.0), axis=1, keepdims=True)
        for j in range(local_experts)
    ] + [span_gates[:, expert_count : expert_count + 1]]
    gate_wide = jnp.concatenate(
        [jnp.broadcast_to(column, (span_rows, seg)) for column in gate_of], axis=1
    )

    first_lin = dot_nt(span_normed, first_weight)
    pre_gate = first_lin[:, : segments * seg]
    pre_up = first_lin[:, segments * seg :]
    sigmoid = jax.nn.sigmoid(pre_gate)
    act = pre_gate * sigmoid
    slope = sigmoid * (1.0 + pre_gate * (1.0 - sigmoid))
    hidden_low = (act * pre_up).astype(BF16)
    hidden_gated = (gate_wide * hidden_low.astype(F32)).astype(BF16)
    back_lin = dot_nt(upstream, down_weight)
    gate_terms = hidden_low.astype(F32) * back_lin
    gate_parts = jnp.concatenate(
        [
            jnp.sum(gate_terms[:, j * seg : (j + 1) * seg], axis=1, keepdims=True)
            for j in range(segments)
        ],
        axis=1,
    )
    hidden_grad = gate_wide * back_lin
    gate_grad_low = (hidden_grad * pre_up * slope).astype(BF16)
    up_grad_low = (hidden_grad * act).astype(BF16)
    first_grad = jnp.concatenate([gate_grad_low, up_grad_low], axis=1)

    normed_part = dot_nn(first_grad, first_weight).astype(BF16)
    column_of = jnp.concatenate(
        [ep_index * local_experts + jnp.arange(local_experts), jnp.array([expert_count])]
    )
    part_place = (column_of[:, None] == jnp.arange(half)[None, :]).astype(F32)
    placed = jnp.sum(gate_parts[:, :, None] * part_place[None], axis=1)
    placed_high, placed_low = split_pair(placed)
    back_rows = jnp.concatenate([normed_part, placed_high, placed_low], axis=1)
    back_own = lax.psum_scatter(back_rows, ("ep", "tp"), scatter_dimension=0, tiled=True).astype(F32)
    branch = dot_nn(hidden_gated, down_weight).astype(BF16)
    branch_own = lax.psum_scatter(branch, ("ep", "tp"), scatter_dimension=0, tiled=True).astype(F32)
    layer_output = (hidden_state + branch_own).astype(BF16)

    down_grad = dot_tn(hidden_gated, upstream).astype(BF16)
    first_weight_grad = dot_tn(first_grad, span_normed).astype(BF16)

    def segment_rows(matrix, place, count):
        return matrix[place * seg : place * seg + count]

    expert_first = jnp.concatenate(
        [segment_rows(first_weight_grad, j, hidden) for j in range(local_experts)]
        + [segment_rows(first_weight_grad, segments + j, hidden) for j in range(local_experts)],
        axis=0,
    )
    expert_last = jnp.concatenate(
        [segment_rows(down_grad, j, hidden) for j in range(local_experts)], axis=0
    )
    expert_last_sum = whole_sum(expert_last, "dp").reshape(local_experts, hidden, width)
    expert_first_sum = whole_sum(expert_first, "dp").reshape(2, local_experts, hidden, width)
    shared_grad = jnp.concatenate(
        [
            segment_rows(first_weight_grad, local_experts, shared_hidden),
            segment_rows(first_weight_grad, segments + local_experts, shared_hidden),
            segment_rows(down_grad, local_experts, shared_hidden),
        ],
        axis=0,
    )
    shared_grad = shared_grad.reshape(3 * shared_hidden, dp_count, ep_count, slice_rows)
    shared_grad = shared_grad.transpose(1, 2, 0, 3)
    shared_mine = shard_sum(shared_grad, "dp").astype(BF16)
    shared_back = lax.all_to_all(shared_mine, "ep", split_axis=0, concat_axis=0, tiled=True)
    shared_back = shared_back.reshape(ep_count, 3, shared_hidden, slice_rows).astype(F32)

    normed_own = back_own[:, :width]
    gate_sums = back_own[:, width : width + half] + back_own[:, width + half :]
    prob_grad = own_keep * route_mask * gate_sums[:, :expert_count]
    logit_grad = expert_probs * (
        prob_grad - jnp.sum(expert_probs * prob_grad, axis=-1, keepdims=True)
    )
    switch_grad = (
        own_keep
        * gate_sums[:, expert_count : expert_count + 1]
        * switch_value
        * (1.0 - switch_value)
    )
    score_grad = jnp.concatenate([logit_grad, switch_grad], axis=1)
    normed_total = normed_own + dot_exact(score_grad, small_rows[: expert_count + 1], ((1,), (0,)))
    router_part = dot_exact(score_grad, middle_normed.astype(F32), ((0,), (0,)))
    middle_part = jnp.sum(normed_total * middle_unit, axis=0, keepdims=True)
    state_grad = cotangent.astype(F32) + norm_back(
        normed_total, middle_full, middle_unit, middle_inverse
    )
    attention_grad_own = (own_keep * state_grad).astype(BF16)
    attention_grad = jnp.concatenate(gather_blocks(attention_grad_own, "tp"), axis=0)

    mixing_grad = dot_tn(attention_grad, context_low)
    context_grad = dot_nn(attention_grad, out_weight)
    context_grad = context_grad.astype(BF16).reshape(group_rows, head_count, HD)
    probs_again = jnp.exp(score_matrix() - log_total)
    probs_low = probs_again.astype(BF16)
    value_grad = jnp.einsum("hqk,qhd->khd", probs_low, context_grad, preferred_element_type=F32)
    value_grad = value_grad.astype(BF16).reshape(group_rows, head_cols)
    prob_grads = jnp.einsum("qhd,khd->hqk", context_grad, value_heads, preferred_element_type=F32)
    row_delta = jnp.sum(probs_again * prob_grads, axis=-1, keepdims=True)
    score_grads = (probs_again * (prob_grads - row_delta)).astype(BF16)
    query_rot_grad = (
        jnp.einsum("hqk,khd->qhd", score_grads, key_rot, preferred_element_type=F32) * score_scale
    )
    key_rot_grad = (
        jnp.einsum("hqk,qhd->khd", score_grads, query_rot, preferred_element_type=F32) * score_scale
    )
    query_grad = (query_rot_grad * cosine + unrotate(query_rot_grad * sine)).astype(BF16)
    key_grad = (key_rot_grad * cosine + unrotate(key_rot_grad * sine)).astype(BF16)
    in_grad = jnp.concatenate(
        [query_grad.reshape(group_rows, head_cols), key_grad.reshape(group_rows, head_cols), value_grad],
        axis=1,
    )
    bias_grad = jnp.sum(in_grad.astype(F32), axis=0)
    entry_part = dot_nt(in_grad, in_weight)
    entry_own = scatter_blocks(
        [entry_part[j * own_rows : (j + 1) * own_rows] for j in range(tp_count)], "tp"
    )
    input_gradient = state_grad + norm_back(
        entry_own, entry_full, entry_unit[:own_rows], entry_inverse[:own_rows]
    )

    entry_gain_part = jnp.sum(entry_part * entry_unit, axis=0, keepdims=True)
    small_part = exchange_sum(
        jnp.concatenate([router_part, entry_gain_part, middle_part], axis=0), "tp"
    )
    bias_part = bias_grad.reshape(3, head_count, part_count, -1).transpose(2, 0, 1, 3)
    bias_part = bias_part.reshape(part_count, bias_rows)
    bias_part = jnp.pad(bias_part, ((0, 0), (0, bias_depth * slice_rows - bias_rows)))
    bias_part = bias_part.reshape(part_count, bias_depth, slice_rows).transpose(1, 0, 2)
    bias_part = bias_part.reshape(bias_depth, width)
    small_part = jnp.concatenate([small_part, bias_part], axis=0)
    small_high, small_low = split_pair(small_part)
    small_count = small_part.shape[0]
    small_cols = jnp.concatenate(
        [
            jnp.pad(small_high, ((0, half - small_count), (0, 0))),
            jnp.pad(small_low, ((0, half - small_count), (0, 0))),
        ],
        axis=0,
    ).T
    dense_grad = jnp.concatenate(
        [
            dot_tn(entry_normed, in_grad).astype(BF16),
            mixing_grad.astype(BF16),
            small_cols,
        ],
        axis=1,
    )
    dense_sum = lax.psum_scatter(
        dense_grad, ("dp", "ep"), scatter_dimension=0, tiled=True
    ).astype(F32)
    small_sum = dense_sum[:, 4 * head_cols : 4 * head_cols + half] + dense_sum[:, 4 * head_cols + half :]
    bias_sum = small_sum[:, expert_count + 3 : expert_count + 3 + bias_depth]
    bias_sum = bias_sum.T.reshape(-1)[:bias_rows].reshape(heads_bias.shape)

    def by_columns(rows):
        return rows.transpose(2, 0, 1).reshape(slice_rows, ep_count * shared_hidden)

    return (
        layer_output,
        input_gradient,
        dense_sum[:, :head_cols],
        dense_sum[:, head_cols : 2 * head_cols],
        dense_sum[:, 2 * head_cols : 3 * head_cols],
        dense_sum[:, 3 * head_cols : 4 * head_cols].T,
        bias_sum,
        small_sum[:, expert_count + 1],
        small_sum[:, expert_count + 2],
        small_sum[:, :expert_count],
        small_sum[:, expert_count],
        by_columns(shared_back[:, 0]),
        by_columns(shared_back[:, 1]),
        shared_back[:, 2].reshape(ep_count * shared_hidden, slice_rows),
        expert_first_sum[0].transpose(0, 2, 1),
        expert_first_sum[1].transpose(0, 2, 1),
        expert_last_sum,
    )


def solution(mesh):
    rows = P(("dp", "ep", "tp"), None)
    parts = P(("dp", "ep"))
    in_cols = P(("dp", "ep"), "tp")
    out_cols = P("tp", ("dp", "ep"))
    weights = (
        in_cols,
        in_cols,
        in_cols,
        out_cols,
        P(None, "tp", ("dp", "ep")),
        parts,
        parts,
        P(("dp", "ep"), None),
        parts,
        in_cols,
        in_cols,
        out_cols,
        P("ep", None, "tp"),
        P("ep", None, "tp"),
        P("ep", "tp", None),
    )
    return jax.shard_map(
        body,
        mesh=mesh,
        in_specs=(rows, rows, P(), P(), P(("dp", "ep"), None)) + weights,
        out_specs=(rows, rows) + weights,
        check_vma=False,
    )
```

time: 2210 us -> 1020 us (0.46)
  waiting for transfers between devices: 1170 us -> 563 us
  blocking collectives: 355 us -> 0 us
  other arithmetic: 183 us -> 70.2 us
  local copies, waits for them, and re-layouts: 221 us -> 109 us
  matrix products: 229 us -> 183 us
  starting transfers between devices: 21.8 us -> 64.2 us
    ppermute x0 -> x18, waiting for transfers between devices: none -> 412 us  [the longest x1 167 us: shard_sum(): lax.ppermute(lax.dynamic_index_in_dim(values, 1 - place, 0, False), axis,...]
    psum x4 -> x0, waiting for transfers between devices: 344 us -> none  [the longest x1 204 us: body(): lax.psum(expert_gate_grad.astype(jnp.bfloat16), 'dp').astype(jnp.float32)]
    reduce_scatter x9 -> x1, waiting for transfers between devices: 338 us -> 0.01 us  [body(): lax.psum_scatter(dense_grad, ('dp', 'ep'), scatter_dimension=0, tiled=True)]
    all_to_all x3 -> x2, waiting for transfers between devices: 337 us -> 32.1 us  [the longest x1 32.1 us: body(): lax.all_to_all(shared_own, 'ep', split_axis=0, concat_axis=0, tiled=True)]
    all_gather x5 -> x0, blocking collectives: 178 us -> none  [the longest x1 140 us: body(): lax.all_gather(shared_switch, ('dp', 'ep'), axis=0, tiled=True)]
    all_to_all x1 -> x0, blocking collectives: 142 us -> none  [body(): lax.all_to_all(outgoing_grads, 'ep', split_axis=0, concat_axis=0, tiled=T...]
    gather x4 -> x0, local copies, waits for them, and re-layouts: 103 us -> none  [the longest x1 28.3 us: body(): slot_grads_in = jnp.take(route_grads, slot_pair, axis=0)]
    convert_element_type x31 -> x19, other arithmetic: 79.1 us -> 8.41 us  [the longest x1 1.83 us: body(): shared_mine = shard_sum(shared_grad, 'dp').astype(BF16)]
  transfers between devices with their start and end apart: 26 -> 26, of which waited for: 20 -> 16; matrix products, arithmetic and copies ran while one was open for 17% -> 23% of each run, Pallas kernels for 0% -> 0%
where the time goes in v1:
time: 1020 us; the launch traced here: 1010 us
  waiting for transfers between devices  563 us (55%)
  matrix products  183 us (18%)
  local copies, waits for them, and re-layouts  109 us (11%)
  other arithmetic  70.2 us (7%)
  starting transfers between devices  64.2 us (6%)
  between operations  17.3 us (2%)
    ppermute x1, waiting for transfers between devices, shard_sum(): lax.ppermute(lax.dynamic_index_in_dim(values, 1 - place, 0, False), axis,...  167 us
    ppermute x12, waiting for transfers between devices, shifted(): lax.ppermute(block, axis, [(i, (i + step) % count) for i in range(count)])  134 us
    dot_general x4, matrix products, dot_nt(): lax.dot_general(left, right, (((1,), (1,)), ((), ())), preferred_element_...  65.5 us
    unnamed x8, waiting for transfers between devices  60.8 us
    ppermute x2, waiting for transfers between devices, whole_sum(): other = lax.ppermute(values, axis, [(0, 1), (1, 0)])  54.6 us
    dot_general x4, matrix products, dot_tn(): lax.dot_general(left, right, (((0,), (0,)), ((), ())), preferred_element_...  54.3 us
    dot_general x5, matrix products, dot_nn(): lax.dot_general(left, right, (((1,), (0,)), ((), ())), preferred_element_...  52.3 us
    unnamed x192, local copies, waits for them, and re-layouts  50.4 us
  transfers between devices with their start and end apart: 26, of which 16 were waited for; matrix products, arithmetic and copies ran while one was open for 23% of the time, Pallas kernels for 0%

profile of v1, /device:TPU:0, one launch (start us, length us, event | category | flops | bytes accessed | tf_op | source)
XLA Modules:
  0.0 1007.4 jit_solution(14535161952049771545)
XLA Ops:
  16.5 3.1 collective-permute-start
  19.6 2.6 collective-permute-start.1
  28.2 6.3 collective-permute-done
  34.5 21.6 %collective-permute-done.1 = bf16[128,2048]{0,1:T(8,128)(2,1)S(1)} collective-permute-done((bf16[128,2048]{0,1:T(8,128)(2,1)S(1)}, bf16[128,2048]{0,1:T(8,128)(2,1)S(1)}, u32[]{:S(2)}, u32[]{:S(2)}) %collective-permute-start.1) | collective-permute-done | bytes 524320 | tf_op jit(solution)/shard_map/ppermute | solution.py:61
  56.7 20.6 %all-gather.4.cloned.1.call-done = bf16[2048,2176]{0,1:T(8,128)(2,1)} async-done(((bf16[256,2176]{0,1:T(8,128)(2,1)}), bf16[2048,2176]{0,1:T(8,128)(2,1)}) %all-gather.4.cloned.1.call-update) | async-done | bytes 8912912 | tf_op jit(solution)/shard_map/all_gather | solution.py:179
  79.8 6.8 fusion.17
  94.2 3.0 convolution_convert_fusion.7
  97.3 3.1 fusion.121
  100.7 3.9 collective-permute-start.3
  106.0 10.9 %collective-permute-done.3 = bf16[128,2048]{0,1:T(8,128)(2,1)S(1)} collective-permute-done((bf16[128,2048]{0,1:T(8,128)(2,1)S(1)}, bf16[128,2048]{0,1:T(8,128)(2,1)S(1)}, u32[]{:S(2)}, u32[]{:S(2)}) %collective-permute-start.3) | collective-permute-done | bytes 524320 | tf_op jit(solution)/shard_map/ppermute | solution.py:61
  116.9 33.0 %collective-permute-done.4 = bf16[128,2048]{0,1:T(8,128)(2,1)S(1)} collective-permute-done((bf16[128,2048]{0,1:T(8,128)(2,1)S(1)}, bf16[128,2048]{0,1:T(8,128)(2,1)S(1)}, u32[]{:S(2)}, u32[]{:S(2)}) %collective-permute-start.4) | collective-permute-done | bytes 524320 | tf_op jit(solution)/shard_map/ppermute | solution.py:61
  158.1 3.6 all-to-all-start
  161.9 32.1 %all-to-all-done = bf16[4,1056,256]{2,1,0:T(8,128)(2,1)S(1)} async-done(((bf16[4,1056,256]{2,1,0:T(8,128)(2,1)}), bf16[4,1056,256]{2,1,0:T(8,128)(2,1)S(1)}, u32[]{:S(2)}, u32[]{:S(2)}) %all-to-all-start) | async-done | bytes 2162720 | tf_op jit(solution)/shard_map/all_to_all | solution.py:202
  203.0 39.7 %collective-permute-done.6 = bf16[4,1056,256]{2,1,0:T(8,128)(2,1)S(1)} collective-permute-done((bf16[4,1056,256]{2,1,0:T(8,128)(2,1)S(1)}, bf16[4,1056,256]{2,1,0:T(8,128)(2,1)S(1)}, u32[]{:S(2)}, u32[]{:S(2)}) %collective-permute-start.6) | collective-permute-done | bytes 2162720 | tf_op jit(solution)/shard_map/ppermute | solution.py:107
  252.1 28.2 %fusion.8 = f32[2048,2304]{1,0:T(8,128)} fusion(bf16[2304,2048]{1,0:T(8,128)(2,1)} %pad_dynamic-update-slice_fusion, bf16[2048,2176]{0,1:T(8,128)(2,1)} %all-gather.6.cloned.1.call-done), kind=kOutput, calls=%fused_computation.28 | convolution fusion | flops 19327352832 | bytes 36700160 | tf_op jit(solution)/shard_map/dot_general | solution.py:20
  280.2 37.6 %all-gather.8.cloned.1.call-done = bf16[2048,2048]{1,0:T(8,128)(2,1)} async-done(((bf16[128,2048]{1,0:T(8,128)(2,1)}), bf16[2048,2048]{1,0:T(8,128)(2,1)}) %all-gather.8.cloned.1.call-update) | async-done | bytes 8388624 | tf_op jit(solution)/shard_map/all_gather | solution.py:270
  322.3 27.9 %multiply_convert_fusion.1 = (bf16[2048,1152]{1,0:T(8,128)(2,1)}, bf16[2048,1152]{1,0:T(8,128)(2,1)}, f32[2048,1152]{1,0:T(8,128)}, bf16[2048,1152]{1,0:T(8,128)(2,1)}) fusion(f32[2048,2304]{1,0:T(8,128)} %fusion.8, f32[2048,384]{1,0:T(8,128)S(1)} %broadcast_in_dim.123, f32[2048,384]{1,0:T(8,128)} %broadcast_in_dim.121, f32[2048,384]{1,0:T(8,128)} %broadcast_in_dim.119, ...), kind=kOutput, calls=%fused_computation.13 | convolution fusion | flops 9743892480 | bytes 64618496 | tf_op jit(solution)/shard_map/dot_general | solution.py:20
  350.2 4.8 slice_reduce_fusion.2
  355.3 24.9 %convolution_convert_fusion.2 = bf16[2048,2048]{0,1:T(8,128)(2,1)} fusion(bf16[2304,2048]{1,0:T(8,128)(2,1)} %pad_dynamic-update-slice_fusion, bf16[2048,1152]{1,0:T(8,128)(2,1)} %get-tuple-element.173, bf16[2048,1152]{1,0:T(8,128)(2,1)S(1)} %copy-done.76), kind=kOutput, calls=%fused_computation.24 | convolution fusion | flops 19350421504 | bytes 27262976 | tf_op jit(solution)/shard_map/dot_general | solution.py:16
  380.2 7.4 pad_maximum_fusion.2
  387.6 11.7 %copy.353 = bf16[2048,2176]{1,0:T(8,128)(2,1)} copy(bf16[2048,2176]{0,1:T(8,128)(2,1)} %pad_maximum_fusion.2) | data formatting | bytes 17825792
  400.9 17.8 %convolution_convert_fusion.3 = bf16[2048,2048]{1,0:T(8,128)(2,1)} fusion(bf16[2048,1152]{1,0:T(8,128)(2,1)} %get-tuple-element.175, f32[2048,384]{1,0:T(8,128)} %copy-done.28, f32[2048,384]{1,0:T(8,128)} %broadcast_in_dim.121, f32[2048,384]{1,0:T(8,128)} %broadcast_in_dim.119, bf16[352,2048]{1,0:T(8,128)(2,1)S(1)} %bitcast.189, ...), kind=kOutput, calls=%fused_computation.25 | convolution fusion | flops 9712697344 | bytes 26869760 | tf_op jit(solution)/shard_map/dot_general | solution.py:16
  418.9 26.7 %convolution_convert_fusion = bf16[2304,2048]{1,0:T(8,128)(2,1)} fusion(bf16[2048,2176]{0,1:T(8,128)(2,1)} %all-gather.6.cloned.1.call-done, bf16[2048,1152]{1,0:T(8,128)(2,1)} %get-tuple-element.173, bf16[2048,1152]{1,0:T(8,128)(2,1)} %get-tuple-element.172), kind=kOutput, calls=%fused_computation.5 | convolution fusion | flops 19350945792 | bytes 27262976 | tf_op jit(solution)/shard_map/dot_general | solution.py:24
  445.6 60.0 %reduce-scatter.12.cloned.1.call-done = bf16[128,2176]{1,0:T(8,128)(2,1)} async-done(((bf16[2048,2176]{1,0:T(8,128)(2,1)}), bf16[128,2176]{1,0:T(8,128)(2,1)}) %reduce-scatter.12.cloned.1.call-update) | async-done | bytes 557072
  515.5 7.9 fusion.108
  523.9 3.2 collective-permute-done.7
  527.1 29.6 %collective-permute-done.8 = bf16[128,2048]{0,1:T(8,128)(2,1)S(1)} collective-permute-done((bf16[128,2048]{0,1:T(8,128)(2,1)S(1)}, bf16[128,2048]{0,1:T(8,128)(2,1)S(1)}, u32[]{:S(2)}, u32[]{:S(2)}) %collective-permute-start.8) | collective-permute-done | bytes 524320 | tf_op jit(solution)/shard_map/ppermute | solution.py:61
  558.0 2.7 multiply_reduce_fusion.1
  566.0 6.3 multiply_reduce_fusion
  572.4 34.2 %collective-permute-start.13 = (f32[11,2048]{1,0:T(8,128)S(1)}, f32[11,2048]{1,0:T(8,128)S(1)}, u32[]{:S(2)}, u32[]{:S(2)}) collective-permute-start(f32[11,2048]{1,0:T(8,128)S(1)} %pad_maximum_fusion.16), channel_id=1, source_target_pairs={{0,1},{1,0},{2,3},{3,2},{4,5},{5,4},{6,7},{7,6},{8,9},{9,8},{10,11... | collective-permute-start | bytes 270344 | tf_op jit(solution)/shard_map/ppermute | solution.py:82
  606.6 2.6 convolution_convert_fusion.5
  609.2 5.7 convolution_convert_fusion.1
  615.5 15.9 %collective-permute-done.14 = f32[11,2048]{1,0:T(8,128)S(1)} collective-permute-done((f32[11,2048]{1,0:T(8,128)S(1)}, f32[11,2048]{1,0:T(8,128)S(1)}, u32[]{:S(2)}, u32[]{:S(2)}) %collective-permute-start.14) | collective-permute-done | bytes 90144 | tf_op jit(solution)/shard_map/ppermute | solution.py:82
  631.6 7.4 pad_maximum_fusion.3
  639.0 5.2 pad_maximum_fusion.6
  645.3 19.3 %convolution_convert_fusion.4 = bf16[1152,2048]{1,0:T(8,128)(2,1)S(1)} fusion(bf16[2048,2048]{1,0:T(8,128)(2,1)} %all-gather.8.cloned.1.call-done, bf16[2048,1152]{1,0:T(8,128)(2,1)} %get-tuple-element.175, f32[2048,384]{1,0:T(8,128)} %copy-done.28, f32[2048,384]{1,0:T(8,128)} %broadcast_in_dim.121, f32[2048,384]{1,0:T(8,128)} %broadcast_in_dim.119), kind=kOutput, calls=%fused_computation.26 | convolution fusion | flops 9677832192 | bytes 27262976 | tf_op jit(solution)/shard_map/dot_general | solution.py:24
  669.2 9.9 reshape.403
  679.1 3.1 constant_dynamic-slice_fusion.1
  686.4 167.4 %collective-permute-done.15 = bf16[4,1056,256]{2,1,0:T(8,128)(2,1)S(1)} collective-permute-done((bf16[4,1056,256]{2,1,0:T(8,128)(2,1)S(1)}, bf16[4,1056,256]{2,1,0:T(8,128)(2,1)S(1)}, u32[]{:S(2)}, u32[]{:S(2)}) %collective-permute-start.15) | collective-permute-done | bytes 2162720 | tf_op jit(solution)/shard_map/ppermute | solution.py:97
  855.6 3.8 all-to-all-start.1
  859.4 54.6 %collective-permute-done.17 = bf16[704,2048]{1,0:T(8,128)(2,1)} collective-permute-done((bf16[704,2048]{1,0:T(8,128)(2,1)}, bf16[704,2048]{1,0:T(8,128)(2,1)}, u32[]{:S(2)}, u32[]{:S(2)}) %collective-permute-start.17) | collective-permute-done | bytes 2883616 | tf_op jit(solution)/shard_map/ppermute | solution.py:89
  914.0 6.4 convert_add_fusion.1
  922.6 3.0 copy.338
  925.6 2.9 copy.339
  928.5 9.0 convert_add_fusion
  940.8 10.7 %fusion.107 = (f32[704,2048]{1,0:T(8,128)}, f32[704,2048]{1,0:T(8,128)}) fusion(f32[1408,2048]{1,0:T(8,128)} %convert_add_fusion), kind=kLoop, calls=%fused_computation.250 | loop fusion | bytes 23068672 | tf_op jit(solution)/shard_map/slice | solution.py:456
  953.0 29.6 %collective-permute-done.11 = bf16[128,2048]{0,1:T(8,128)(2,1)} collective-permute-done((bf16[128,2048]{0,1:T(8,128)(2,1)}, bf16[128,2048]{0,1:T(8,128)(2,1)}, u32[]{:S(2)}, u32[]{:S(2)}) %collective-permute-start.11) | collective-permute-done | bytes 524320 | tf_op jit(solution)/shard_map/ppermute | solution.py:61
  985.1 3.3 multiply_add_fusion
  (343 shorter events, 109.2 us)
Async XLA Ops:
  7.2 70.1 %all-gather.4.cloned.1.call-start = ((), (), s32[]{:S(2)}) async-start(), calls=%async_computation.5 | async-start | bytes 10027008 | tf_op jit(solution)/shard_map/all_gather | solution.py:179
  16.2 234.5 %all-gather.6.cloned.1.call-start = ((), (), s32[]{:S(2)}) async-start(), calls=%async_computation.6 | async-start | bytes 9469952 | tf_op jit(solution)/shard_map/all_gather | solution.py:272
  16.5 89.1 %copy-start.19 = (bf16[128,2048]{0,1:T(8,128)(2,1)}, bf16[128,2048]{0,1:T(8,128)(2,1)S(1)}, u32[]{:S(2)}) copy-start(bf16[128,2048]{0,1:T(8,128)(2,1)S(1)} %copy.296) | copy-start | bytes 1572868
  16.5 18.0 %collective-permute-start = (bf16[128,2048]{0,1:T(8,128)(2,1)S(1)}, bf16[128,2048]{0,1:T(8,128)(2,1)S(1)}, u32[]{:S(2)}, u32[]{:S(2)}) collective-permute-start(bf16[128,2048]{0,1:T(8,128)(2,1)S(1)} %copy.296), channel_id=1, source_target_pairs={{0,1},{1,2},{2,3},{3,0},{4,5},{5,6},{6,7},{7,4},{8,9},{9,10},{10,1... | collective-permute-start | bytes 1572872 | tf_op jit(solution)/shard_map/ppermute | solution.py:61
  19.6 36.6 %collective-permute-start.1 = (bf16[128,2048]{0,1:T(8,128)(2,1)S(1)}, bf16[128,2048]{0,1:T(8,128)(2,1)S(1)}, u32[]{:S(2)}, u32[]{:S(2)}) collective-permute-start(bf16[128,2048]{0,1:T(8,128)(2,1)S(1)} %copy.296), channel_id=1, source_target_pairs={{0,2},{1,3},{2,0},{3,1},{4,6},{5,7},{6,4},{7,5},{8,10},{9,11},{10,... | collective-permute-start | bytes 1572872 | tf_op jit(solution)/shard_map/ppermute | solution.py:61
  22.2 34.0 %collective-permute-start.2 = (bf16[128,2048]{0,1:T(8,128)(2,1)S(1)}, bf16[128,2048]{0,1:T(8,128)(2,1)S(1)}, u32[]{:S(2)}, u32[]{:S(2)}) collective-permute-start(bf16[128,2048]{0,1:T(8,128)(2,1)S(1)} %copy.296), channel_id=1, source_target_pairs={{0,3},{1,0},{2,1},{3,2},{4,7},{5,4},{6,5},{7,6},{8,11},{9,8},{10,9... | collective-permute-start | bytes 1572872 | tf_op jit(solution)/shard_map/ppermute | solution.py:61
  28.2 66.0 %copy-start.14 = (pred[512,512]{0,1:T(8,128)(4,1)}, pred[512,512]{0,1:T(8,128)(4,1)S(1)}, u32[]{:S(2)}) copy-start(pred[512,512]{0,1:T(8,128)(4,1)S(1)} %broadcast_compare_fusion) | copy-start | bytes 786436
  34.5 71.1 %copy-start.31 = (bf16[128,2048]{0,1:T(8,128)(2,1)}, bf16[128,2048]{0,1:T(8,128)(2,1)S(1)}, u32[]{:S(2)}) copy-start(bf16[128,2048]{0,1:T(8,128)(2,1)S(1)} %collective-permute-done) | copy-start | bytes 1572868
  78.8 71.6 %copy-start.54 = (f32[1,2048]{1,0:T(1,128)}, f32[1,2048]{1,0:T(1,128)S(1)}, u32[]{:S(2)}) copy-start(f32[1,2048]{1,0:T(1,128)S(1)} %get-tuple-element.241) | copy-start | bytes 24580
  100.7 16.2 %collective-permute-start.3 = (bf16[128,2048]{0,1:T(8,128)(2,1)S(1)}, bf16[128,2048]{0,1:T(8,128)(2,1)S(1)}, u32[]{:S(2)}, u32[]{:S(2)}) collective-permute-start(bf16[128,2048]{0,1:T(8,128)(2,1)S(1)} %get-tuple-element.213), channel_id=1, source_target_pairs={{0,3},{1,0},{2,1},{3,2},{4,7},{5,4},{6,5},{7,6},{8,11},{9,8},{10,9... | collective-permute-start | bytes 1572872 | tf_op jit(solution)/shard_map/ppermute | solution.py:61
  104.5 45.4 %collective-permute-start.4 = (bf16[128,2048]{0,1:T(8,128)(2,1)S(1)}, bf16[128,2048]{0,1:T(8,128)(2,1)S(1)}, u32[]{:S(2)}, u32[]{:S(2)}) collective-permute-start(bf16[128,2048]{0,1:T(8,128)(2,1)S(1)} %get-tuple-element.215), channel_id=1, source_target_pairs={{0,2},{1,3},{2,0},{3,1},{4,6},{5,7},{6,4},{7,5},{8,10},{9,11},{10,... | collective-permute-start | bytes 1572872 | tf_op jit(solution)/shard_map/ppermute | solution.py:61
  104.5 45.4 %collective-permute-start.5 = (bf16[128,2048]{0,1:T(8,128)(2,1)S(1)}, bf16[128,2048]{0,1:T(8,128)(2,1)S(1)}, u32[]{:S(2)}, u32[]{:S(2)}) collective-permute-start(bf16[128,2048]{0,1:T(8,128)(2,1)S(1)} %get-tuple-element.214), channel_id=1, source_target_pairs={{0,1},{1,2},{2,3},{3,0},{4,5},{5,6},{6,7},{7,4},{8,9},{9,10},{10,1... | collective-permute-start | bytes 1572872 | tf_op jit(solution)/shard_map/ppermute | solution.py:61
  105.6 48.2 %copy-start.63 = (f32[128]{0:T(128)}, f32[128]{0:T(128)S(1)}, u32[]{:S(2)}) copy-start(f32[128]{0:T(128)S(1)} %compare_convert_fusion) | copy-start | bytes 1540
  105.7 48.1 %copy-start.61 = (pred[128,8]{0,1:T(8,128)(4,1)}, pred[128,8]{0,1:T(8,128)(4,1)S(1)}, u32[]{:S(2)}) copy-start(pred[128,8]{0,1:T(8,128)(4,1)S(1)} %fusion.67) | copy-start | bytes 3076
  155.3 162.5 %all-gather.8.cloned.1.call-start = ((), (), s32[]{:S(2)}) async-start(), calls=%async_computation.7 | async-start | bytes 8912896 | tf_op jit(solution)/shard_map/all_gather | solution.py:270
  158.1 36.0 %all-to-all-start = ((bf16[4,1056,256]{2,1,0:T(8,128)(2,1)}), bf16[4,1056,256]{2,1,0:T(8,128)(2,1)S(1)}, u32[]{:S(2)}, u32[]{:S(2)}) async-start(bf16[4,1056,256]{2,1,0:T(8,128)(2,1)} %pad_maximum_fusion.10), calls=%async_computation | async-start | bytes 4325376 | tf_op jit(solution)/shard_map/all_to_all | solution.py:202
  161.7 343.9 %reduce-scatter.12.cloned.1.call-start = ((), (), s32[]{:S(2)}) async-start(), calls=%async_computation.10 | async-start | bytes 9469952
  194.0 48.7 %collective-permute-start.6 = (bf16[4,1056,256]{2,1,0:T(8,128)(2,1)S(1)}, bf16[4,1056,256]{2,1,0:T(8,128)(2,1)S(1)}, u32[]{:S(2)}, u32[]{:S(2)}) collective-permute-start(bf16[4,1056,256]{2,1,0:T(8,128)(2,1)S(1)} %all-to-all-done), channel_id=1, source_target_pairs={{0,16},{16,0},{1,17},{17,1},{2,18},{18,2},{3,19},{19,3},{4,20},{20... | collective-permute-start | bytes 6488072 | tf_op jit(solution)/shard_map/ppermute | solution.py:107
  399.4 552.1 %reduce-scatter.10.cloned.1.call-start = ((), (), s32[]{:S(2)}) async-start(), calls=%async_computation.9 | async-start | bytes 8912896
  400.7 109.2 %copy-start.21 = (bf16[128,2048]{0,1:T(8,128)(2,1)}, bf16[128,2048]{0,1:T(8,128)(2,1)S(1)}, u32[]{:S(2)}) copy-start(bf16[128,2048]{0,1:T(8,128)(2,1)S(1)} %copy.319) | copy-start | bytes 1572868
  418.8 88.3 %copy-start.62 = (pred[128,8]{0,1:T(8,128)(4,1)S(1)}, pred[128,8]{0,1:T(8,128)(4,1)}, u32[]{:S(2)}) copy-start(pred[128,8]{0,1:T(8,128)(4,1)} %copy-done.61) | copy-start | bytes 3076
  418.8 88.3 %copy-start.64 = (f32[128]{0:T(128)S(1)}, f32[128]{0:T(128)}, u32[]{:S(2)}) copy-start(f32[128]{0:T(128)} %copy-done.63) | copy-start | bytes 1540
  418.8 88.3 %copy-start.66 = (f32[128]{0:T(128)S(1)}, f32[128]{0:T(128)}, u32[]{:S(2)}) copy-start(f32[128]{0:T(128)} %copy-done.65) | copy-start | bytes 1540
  418.8 88.3 %copy-start.70 = (f32[128]{0:T(128)S(1)}, f32[128]{0:T(128)}, u32[]{:S(2)}) copy-start(f32[128]{0:T(128)} %copy-done.69) | copy-start | bytes 1540
  418.8 89.0 %copy-start.71 = (f32[128,1]{0,1:T(1,128)S(1)}, f32[128,1]{0,1:T(1,128)}, u32[]{:S(2)}) copy-start(f32[128,1]{0,1:T(1,128)} %get-tuple-element.169) | copy-start | bytes 1540
  418.8 89.7 %copy-start.5 = (f32[128,2048]{0,1:T(8,128)S(1)}, f32[128,2048]{0,1:T(8,128)}, u32[]{:S(2)}) copy-start(f32[128,2048]{0,1:T(8,128)} %copy-done.4) | copy-start | bytes 3145732
  418.8 89.7 %copy-start.53 = (bf16[11,2048]{1,0:T(8,128)(2,1)S(1)}, bf16[11,2048]{1,0:T(8,128)(2,1)}, u32[]{:S(2)}) copy-start(bf16[11,2048]{1,0:T(8,128)(2,1)} %get-tuple-element.184) | copy-start | bytes 135172
  418.8 89.7 %copy-start.55 = (f32[1,2048]{1,0:T(1,128)S(1)}, f32[1,2048]{1,0:T(1,128)}, u32[]{:S(2)}) copy-start(f32[1,2048]{1,0:T(1,128)} %copy-done.54) | copy-start | bytes 24580
  418.8 89.7 %copy-start.68 = (f32[128]{0:T(128)S(1)}, f32[128]{0:T(128)}, u32[]{:S(2)}) copy-start(f32[128]{0:T(128)} %copy-done.67) | copy-start | bytes 1540
  418.9 574.1 %reduce-scatter.8.cloned.1.call-start = ((), (), s32[]{:S(2)}) async-start(), calls=%async_computation.8 | async-start | bytes 10027008 | tf_op jit(solution)/shard_map/reduce_scatter | solution.py:430
  509.9 46.8 %slice-start = ((s8[8912896]{0:T(1024)(128)(4,1)}), s8[4194304]{0:T(1024)(128)(4,1)S(1)}, s32[]{:S(2)}) async-start(s8[8912896]{0:T(1024)(128)(4,1)} %bitcast.191), calls=%async_computation.11 | async-start | bytes 8388608
  510.3 46.4 %slice-start.1 = ((s8[8912896]{0:T(1024)(128)(4,1)}), s8[4194304]{0:T(1024)(128)(4,1)S(1)}, s32[]{:S(2)}) async-start(s8[8912896]{0:T(1024)(128)(4,1)} %bitcast.191), calls=%async_computation.12 | async-start | bytes 8388608
  510.3 46.4 %slice-start.2 = ((s8[8912896]{0:T(1024)(128)(4,1)}), s8[524288]{0:T(1024)(128)(4,1)S(1)}, s32[]{:S(2)}) async-start(s8[8912896]{0:T(1024)(128)(4,1)} %bitcast.191), calls=%async_computation.13 | async-start | bytes 1048576
  510.3 16.8 %collective-permute-start.7 = (bf16[128,2048]{0,1:T(8,128)(2,1)S(1)}, bf16[128,2048]{0,1:T(8,128)(2,1)S(1)}, u32[]{:S(2)}, u32[]{:S(2)}) collective-permute-start(bf16[128,2048]{0,1:T(8,128)(2,1)S(1)} %multiply_convert_fusion.5), channel_id=1, source_target_pairs={{0,1},{1,2},{2,3},{3,0},{4,5},{5,6},{6,7},{7,4},{8,9},{9,10},{10,1... | collective-permute-start | bytes 1572872 | tf_op jit(solution)/shard_map/ppermute | solution.py:61
  512.0 44.6 %collective-permute-start.8 = (bf16[128,2048]{0,1:T(8,128)(2,1)S(1)}, bf16[128,2048]{0,1:T(8,128)(2,1)S(1)}, u32[]{:S(2)}, u32[]{:S(2)}) collective-permute-start(bf16[128,2048]{0,1:T(8,128)(2,1)S(1)} %multiply_convert_fusion.5), channel_id=1, source_target_pairs={{0,2},{1,3},{2,0},{3,1},{4,6},{5,7},{6,4},{7,5},{8,10},{9,11},{10,... | collective-permute-start | bytes 1572872 | tf_op jit(solution)/shard_map/ppermute | solution.py:61
  513.1 43.6 %collective-permute-start.9 = (bf16[128,2048]{0,1:T(8,128)(2,1)S(1)}, bf16[128,2048]{0,1:T(8,128)(2,1)S(1)}, u32[]{:S(2)}, u32[]{:S(2)}) collective-permute-start(bf16[128,2048]{0,1:T(8,128)(2,1)S(1)} %multiply_convert_fusion.5), channel_id=1, source_target_pairs={{0,3},{1,0},{2,1},{3,2},{4,7},{5,4},{6,5},{7,6},{8,11},{9,8},{10,9... | collective-permute-start | bytes 1572872 | tf_op jit(solution)/shard_map/ppermute | solution.py:61
  523.3 115.6 %copy-start.6 = (bf16[352,2048]{1,0:T(8,128)(2,1)}, bf16[352,2048]{1,0:T(8,128)(2,1)S(1)}, u32[]{:S(2)}) copy-start(bf16[352,2048]{1,0:T(8,128)(2,1)S(1)} %get-tuple-element.178) | copy-start | bytes 4325380
  566.0 40.6 %copy-start.51 = (bf16[4,128,512]{2,1,0:T(8,128)(2,1)S(1)}, bf16[4,128,512]{2,1,0:T(8,128)(2,1)}, u32[]{:S(2)}) copy-start(bf16[4,128,512]{2,1,0:T(8,128)(2,1)} %copy-done.50) | copy-start | bytes 1572868
  572.3 36.9 %copy-start.58 = (f32[1,2048]{1,0:T(1,128)S(1)}, f32[1,2048]{1,0:T(1,128)}, u32[]{:S(2)}) copy-start(f32[1,2048]{1,0:T(1,128)} %copy-done.57) | copy-start | bytes 24580
  572.4 43.0 %collective-permute-start.13 = (f32[11,2048]{1,0:T(8,128)S(1)}, f32[11,2048]{1,0:T(8,128)S(1)}, u32[]{:S(2)}, u32[]{:S(2)}) collective-permute-start(f32[11,2048]{1,0:T(8,128)S(1)} %pad_maximum_fusion.16), channel_id=1, source_target_pairs={{0,1},{1,0},{2,3},{3,2},{4,5},{5,4},{6,7},{7,6},{8,9},{9,8},{10,11... | collective-permute-start | bytes 270344 | tf_op jit(solution)/shard_map/ppermute | solution.py:82
  615.4 16.0 %collective-permute-start.14 = (f32[11,2048]{1,0:T(8,128)S(1)}, f32[11,2048]{1,0:T(8,128)S(1)}, u32[]{:S(2)}, u32[]{:S(2)}) collective-permute-start(f32[11,2048]{1,0:T(8,128)S(1)} %fusion.138), channel_id=1, source_target_pairs={{0,2},{1,3},{2,0},{3,1},{4,6},{5,7},{6,4},{7,5},{8,10},{9,11},{10,... | collective-permute-start | bytes 270344 | tf_op jit(solution)/shard_map/ppermute | solution.py:82
  644.2 284.3 %collective-permute-start.16 = (bf16[1408,2048]{1,0:T(8,128)(2,1)}, bf16[1408,2048]{1,0:T(8,128)(2,1)}, u32[]{:S(2)}, u32[]{:S(2)}) collective-permute-start(bf16[1408,2048]{1,0:T(8,128)(2,1)} %pad_maximum_fusion.6), channel_id=1, source_target_pairs={{0,16},{16,0},{1,17},{17,1},{2,18},{18,2},{3,19},{19,3},{4,20},{20... | collective-permute-start | bytes 17301512 | tf_op jit(solution)/shard_map/ppermute | solution.py:89
  682.5 171.2 %collective-permute-start.15 = (bf16[4,1056,256]{2,1,0:T(8,128)(2,1)S(1)}, bf16[4,1056,256]{2,1,0:T(8,128)(2,1)S(1)}, u32[]{:S(2)}, u32[]{:S(2)}) collective-permute-start(bf16[4,1056,256]{2,1,0:T(8,128)(2,1)S(1)} %bitcast.181), channel_id=1, source_target_pairs={{0,16},{16,0},{1,17},{17,1},{2,18},{18,2},{3,19},{19,3},{4,20},{20... | collective-permute-start | bytes 6488072 | tf_op jit(solution)/shard_map/ppermute | solution.py:97
  685.5 228.5 %collective-permute-start.17 = (bf16[704,2048]{1,0:T(8,128)(2,1)}, bf16[704,2048]{1,0:T(8,128)(2,1)}, u32[]{:S(2)}, u32[]{:S(2)}) collective-permute-start(bf16[704,2048]{1,0:T(8,128)(2,1)} %pad_maximum_fusion.9), channel_id=1, source_target_pairs={{0,16},{16,0},{1,17},{17,1},{2,18},{18,2},{3,19},{19,3},{4,20},{20... | collective-permute-start | bytes 8650760 | tf_op jit(solution)/shard_map/ppermute | solution.py:89
  855.6 64.8 %all-to-all-start.1 = ((bf16[4,1056,256]{2,1,0:T(8,128)(2,1)}), bf16[4,1056,256]{2,1,0:T(8,128)(2,1)S(1)}, u32[]{:S(2)}, u32[]{:S(2)}) async-start(bf16[4,1056,256]{2,1,0:T(8,128)(2,1)} %fusion.16), calls=%async_computation.2 | async-start | bytes 4325376 | tf_op jit(solution)/shard_map/all_to_all | solution.py:347
  938.7 14.3 %collective-permute-start.10 = (bf16[128,2048]{0,1:T(8,128)(2,1)}, bf16[128,2048]{0,1:T(8,128)(2,1)}, u32[]{:S(2)}, u32[]{:S(2)}) collective-permute-start(bf16[128,2048]{0,1:T(8,128)(2,1)} %get-tuple-element.210), channel_id=1, source_target_pairs={{0,3},{1,0},{2,1},{3,2},{4,7},{5,4},{6,5},{7,6},{8,11},{9,8},{10,9... | collective-permute-start | bytes 1572872 | tf_op jit(solution)/shard_map/ppermute | solution.py:61
  938.7 43.9 %collective-permute-start.11 = (bf16[128,2048]{0,1:T(8,128)(2,1)}, bf16[128,2048]{0,1:T(8,128)(2,1)}, u32[]{:S(2)}, u32[]{:S(2)}) collective-permute-start(bf16[128,2048]{0,1:T(8,128)(2,1)} %get-tuple-element.212), channel_id=1, source_target_pairs={{0,2},{1,3},{2,0},{3,1},{4,6},{5,7},{6,4},{7,5},{8,10},{9,11},{10,... | collective-permute-start | bytes 1572872 | tf_op jit(solution)/shard_map/ppermute | solution.py:61
  938.7 43.9 %collective-permute-start.12 = (bf16[128,2048]{0,1:T(8,128)(2,1)}, bf16[128,2048]{0,1:T(8,128)(2,1)}, u32[]{:S(2)}, u32[]{:S(2)}) collective-permute-start(bf16[128,2048]{0,1:T(8,128)(2,1)} %get-tuple-element.211), channel_id=1, source_target_pairs={{0,1},{1,2},{2,3},{3,0},{4,5},{5,6},{6,7},{7,4},{8,9},{9,10},{10,1... | collective-permute-start | bytes 1572872 | tf_op jit(solution)/shard_map/ppermute | solution.py:61
  (59 other events, 538.6 us)
Sparse Core Ops, SparseCore 0:
  16.3 60.9 all-gather.3
  155.4 87.0 all-gather.5
  244.7 73.0 all-gather.7
  399.5 106.0 reduce-scatter.11
  510.1 128.7 reduce-scatter.9
  642.7 108.5 reduce-scatter.7

commit v2 on v1

v2 whole, which is shorter than its diff:
```python
import jax
import jax.numpy as jnp
from jax import lax
from jax.experimental import pallas as pl
from jax.experimental.pallas import tpu as pltpu
from jax.sharding import PartitionSpec as P

HD = 128
TOP = 4
EPS = 1e-06
THETA = 1000000.0
LANES = 128
F32 = jnp.float32
BF16 = jnp.bfloat16


def dot_nn(left, right):
    return lax.dot_general(left, right, (((1,), (0,)), ((), ())), preferred_element_type=F32)


def dot_nt(left, right):
    return lax.dot_general(left, right, (((1,), (1,)), ((), ())), preferred_element_type=F32)


def dot_tn(left, right):
    return lax.dot_general(left, right, (((0,), (0,)), ((), ())), preferred_element_type=F32)


def dot_exact(left, right, dims):
    return lax.dot_general(
        left, right, (dims, ((), ())), precision=lax.Precision.HIGHEST, preferred_element_type=F32
    )


def norm_parts(values):
    inverse = lax.rsqrt(jnp.mean(values * values, axis=-1, keepdims=True) + EPS)
    return (values * inverse, inverse)


def norm_back(grad_normed, gain_vector, unit_rows, inverse):
    scaled = grad_normed * gain_vector
    return inverse * (scaled - unit_rows * jnp.mean(scaled * unit_rows, axis=-1, keepdims=True))


def rotate(values):
    middle = values.shape[-1] // 2
    return jnp.concatenate([-values[..., middle:], values[..., :middle]], axis=-1)


def unrotate(values):
    middle = values.shape[-1] // 2
    return jnp.concatenate([values[..., middle:], -values[..., :middle]], axis=-1)


def split_pair(values):
    high = values.astype(BF16)
    rest = values - lax.reduce_precision(values, exponent_bits=8, mantissa_bits=7)
    return high, rest.astype(BF16)


def shifted(block, axis, step):
    count = lax.axis_size(axis)
    return lax.ppermute(block, axis, [(i, (i + step) % count) for i in range(count)])


def gather_blocks(block, axis):
    count = lax.axis_size(axis)
    return [block] + [shifted(block, axis, step) for step in range(1, count)]


def send_blocks(blocks, axis):
    return [shifted(blocks[step], axis, -step) for step in range(1, len(blocks))]


def split_rows(values, count):
    rows = values.shape[0] // count
    return [values[j * rows : (j + 1) * rows] for j in range(count)]


def add_up(values):
    total = values[0].astype(F32)
    for value in values[1:]:
        total = total + value.astype(F32)
    return total


def ordered_sum(values, axis):
    count = lax.axis_size(axis)
    place = lax.axis_index(axis)
    blocks = gather_blocks(values, axis)
    total = None
    for j in range(count):
        steps = (place - j) % count
        block = blocks[0]
        for step in range(1, count):
            block = jnp.where(steps == step, blocks[step], block)
        total = block if total is None else total + block
    return total


def swapped_or_none(values, axis):
    return swapped(values, axis, 1) if lax.axis_size(axis) == 2 else None


def whole_sum(values, other, axis):
    if other is not None:
        return values.astype(F32) + other.astype(F32)
    return lax.psum(values, axis).astype(F32)


def swapped(values, axis, bit):
    count = lax.axis_size(axis)
    return lax.ppermute(values, axis, [(i, i ^ bit) for i in range(count)])


def in_order(values, other, place, bit):
    first = (place & bit) == 0
    return jnp.concatenate(
        [jnp.where(first, values, other), jnp.where(first, other, values)], axis=0
    )


def after(value, *others):
    return lax.optimization_barrier((value,) + others)[0]


def move_blocks(moves, shapes, arrays, name):
    count = len(moves(0, 0, 0))

    def shape_of(move):
        index = move[1] if isinstance(move[1], tuple) else (move[1],)
        whole = arrays[move[0]].shape
        return tuple(i.size for i in index) + whole[len(index) :]

    def kernel(*refs):
        given, made = refs[: len(arrays)], refs[len(arrays) : len(arrays) + len(shapes)]
        held, (came, gone) = refs[len(arrays) + len(shapes) : -2], refs[-2:]
        todo = moves(lax.axis_index("dp"), lax.axis_index("ep"), lax.axis_index("tp"))
        loads = [
            pltpu.make_async_copy(given[move[0]].at[move[1]], held[k], came.at[k])
            for k, move in enumerate(todo)
        ]
        stores = [
            pltpu.make_async_copy(held[k], made[move[2]].at[move[3]], gone.at[k])
            for k, move in enumerate(todo)
        ]
        for load in loads:
            load.start()
        for load, store in zip(loads, stores):
            load.wait()
            store.start()
        for store in stores:
            store.wait()

    size = sum(2 * shape.size * shape.dtype.itemsize for shape in shapes)
    anywhere = pl.BlockSpec(memory_space=pl.ANY)
    return pl.pallas_call(
        kernel,
        in_specs=[anywhere] * len(arrays),
        out_specs=[anywhere] * len(shapes),
        out_shape=shapes,
        scratch_shapes=[pltpu.VMEM(shape_of(move), BF16) for move in moves(0, 0, 0)]
        + [pltpu.SemaphoreType.DMA((count,))] * 2,
        compiler_params=pltpu.CompilerParams(vmem_limit_bytes=24 << 20),
        cost_estimate=pl.CostEstimate(flops=0, bytes_accessed=size, transcendentals=0),
        name=name,
    )(*arrays)


def expert_kernel(
    half_count,
    expert_count,
    place_ref,
    rows_ref,
    upstream_ref,
    mask_ref,
    pick_ref,
    router_ref,
    first_ref,
    down_ref,
    *refs,
):
    *back_refs, grad_ref, gated_ref, gate_scratch, extra_scratch, back_scratch = refs[-7:]
    rows, width = rows_ref.shape
    segments = gate_scratch.shape[0]
    seg = down_ref.shape[0] // segments
    logits = dot_nt(rows_ref[...], router_ref[...])
    lane = lax.broadcasted_iota(jnp.int32, logits.shape, 1)
    routed = lane < expert_count
    top = jnp.max(jnp.where(routed, logits, -1e30), axis=1, keepdims=True)
    powers = jnp.where(routed, jnp.exp(jnp.where(routed, logits, top) - top), 0.0)
    probs = powers / jnp.sum(powers, axis=1, keepdims=True)
    switch = jax.nn.sigmoid(logits)
    gates = jnp.where(routed, probs, jnp.where(lane == expert_count, switch, 0.0))
    gates = gates * mask_ref[...].astype(F32)
    for j in range(segments):
        column = jnp.sum(gates * pick_ref[j : j + 1, :], axis=1, keepdims=True)
        gate_scratch[j] = jnp.broadcast_to(column, (rows, LANES))
    extra_scratch[...] = jnp.zeros_like(extra_scratch)
    back_scratch[...] = dot_nt(upstream_ref[...], down_ref[...])

    @pl.loop(0, segments)
    def _(j):
        low = pl.multiple_of(j * seg, LANES)
        first = pl.multiple_of(2 * j * seg, LANES)
        second = pl.multiple_of((2 * j + 1) * seg, LANES)
        gate = jnp.concatenate([gate_scratch[j]] * (seg // LANES), axis=1)
        pre = dot_nt(rows_ref[...], first_ref[pl.ds(first, 2 * seg), :])
        pre_gate, pre_up = pre[:, :seg], pre[:, seg:]
        back_lin = back_scratch[:, pl.ds(low, seg)]
        sigmoid = jax.nn.sigmoid(pre_gate)
        act = pre_gate * sigmoid
        hidden_low = (act * pre_up).astype(BF16).astype(F32)
        gated_ref[:, pl.ds(low, seg)] = (gate * hidden_low).astype(BF16)
        total = jnp.sum(hidden_low * back_lin, axis=1, keepdims=True)
        total_high = total.astype(BF16).astype(F32)
        extra_scratch[...] += total_high * pick_ref[pl.ds(j, 1), :]
        extra_scratch[...] += (total - total_high) * pick_ref[pl.ds(segments + j, 1), :]
        hidden_grad = gate * back_lin
        grad_ref[:, pl.ds(second, seg)] = (hidden_grad * act).astype(BF16)
        slope = sigmoid * (1.0 + pre_gate * (1.0 - sigmoid))
        grad_ref[:, pl.ds(first, seg)] = (hidden_grad * pre_up * slope).astype(BF16)

    count = rows // half_count
    place = place_ref[pl.num_programs(0)]

    def store(columns, values):
        for b in range(half_count):
            slot = lax.rem(place - b + half_count, half_count)
            start = pl.multiple_of(slot * count, count)
            part = values[b * count : (b + 1) * count].astype(BF16)
            for k, back_ref in enumerate(back_refs):

                @pl.when(pl.program_id(0) == k)
                def _(back_ref=back_ref, part=part, start=start):
                    back_ref[pl.ds(start, count), columns] = part


    step = width // 2

    @pl.loop(0, width // step)
    def _(n):
        columns = pl.ds(pl.multiple_of(n * step, step), step)
        store(columns, dot_nn(grad_ref[...], first_ref[:, columns]))

    store(pl.ds(width, LANES), extra_scratch[...])


def run_experts(
    groups, tp_index, tp_count, expert_count, rows, upstream, mask, picks, router, first, down, earlier
):
    span_rows, width = rows.shape
    steps = len(groups)
    hidden_all = down.shape[0]
    segments = picks.shape[0] // 2
    group_rows = mask.shape[0] // 4
    here = lambda k, place: (place[k], 0)
    fixed = lambda k, place: (0, 0)

    def whole(array):
        return pl.BlockSpec(array.shape, fixed, pipeline_mode=pl.Buffered(1))

    in_specs = [
        pl.BlockSpec((group_rows, width), here),
        pl.BlockSpec((group_rows, width), here),
        pl.BlockSpec((group_rows, LANES), here),
        whole(picks),
        whole(router),
        whole(first),
        whole(down),
    ] + [pl.BlockSpec(memory_space=pl.ANY)] * len(earlier)
    flops = 2 * steps * group_rows * width * 5 * hidden_all
    return pl.pallas_call(
        lambda *refs: expert_kernel(tp_count, expert_count, *refs),
        grid_spec=pltpu.PrefetchScalarGridSpec(
            num_scalar_prefetch=1,
            grid=(steps,),
            in_specs=in_specs,
            out_specs=[pl.BlockSpec((group_rows, width + LANES), fixed)] * 2
            + [
                pl.BlockSpec((group_rows, 2 * hidden_all), here),
                pl.BlockSpec((group_rows, hidden_all), here),
            ],
            scratch_shapes=[
                pltpu.VMEM((segments, group_rows, LANES), F32),
                pltpu.VMEM((group_rows, LANES), F32),
                pltpu.VMEM((group_rows, hidden_all), F32),
            ],
        ),
        out_shape=[jax.ShapeDtypeStruct((group_rows, width + LANES), BF16)] * 2
        + [
            jax.ShapeDtypeStruct((span_rows, 2 * hidden_all), BF16),
            jax.ShapeDtypeStruct((span_rows, hidden_all), BF16),
        ],
        input_output_aliases={8 + i: 2 + i for i in range(len(earlier))},
        compiler_params=pltpu.CompilerParams(vmem_limit_bytes=58 << 20),
        cost_estimate=pl.CostEstimate(
            flops=flops,
            bytes_accessed=2 * (first.size + down.size + steps * group_rows * (3 * width + 3 * hidden_all)),
            transcendentals=steps * group_rows * hidden_all,
        ),
        name="experts",
    )(jnp.stack([*groups, tp_index]).astype(jnp.int32), rows, upstream, mask, picks, router, first, down, *earlier)


def body(
    layer_input,
    cotangent,
    lengths,
    seq_order,
    routes,
    query_weight,
    key_weight,
    value_weight,
    mixing_weight,
    heads_bias,
    entry_gain,
    middle_gain,
    router_weight,
    shared_switch,
    shared_gate,
    shared_up,
    shared_down,
    expert_gate,
    expert_up,
    expert_down,
):
    tp_count = lax.axis_size("tp")
    ep_count = lax.axis_size("ep")
    dp_count = lax.axis_size("dp")
    part_count = dp_count * ep_count
    tp_index = lax.axis_index("tp")
    ep_index = lax.axis_index("ep")
    own_rows, width = layer_input.shape
    group_rows = own_rows * tp_count
    span_rows = group_rows * ep_count
    slice_rows = query_weight.shape[0]
    head_cols = query_weight.shape[1]
    head_count = head_cols // HD
    local_experts = expert_gate.shape[0]
    expert_count = router_weight.shape[1]
    hidden = expert_gate.shape[2]
    shared_hidden = shared_gate.shape[1] // ep_count
    segments = local_experts + 1
    seg = -(-max(hidden, shared_hidden) // LANES) * LANES

    span_lengths = jnp.take(
        lengths,
        lax.dynamic_slice_in_dim(seq_order, lax.axis_index("dp") * ep_count, ep_count, 0),
    )
    length = span_lengths[ep_index]
    own_keep = ((tp_index * own_rows + jnp.arange(own_rows)) < length).astype(F32)[:, None]
    block_of = jnp.arange(group_rows) // own_rows
    position = ((tp_index - block_of) % tp_count) * own_rows + jnp.arange(group_rows) % own_rows

    span_keep = (jnp.arange(group_rows)[None, :] < span_lengths[:, None]).reshape(span_rows, 1)
    lanes = jnp.arange(LANES)[None, :]
    column_of = jnp.concatenate(
        [ep_index * local_experts + jnp.arange(local_experts), jnp.array([expert_count])]
    )
    half = LANES // 2
    picks = jnp.concatenate([column_of, column_of + half])[:, None] == lanes
    picks = picks.astype(F32)

    bias_rows = heads_bias.size
    small = jnp.concatenate(
        [
            router_weight,
            shared_switch[:, None],
            entry_gain[:, None],
            middle_gain[:, None],
        ],
        axis=1,
    )
    bias_depth = -(-bias_rows // slice_rows)
    bias_cols = jnp.pad(heads_bias.reshape(-1), (0, bias_depth * slice_rows - bias_rows))
    bias_cols = bias_cols.reshape(bias_depth, slice_rows).T
    route_depth = -(-routes.size // slice_rows)
    route_cols = jnp.pad(routes.reshape(-1), (0, route_depth * slice_rows - routes.size))
    route_cols = route_cols.reshape(route_depth, slice_rows).T.astype(BF16)
    small = jnp.concatenate([small, bias_cols, route_cols], axis=1)
    small = jnp.pad(small, ((0, 0), (0, LANES - small.shape[1])))
    dense_own = jnp.concatenate(
        [query_weight, key_weight, value_weight, small], axis=1
    )
    dense_full = lax.all_gather(dense_own, ("dp", "ep"), axis=0, tiled=True)
    in_weight = dense_full[:, : 3 * head_cols]
    small_full = dense_full[:, 3 * head_cols :]
    out_weight = lax.all_gather(
        after(mixing_weight, dense_full), ("dp", "ep"), axis=1, tiled=True
    )
    small_rows = small_full[:, : expert_count + 3].astype(F32).T
    entry_full = small_rows[expert_count + 1][None]
    middle_full = small_rows[expert_count + 2][None]
    bias_full = small_full[:, expert_count + 3 : expert_count + 3 + bias_depth]
    bias_full = bias_full.reshape(part_count, slice_rows, bias_depth).transpose(0, 2, 1)
    bias_full = bias_full.reshape(part_count, -1)[:, :bias_rows]
    bias_full = bias_full.reshape((part_count,) + heads_bias.shape).transpose(1, 2, 0, 3)
    bias_full = bias_full.reshape(1, 3 * head_cols).astype(F32)

    route_at = expert_count + 3 + bias_depth
    span_routes = lax.dynamic_slice_in_dim(
        small_full[:, route_at : route_at + route_depth],
        lax.axis_index("dp") * ep_count * slice_rows,
        ep_count * slice_rows,
        0,
    )
    span_routes = span_routes.reshape(ep_count, slice_rows, route_depth).transpose(0, 2, 1)
    span_routes = span_routes.reshape(ep_count, -1)[:, : routes.size].reshape(span_rows, TOP)
    named = lanes == expert_count
    for k in range(TOP):
        named = named | (lanes == span_routes[:, k : k + 1].astype(jnp.int32))
    span_mask = (named & span_keep).astype(BF16)

    input_blocks = gather_blocks(layer_input, "tp")
    grad_blocks = gather_blocks(after(cotangent, input_blocks), "tp")
    input_values = jnp.concatenate(input_blocks, axis=0)

    def to_owners(matrix):
        return matrix.reshape(ep_count, shared_hidden, slice_rows)

    shared_own = jnp.concatenate(
        [to_owners(shared_gate.T), to_owners(shared_up.T), to_owners(shared_down)], axis=1
    )
    shared_own = after(shared_own, dense_full)
    shared_span = lax.all_to_all(shared_own, "ep", split_axis=0, concat_axis=0, tiled=True)
    freqs = THETA ** (-(jnp.arange(HD // 2).astype(F32) * 2.0) / HD)
    angles = position.astype(F32)[:, None] * freqs[None, :]
    angles = jnp.concatenate([angles, angles], axis=-1)
    cosine = jnp.cos(angles)[:, None, :]
    sine = jnp.sin(angles)[:, None, :]
    input_values = after(input_values, picks, cosine, sine).astype(F32)
    entry_unit, entry_inverse = norm_parts(input_values)
    entry_normed = (entry_unit * entry_full).astype(BF16)
    in_lin = dot_nn(entry_normed, in_weight) + bias_full
    query_heads = in_lin[:, :head_cols].reshape(group_rows, head_count, HD)
    key_heads = in_lin[:, head_cols : 2 * head_cols].reshape(group_rows, head_count, HD)
    query_rot = (query_heads * cosine + rotate(query_heads) * sine).astype(BF16)
    key_rot = (key_heads * cosine + rotate(key_heads) * sine).astype(BF16)
    value_heads = in_lin[:, 2 * head_cols :].astype(BF16).reshape(group_rows, head_count, HD)
    score_scale = HD ** (-0.5)
    causal = position[:, None] >= position[None, :]

    def score_matrix():
        raw_scores = jnp.einsum("qhd,khd->hqk", query_rot, key_rot, preferred_element_type=F32)
        return jnp.where(causal[None], raw_scores * score_scale, -1e30)

    scores = score_matrix()
    top_score = jnp.max(scores, axis=-1, keepdims=True)
    log_total = top_score + jnp.log(jnp.sum(jnp.exp(scores - top_score), axis=-1, keepdims=True))
    attn_probs = jnp.exp(scores - log_total).astype(BF16)
    context = jnp.einsum("hqk,khd->qhd", attn_probs, value_heads, preferred_element_type=F32)
    context_low = context.astype(BF16).reshape(group_rows, head_cols)
    context_low = after(context_low, shared_span)
    head_blocks = split_rows(dot_nn(context_low, out_weight).astype(BF16), tp_count)
    attention_parts = send_blocks(head_blocks, "tp")

    shared_span = after(shared_span, head_blocks)
    if dp_count == 2:
        shared_other = swapped(shared_span, "dp", 1)
        attention_parts = after(attention_parts, shared_other)
        shared_parts = in_order(shared_span, shared_other, lax.axis_index("dp"), 1)
    else:
        shared_parts = lax.all_gather(shared_span, "dp", axis=0, tiled=True)
    shared_parts = shared_parts.reshape(part_count, 3, shared_hidden, slice_rows)
    shared_parts = shared_parts.transpose(1, 2, 0, 3).reshape(3, shared_hidden, width)

    def stack_hidden(expert_rows, shared_rows):
        padded = [jnp.pad(rows, ((0, seg - rows.shape[0]), (0, 0))) for rows in expert_rows]
        padded.append(jnp.pad(shared_rows, ((0, seg - shared_hidden), (0, 0))))
        return padded

    gate_rows = stack_hidden([expert_gate[j].T for j in range(local_experts)], shared_parts[0])
    up_rows = stack_hidden([expert_up[j].T for j in range(local_experts)], shared_parts[1])
    down_rows = stack_hidden([expert_down[j] for j in range(local_experts)], shared_parts[2])
    first_weight = jnp.concatenate(
        [rows for pair in zip(gate_rows, up_rows) for rows in pair], axis=0
    )
    down_weight = jnp.concatenate(down_rows, axis=0)

    grad_blocks = after(grad_blocks, head_blocks)
    group_upstream = jnp.concatenate(grad_blocks, axis=0)
    near = swapped(group_upstream, "ep", 2)

    attention_parts = after(attention_parts, near)
    attention_own = add_up([head_blocks[0], *attention_parts])
    hidden_state = input_values[:own_rows] + own_keep * attention_own
    middle_unit, middle_inverse = norm_parts(hidden_state)
    middle_normed = (middle_unit * middle_full).astype(BF16)

    span_normed = lax.all_gather(middle_normed, ("ep", "tp"), axis=0, tiled=True)
    sibling, far = swapped(group_upstream, "ep", 1), swapped(near, "ep", 1)

    def upstream_moves(_, place, turn):
        moves = []
        for k in range(4):
            for j in range(tp_count):
                block = (place ^ k) * tp_count + lax.rem(turn - j + tp_count, tp_count)
                start = pl.multiple_of(block * own_rows, own_rows)
                moves.append((k, pl.ds(j * own_rows, own_rows), 0, pl.ds(start, own_rows)))
        return moves

    upstream = move_blocks(
        upstream_moves,
        [jax.ShapeDtypeStruct((span_rows, width), BF16)],
        [group_upstream, sibling, near, far],
        "order_rows",
    )[0]

    own_logits = dot_nn(middle_normed, small_full)
    expert_probs = jax.nn.softmax(own_logits[:, :expert_count], axis=-1)
    switch_value = jax.nn.sigmoid(own_logits[:, expert_count : expert_count + 1])
    own_routes = lax.dynamic_slice_in_dim(routes, tp_index * own_rows, own_rows, 0)
    route_mask = jnp.any(
        own_routes[:, :, None] == jnp.arange(expert_count)[None, None, :], axis=1
    ).astype(F32)

    first_weight, down_weight = after((first_weight, down_weight), middle_normed)
    span_mask = after(span_mask, expert_probs, switch_value, route_mask)
    shared_operands = (span_normed, upstream, span_mask, picks, small_full.T, first_weight, down_weight)
    sibling_back, chip_back, *made = run_experts(
        (ep_index ^ 3, ep_index ^ 2), tp_index, tp_count, expert_count, *shared_operands, ()
    )
    chip_sum = add_up([chip_back, swapped(sibling_back, "ep", 1)]).astype(BF16)
    from_chip = swapped(chip_sum, "ep", 2)
    sibling_back, group_back, first_grad, hidden_gated = run_experts(
        (after(ep_index ^ 1, chip_sum), ep_index),
        tp_index,
        tp_count,
        expert_count,
        *shared_operands,
        made,
    )
    from_core = [swapped(block, "ep", 1) for block in split_rows(sibling_back, tp_count)]
    down_grad = dot_tn(hidden_gated, upstream).astype(BF16)

    def last_moves(*_):
        return [
            (0, pl.ds(j * seg, hidden), 0, pl.ds(j * hidden, hidden)) for j in range(local_experts)
        ]

    last_own = move_blocks(
        last_moves,
        [jax.ShapeDtypeStruct((local_experts * hidden, width), BF16)],
        [down_grad],
        "down_rows",
    )[0]
    last_other = swapped_or_none(last_own, "dp")
    from_core = after(from_core, last_own)
    back_blocks = [
        add_up(blocks)
        for blocks in zip(
            split_rows(group_back, tp_count), from_core, split_rows(from_chip, tp_count)
        )
    ]
    back_blocks = [back_blocks[0]] + [block.astype(BF16) for block in back_blocks[1:]]
    back_parts = send_blocks(back_blocks, "tp")

    first_grad = after(first_grad, back_blocks)
    first_weight_grad = dot_tn(first_grad, span_normed).astype(BF16)
    shared_size = width // dp_count

    def first_moves(place, *_):
        moves = [
            (0, pl.ds((2 * j + part) * seg, hidden), part, pl.ds(j * hidden, hidden))
            for part in range(2)
            for j in range(local_experts)
        ]
        starts = (place, 1 - place) if dp_count == 2 else (0, 0)
        for k, start in enumerate(starts):
            columns = pl.ds(0, width)
            if dp_count == 2:
                columns = pl.ds(pl.multiple_of(start * shared_size, LANES), shared_size)
            for part, (array, base) in enumerate(
                ((0, 2 * local_experts * seg), (0, (2 * local_experts + 1) * seg), (1, local_experts * seg))
            ):
                moves.append(
                    (
                        array,
                        (pl.ds(base, shared_hidden), columns),
                        2 + k,
                        pl.ds(part * shared_hidden, shared_hidden),
                    )
                )
        return moves

    shared_shape = (3 * shared_hidden, shared_size if dp_count == 2 else width)
    *first_own, shared_kept, shared_given = move_blocks(
        first_moves,
        [jax.ShapeDtypeStruct((local_experts * hidden, width), BF16)] * 2
        + [jax.ShapeDtypeStruct(shared_shape, BF16)] * 2,
        [first_weight_grad, down_grad],
        "first_rows",
    )
    first_other = [swapped_or_none(part, "dp") for part in first_own]
    hidden_gated = after(hidden_gated, first_own)
    branch = dot_nn(hidden_gated, down_weight).astype(BF16)
    branch_terms = lax.all_to_all(
        branch.reshape(ep_count, group_rows, width), "ep", split_axis=0, concat_axis=0, tiled=True
    )
    back_parts = after(back_parts, branch, shared_kept, shared_given)
    if dp_count == 2:
        back_parts = after(back_parts, last_other)
    back_own = add_up([back_blocks[0], *back_parts])

    normed_own = back_own[:, :width]
    gate_sums = back_own[:, width : width + half] + back_own[:, width + half :]
    prob_grad = own_keep * route_mask * gate_sums[:, :expert_count]
    logit_grad = expert_probs * (
        prob_grad - jnp.sum(expert_probs * prob_grad, axis=-1, keepdims=True)
    )
    switch_grad = (
        own_keep
        * gate_sums[:, expert_count : expert_count + 1]
        * switch_value
        * (1.0 - switch_value)
    )
    score_grad = jnp.concatenate([logit_grad, switch_grad], axis=1)
    normed_total = normed_own + dot_exact(score_grad, small_rows[: expert_count + 1], ((1,), (0,)))
    router_part = dot_exact(score_grad, middle_normed.astype(F32), ((0,), (0,)))
    middle_part = jnp.sum(normed_total * middle_unit, axis=0, keepdims=True)
    state_grad = cotangent.astype(F32) + norm_back(
        normed_total, middle_full, middle_unit, middle_inverse
    )
    attention_grad_own = (own_keep * state_grad).astype(BF16)
    attention_grad_blocks = gather_blocks(attention_grad_own, "tp")

    if dp_count == 2:
        attention_grad_blocks = after(attention_grad_blocks, first_other[0])
    attention_grad = jnp.concatenate(attention_grad_blocks, axis=0)
    shared_other = swapped_or_none(shared_given, "dp")

    mixing_grad = dot_tn(attention_grad, context_low).astype(BF16)
    context_grad = dot_nt(attention_grad, out_weight)
    context_grad = context_grad.astype(BF16).reshape(group_rows, head_count, HD)
    probs_again = jnp.exp(score_matrix() - log_total)
    probs_low = probs_again.astype(BF16)
    value_grad = jnp.einsum("hqk,qhd->khd", probs_low, context_grad, preferred_element_type=F32)
    value_grad = value_grad.astype(BF16).reshape(group_rows, head_cols)
    prob_grads = jnp.einsum("qhd,khd->hqk", context_grad, value_heads, preferred_element_type=F32)
    row_delta = jnp.sum(probs_again * prob_grads, axis=-1, keepdims=True)
    score_grads = (probs_again * (prob_grads - row_delta)).astype(BF16)
    query_rot_grad = (
        jnp.einsum("hqk,khd->qhd", score_grads, key_rot, preferred_element_type=F32) * score_scale
    )
    key_rot_grad = (
        jnp.einsum("hqk,qhd->khd", score_grads, query_rot, preferred_element_type=F32) * score_scale
    )
    query_grad = (query_rot_grad * cosine + unrotate(query_rot_grad * sine)).astype(BF16)
    key_grad = (key_rot_grad * cosine + unrotate(key_rot_grad * sine)).astype(BF16)
    in_grad = jnp.concatenate(
        [query_grad.reshape(group_rows, head_cols), key_grad.reshape(group_rows, head_cols), value_grad],
        axis=1,
    )
    bias_grad = jnp.sum(in_grad.astype(F32), axis=0)
    entry_part = dot_nt(in_grad, in_weight)
    entry_blocks = split_rows(entry_part.astype(BF16), tp_count)
    entry_parts = send_blocks(entry_blocks, "tp")
    if dp_count == 2:
        shared_mine = add_up([shared_kept, after(shared_other, entry_parts)]).astype(BF16)
    else:
        shared_mine = lax.psum_scatter(shared_kept, "dp", scatter_dimension=1, tiled=True)
    shared_mine = shared_mine.reshape(3 * shared_hidden, ep_count, slice_rows).transpose(1, 0, 2)
    shared_back = lax.all_to_all(shared_mine, "ep", split_axis=0, concat_axis=0, tiled=True)
    shared_back = shared_back.reshape(ep_count, 3, shared_hidden, slice_rows).astype(F32)
    entry_own = add_up([entry_blocks[0], *entry_parts])
    input_gradient = state_grad + norm_back(
        entry_own, entry_full, entry_unit[:own_rows], entry_inverse[:own_rows]
    )

    entry_gain_part = jnp.sum(entry_part * entry_unit, axis=0, keepdims=True)
    small_part = jnp.concatenate([router_part, middle_part, entry_gain_part], axis=0)
    bias_part = bias_grad.reshape(3, head_count, part_count, -1).transpose(2, 0, 1, 3)
    bias_part = bias_part.reshape(part_count, bias_rows)
    bias_part = jnp.pad(bias_part, ((0, 0), (0, bias_depth * slice_rows - bias_rows)))
    bias_part = bias_part.reshape(part_count, bias_depth, slice_rows).transpose(1, 0, 2)
    bias_part = bias_part.reshape(bias_depth, width)
    small_part = jnp.concatenate([small_part, bias_part], axis=0)
    small_high, small_low = split_pair(small_part)
    small_count = small_part.shape[0]
    small_cols = jnp.concatenate(
        [
            jnp.pad(small_high, ((0, half - small_count), (0, 0))),
            jnp.pad(small_low, ((0, half - small_count), (0, 0))),
        ],
        axis=0,
    ).T
    dense_grad = jnp.concatenate(
        [
            dot_tn(entry_normed, in_grad).astype(BF16),
            mixing_grad,
            small_cols,
        ],
        axis=1,
    )
    if dp_count == 2:
        dense_grad = after(dense_grad, first_other[1], branch_terms)
    dense_sum = lax.psum_scatter(
        dense_grad, ("dp", "ep"), scatter_dimension=0, tiled=True
    ).astype(F32)
    small_sum = dense_sum[:, 4 * head_cols : 4 * head_cols + half] + dense_sum[:, 4 * head_cols + half :]
    tp_sum = ordered_sum(small_sum[:, : expert_count + 3].T, "tp")
    bias_sum = small_sum[:, expert_count + 3 : expert_count + 3 + bias_depth]
    bias_sum = bias_sum.T.reshape(-1)[:bias_rows].reshape(heads_bias.shape)

    branch_terms = after(branch_terms, entry_blocks)
    branch_blocks = []
    for j in range(tp_count):
        start = ((tp_index - j) % tp_count) * own_rows
        rows = lax.dynamic_slice_in_dim(branch_terms, start, own_rows, 1)
        branch_blocks.append(jnp.sum(rows.astype(F32), axis=0))
    branch_blocks = [branch_blocks[0]] + [block.astype(BF16) for block in branch_blocks[1:]]
    branch_parts = send_blocks(branch_blocks, "tp")
    layer_output = (hidden_state + add_up([branch_blocks[0], *branch_parts])).astype(BF16)
    if dp_count == 2:
        first_other = after(first_other, entry_parts, tp_sum)
    first_sum = [
        whole_sum(own, other, "dp").reshape(local_experts, hidden, width)
        for own, other in zip(first_own, first_other)
    ]
    last_sum = whole_sum(last_own, last_other, "dp").reshape(local_experts, hidden, width)

    def by_columns(rows):
        return rows.transpose(2, 0, 1).reshape(slice_rows, ep_count * shared_hidden)

    return (
        layer_output,
        input_gradient,
        dense_sum[:, :head_cols],
        dense_sum[:, head_cols : 2 * head_cols],
        dense_sum[:, 2 * head_cols : 3 * head_cols],
        dense_sum[:, 3 * head_cols : 4 * head_cols].T,
        bias_sum,
        tp_sum[expert_count + 2],
        tp_sum[expert_count + 1],
        tp_sum[:expert_count].T,
        tp_sum[expert_count],
        by_columns(shared_back[:, 0]),
        by_columns(shared_back[:, 1]),
        shared_back[:, 2].reshape(ep_count * shared_hidden, slice_rows),
        first_sum[0].transpose(0, 2, 1),
        first_sum[1].transpose(0, 2, 1),
        last_sum,
    )


def solution(mesh):
    rows = P(("dp", "ep", "tp"), None)
    parts = P(("dp", "ep"))
    in_cols = P(("dp", "ep"), "tp")
    out_cols = P("tp", ("dp", "ep"))
    weights = (
        in_cols,
        in_cols,
        in_cols,
        out_cols,
        P(None, "tp", ("dp", "ep")),
        parts,
        parts,
        P(("dp", "ep"), None),
        parts,
        in_cols,
        in_cols,
        out_cols,
        P("ep", None, "tp"),
        P("ep", None, "tp"),
        P("ep", "tp", None),
    )
    return jax.shard_map(
        body,
        mesh=mesh,
        in_specs=(rows, rows, P(), P(), P(("dp", "ep"), None)) + weights,
        out_specs=(rows, rows) + weights,
        check_vma=False,
    )
```

time: 1020 us -> 748 us (0.73)
  waiting for transfers between devices: 563 us -> 288 us
  Pallas kernels: 0 us -> 93.5 us
  matrix products: 183 us -> 95.2 us
  local copies, waits for them, and re-layouts: 109 us -> 87.1 us
  other arithmetic: 70.2 us -> 88 us
    ppermute x6 -> x14, waiting for transfers between devices: 278 us -> 102 us  [swapped(): return lax.ppermute(values, axis, [(i, i ^ bit) for i in range(count)])]
    pallas_call x0 -> x5, Pallas kernels: none -> 93.5 us  [the longest x2 85.9 us: run_experts(): pl.pallas_call(lambda *refs: expert_kernel(tp_count, expert_count, *refs)...]
    unnamed x8 -> x4, waiting for transfers between devices: 60.8 us -> 0.07 us
    dot_general x4 -> x2, matrix products: 65.5 us -> 8.61 us  [dot_nt(): lax.dot_general(left, right, (((1,), (1,)), ((), ())), preferred_element_...]
    ppermute x6 -> x14, starting transfers between devices: 37.4 us -> 9.69 us  [swapped(): return lax.ppermute(values, axis, [(i, i ^ bit) for i in range(count)])]
    dot_general x5 -> x4, matrix products: 52.3 us -> 26.1 us  [dot_nn(): lax.dot_general(left, right, (((1,), (0,)), ((), ())), preferred_element_...]
    ppermute x12 -> x24, starting transfers between devices: 19.1 us -> 45.1 us  [shifted(): lax.ppermute(block, axis, [(i, (i + step) % count) for i in range(count)])]
    ppermute x12 -> x24, waiting for transfers between devices: 134 us -> 110 us  [shifted(): lax.ppermute(block, axis, [(i, (i + step) % count) for i in range(count)])]
  transfers between devices with their start and end apart: 26 -> 45, of which waited for: 16 -> 16; matrix products, arithmetic and copies ran while one was open for 23% -> 30% of each run, Pallas kernels for 0% -> 7%
where the time goes in v2:
time: 748 us; the launch traced here: 737 us
  waiting for transfers between devices  288 us (39%)
  matrix products  95.2 us (13%)
  Pallas kernels  93.5 us (12%)
  other arithmetic  88 us (12%)
  local copies, waits for them, and re-layouts  87.1 us (12%)
  starting transfers between devices  69.9 us (9%)
  between operations  15.6 us (2%)
    ppermute x24, waiting for transfers between devices, shifted(): lax.ppermute(block, axis, [(i, (i + step) % count) for i in range(count)])  110 us
    ppermute x14, waiting for transfers between devices, swapped(): return lax.ppermute(values, axis, [(i, i ^ bit) for i in range(count)])  102 us
    pallas_call x2, Pallas kernels, run_experts(): pl.pallas_call(lambda *refs: expert_kernel(tp_count, expert_count, *refs)...  85.9 us
    dot_general x4, matrix products, dot_tn(): lax.dot_general(left, right, (((0,), (0,)), ((), ())), preferred_element_...  47.4 us
    ppermute x24, starting transfers between devices, shifted(): lax.ppermute(block, axis, [(i, (i + step) % count) for i in range(count)])  45.1 us
    unnamed x181, local copies, waits for them, and re-layouts  39.9 us
    all_gather x1, waiting for transfers between devices, body(): lax.all_gather(middle_normed, ('ep', 'tp'), axis=0, tiled=True)  33.4 us
    dot_general x4, matrix products, dot_nn(): lax.dot_general(left, right, (((1,), (0,)), ((), ())), preferred_element_...  26.1 us
  transfers between devices with their start and end apart: 45, of which 16 were waited for; matrix products, arithmetic and copies ran while one was open for 30% of the time, Pallas kernels for 7%

profile of v2, /device:TPU:0, one launch (start us, length us, event | category | flops | bytes accessed | tf_op | source)
XLA Modules:
  0.0 736.9 jit_solution(15280549782721130281)
XLA Ops:
  16.3 5.1 collective-permute-start.2
  26.0 2.7 pad_maximum_fusion.2
  28.6 5.4 collective-permute-done.2
  34.1 32.4 %collective-permute-done.1 = bf16[128,2048]{1,0:T(8,128)(2,1)} collective-permute-done((bf16[128,2048]{1,0:T(8,128)(2,1)}, bf16[128,2048]{1,0:T(8,128)(2,1)}, u32[]{:S(2)}, u32[]{:S(2)}) %collective-permute-start.1) | collective-permute-done | bytes 524320 | tf_op jit(solution)/shard_map/ppermute | solution.py:63
  69.3 2.9 collective-permute-start.9
  77.0 5.7 fusion.10
  88.3 4.5 all-to-all-start
  99.3 24.1 %all-to-all-done = bf16[4,1056,256]{2,1,0:T(8,128)(2,1)} async-done(((bf16[4,1056,256]{2,1,0:T(8,128)(2,1)}), bf16[4,1056,256]{2,1,0:T(8,128)(2,1)}, u32[]{:S(2)}, u32[]{:S(2)}) %all-to-all-start) | async-done | bytes 2162720 | tf_op jit(solution)/shard_map/all_to_all | solution.py:426
  123.4 2.9 convolution_convert_fusion.5
  140.9 6.9 collective-permute-done.3
  147.8 32.4 %collective-permute-done.4 = bf16[128,2048]{1,0:T(8,128)(2,1)S(1)} collective-permute-done((bf16[128,2048]{1,0:T(8,128)(2,1)}, bf16[128,2048]{1,0:T(8,128)(2,1)S(1)}, u32[]{:S(2)}, u32[]{:S(2)}) %collective-permute-start.4) | collective-permute-done | bytes 524320 | tf_op jit(solution)/shard_map/ppermute | solution.py:63
  198.2 4.0 fusion.27.refs_3_
  206.8 2.6 broadcast_select_fusion.1
  221.4 3.3 copy-done.3
  224.7 33.4 %all-gather.8.cloned.1.call-done.refs_1_ = bf16[2048,2048]{1,0:T(8,128)(2,1)} async-done(((bf16[128,2048]{1,0:T(8,128)(2,1)}), bf16[2048,2048]{1,0:T(8,128)(2,1)}) %all-gather.8.cloned.1.call-update) | async-done | bytes 8388624 | tf_op jit(solution)/shard_map/all_gather | solution.py:491
  258.1 43.1 %experts.2 = (bf16[512,2176]{1,0:T(8,128)(2,1)}, bf16[512,2176]{1,0:T(8,128)(2,1)}, bf16[2048,2304]{1,0:T(8,128)(2,1)}, bf16[2048,1152]{1,0:T(8,128)(2,1)}) custom-call(s32[3]{0:T(128)} %add_add_fusion.1.refs_0_, bf16[2048,2048]{1,0:T(8,128)(2,1)} %all-gather.8.cloned.1.call-done.refs_1_, bf16[2048,2048]{1,0:T(8,128)(2,1)} %copy-done.3, ...), custom_call_target="tpu_custom_call" | custom-call | flops 24159191040 | bytes 33816576 | tf_op jit(solution)/shard_map/experts/pallas_call | solution.py:273
  302.9 2.9 collective-permute-done.13
  305.7 3.6 add_convert_fusion
  310.5 42.8 %experts.3 = (bf16[512,2176]{1,0:T(8,128)(2,1)}, bf16[512,2176]{1,0:T(8,128)(2,1)}, bf16[2048,2304]{1,0:T(8,128)(2,1)}, bf16[2048,1152]{1,0:T(8,128)(2,1)}) custom-call(s32[3]{0:T(128)} %add_add_fusion.2.refs_0_, bf16[2048,2048]{1,0:T(8,128)(2,1)} %all-gather.8.cloned.1.call-done.refs_1_, ...), custom_call_target="tpu_custom_call", output_to_operand_aliasing={{2}: (8, {}), {3}: (9, {})} | custom-call | flops 24159191040 | bytes 33816576 | tf_op jit(solution)/shard_map/experts/pallas_call | solution.py:273
  356.0 13.8 %convolution_convert_fusion.3.refs_0_.refs_1_ = bf16[1152,2048]{1,0:T(8,128)(2,1)S(1)} fusion(bf16[2048,1152]{1,0:T(8,128)(2,1)} %get-tuple-element.105, bf16[2048,2048]{1,0:T(8,128)(2,1)} %copy-done.3), kind=kOutput, calls=%fused_computation.13 | convolution fusion | flops 9666035712 | bytes 17825792 | tf_op jit(solution)/shard_map/dot_general | solution.py:26
  378.2 26.3 %convolution_convert_fusion.refs_0_ = bf16[2304,2048]{1,0:T(8,128)(2,1)} fusion(bf16[2048,2304]{1,0:T(8,128)(2,1)} %get-tuple-element.102, bf16[2048,2048]{1,0:T(8,128)(2,1)} %all-gather.8.cloned.1.call-done.refs_1_), kind=kOutput, calls=%fused_computation.3 | convolution fusion | flops 19332071424 | bytes 27262976 | tf_op jit(solution)/shard_map/dot_general | solution.py:26
  404.5 3.7 copy-done.2
  408.2 4.0 first_rows.1
  412.9 16.2 %convolution_convert_fusion.2 = bf16[2048,2048]{1,0:T(8,128)(2,1)} fusion(bf16[2048,1152]{1,0:T(8,128)(2,1)} %get-tuple-element.105, bf16[1152,2048]{1,0:T(8,128)(2,1)S(1)} %bitcast.183), kind=kOutput, calls=%fused_computation.12 | convolution fusion | flops 9667870720 | bytes 17825792 | tf_op jit(solution)/shard_map/dot_general | solution.py:18
  429.1 7.4 %collective-permute-done.22 = bf16[704,2048]{1,0:T(8,128)(2,1)S(1)} collective-permute-done((bf16[704,2048]{1,0:T(8,128)(2,1)S(1)}, bf16[704,2048]{1,0:T(8,128)(2,1)S(1)}, u32[]{:S(2)}, u32[]{:S(2)}) %collective-permute-start.22) | collective-permute-done | bytes 2883616 | tf_op jit(solution)/shard_map/ppermute | solution.py:113
  447.1 3.1 multiply_reduce_fusion.3
  458.0 5.7 all-to-all-start.1
  465.3 3.8 collective-permute-done.23
  469.1 19.9 %collective-permute-done.24 = bf16[128,2048]{1,0:T(8,128)(2,1)} collective-permute-done((bf16[128,2048]{1,0:T(8,128)(2,1)}, bf16[128,2048]{1,0:T(8,128)(2,1)}, u32[]{:S(2)}, u32[]{:S(2)}) %collective-permute-start.24) | collective-permute-done | bytes 524320 | tf_op jit(solution)/shard_map/ppermute | solution.py:63
  489.1 9.4 %collective-permute-done.26 = bf16[704,2048]{1,0:T(8,128)(2,1)} collective-permute-done((bf16[704,2048]{1,0:T(8,128)(2,1)}, bf16[704,2048]{1,0:T(8,128)(2,1)}, u32[]{:S(2)}, u32[]{:S(2)}) %collective-permute-start.26) | collective-permute-done | bytes 2883616 | tf_op jit(solution)/shard_map/ppermute | solution.py:113
  505.8 2.7 multiply_reduce_fusion.1
  515.4 7.3 multiply_reduce_fusion
  530.2 3.2 convolution_convert_fusion.4
  533.4 4.1 convolution_convert_fusion.1
  537.5 4.3 pad_maximum_fusion
  541.8 17.6 %collective-permute-done.33 = bf16[704,2048]{1,0:T(8,128)(2,1)} collective-permute-done((bf16[704,2048]{1,0:T(8,128)(2,1)}, bf16[704,2048]{1,0:T(8,128)(2,1)}, u32[]{:S(2)}, u32[]{:S(2)}) %collective-permute-start.33) | collective-permute-done | bytes 2883616 | tf_op jit(solution)/shard_map/ppermute | solution.py:113
  567.0 64.2 %collective-permute-done.37 = bf16[1056,1024]{1,0:T(8,128)(2,1)S(1)} collective-permute-done((bf16[1056,1024]{1,0:T(8,128)(2,1)}, bf16[1056,1024]{1,0:T(8,128)(2,1)S(1)}, u32[]{:S(2)}, u32[]{:S(2)}) %collective-permute-start.37) | collective-permute-done | bytes 2162720 | tf_op jit(solution)/shard_map/ppermute | solution.py:113
  634.6 4.5 all-to-all-start.2
  639.2 5.5 convert_add_fusion
  646.7 5.7 dynamic-slice_reduce_fusion.2
  653.7 2.9 collective-permute-start.27
  657.1 17.9 %all-to-all-done.2 = bf16[4,1056,256]{2,1,0:T(8,128)(2,1)} async-done(((bf16[4,1056,256]{2,1,0:T(8,128)(2,1)}), bf16[4,1056,256]{2,1,0:T(8,128)(2,1)}, u32[]{:S(2)}, u32[]{:S(2)}) %all-to-all-start.2) | async-done | bytes 2162720 | tf_op jit(solution)/shard_map/all_to_all | solution.py:664
  675.0 3.1 fusion.76
  683.4 7.9 %collective-permute-done.28 = bf16[128,2048]{1,0:T(8,128)(2,1)} collective-permute-done((bf16[128,2048]{1,0:T(8,128)(2,1)}, bf16[128,2048]{1,0:T(8,128)(2,1)}, u32[]{:S(2)}, u32[]{:S(2)}) %collective-permute-start.28) | collective-permute-done | bytes 524320 | tf_op jit(solution)/shard_map/ppermute | solution.py:63
  691.3 4.2 multiply_add_fusion
  697.9 11.4 %collective-permute-start.34 = (f32[11,256]{1,0:T(8,128)S(1)}, f32[11,256]{1,0:T(8,128)S(1)}, u32[]{:S(2)}, u32[]{:S(2)}) collective-permute-start(f32[11,256]{1,0:T(8,128)S(1)} %slice_bitcast_fusion.9), channel_id=1, source_target_pairs={{0,3},{1,0},{2,1},{3,2},{4,7},{5,4},{6,5},{7,6},{8,11},{9,8},{10,9... | collective-permute-start | bytes 33800 | tf_op jit(solution)/shard_map/ppermute | solution.py:63
  717.3 6.4 convert_add_fusion.2
  723.7 6.4 convert_add_fusion.1
  (380 shorter events, 168.2 us)
Async XLA Ops:
  7.2 129.7 %copy-start = (s32[8]{0:T(128)S(1)}, s32[8]{0:T(128)}, u32[]{:S(2)}) copy-start(s32[8]{0:T(128)} %param.23) | copy-start | bytes 100
  7.2 67.2 %all-gather.4.cloned.1.call-start = ((), (), s32[]{:S(2)}) async-start(), calls=%async_computation.4 | async-start | bytes 7667712 | tf_op jit(solution)/shard_map/all_gather | solution.py:386
  16.2 107.1 %all-gather.6.cloned.1.call-start = ((), (), s32[]{:S(2)}) async-start(), calls=%async_computation.5 | async-start | bytes 2359296 | tf_op jit(solution)/shard_map/all_gather | solution.py:389
  16.3 17.8 %collective-permute-start.2 = (bf16[128,2048]{1,0:T(8,128)(2,1)}, bf16[128,2048]{1,0:T(8,128)(2,1)}, u32[]{:S(2)}, u32[]{:S(2)}) collective-permute-start(bf16[128,2048]{1,0:T(8,128)(2,1)} %param.21), channel_id=1, source_target_pairs={{0,3},{1,0},{2,1},{3,2},{4,7},{5,4},{6,5},{7,6},{8,11},{9,8},{10,9... | collective-permute-start | bytes 1572872 | tf_op jit(solution)/shard_map/ppermute | solution.py:63
  21.4 45.1 %collective-permute-start.1 = (bf16[128,2048]{1,0:T(8,128)(2,1)}, bf16[128,2048]{1,0:T(8,128)(2,1)}, u32[]{:S(2)}, u32[]{:S(2)}) collective-permute-start(bf16[128,2048]{1,0:T(8,128)(2,1)} %param.21), channel_id=1, source_target_pairs={{0,2},{1,3},{2,0},{3,1},{4,6},{5,7},{6,4},{7,5},{8,10},{9,11},{10,... | collective-permute-start | bytes 1572872 | tf_op jit(solution)/shard_map/ppermute | solution.py:63
  21.4 45.1 %collective-permute-start = (bf16[128,2048]{1,0:T(8,128)(2,1)}, bf16[128,2048]{1,0:T(8,128)(2,1)}, u32[]{:S(2)}, u32[]{:S(2)}) collective-permute-start(bf16[128,2048]{1,0:T(8,128)(2,1)} %param.21), channel_id=1, source_target_pairs={{0,1},{1,2},{2,3},{3,0},{4,5},{5,6},{6,7},{7,4},{8,9},{9,10},{10,1... | collective-permute-start | bytes 1572872 | tf_op jit(solution)/shard_map/ppermute | solution.py:63
  66.5 62.6 %collective-permute-start.7 = (bf16[128,2048]{1,0:T(8,128)(2,1)S(1)}, bf16[128,2048]{1,0:T(8,128)(2,1)}, u32[]{:S(2)}, u32[]{:S(2)}) collective-permute-start(bf16[128,2048]{1,0:T(8,128)(2,1)S(1)} %copy-done.24), channel_id=1, source_target_pairs={{0,1},{1,2},{2,3},{3,0},{4,5},{5,6},{6,7},{7,4},{8,9},{9,10},{10,1... | collective-permute-start | bytes 1572872 | tf_op jit(solution)/shard_map/ppermute | solution.py:63
  67.4 61.7 %collective-permute-start.8 = (bf16[128,2048]{1,0:T(8,128)(2,1)S(1)}, bf16[128,2048]{1,0:T(8,128)(2,1)}, u32[]{:S(2)}, u32[]{:S(2)}) collective-permute-start(bf16[128,2048]{1,0:T(8,128)(2,1)S(1)} %copy-done.24), channel_id=1, source_target_pairs={{0,2},{1,3},{2,0},{3,1},{4,6},{5,7},{6,4},{7,5},{8,10},{9,11},{10,... | collective-permute-start | bytes 1572872 | tf_op jit(solution)/shard_map/ppermute | solution.py:63
  69.3 59.8 %collective-permute-start.9 = (bf16[128,2048]{1,0:T(8,128)(2,1)S(1)}, bf16[128,2048]{1,0:T(8,128)(2,1)}, u32[]{:S(2)}, u32[]{:S(2)}) collective-permute-start(bf16[128,2048]{1,0:T(8,128)(2,1)S(1)} %copy-done.24), channel_id=1, source_target_pairs={{0,3},{1,0},{2,1},{3,2},{4,7},{5,4},{6,5},{7,6},{8,11},{9,8},{10,9... | collective-permute-start | bytes 1572872 | tf_op jit(solution)/shard_map/ppermute | solution.py:63
  77.0 105.0 %copy-start.51 = (f32[1,2048]{1,0:T(1,128)}, f32[1,2048]{1,0:T(1,128)S(1)}, u32[]{:S(2)}) copy-start(f32[1,2048]{1,0:T(1,128)S(1)} %get-tuple-element.295) | copy-start | bytes 24580
  88.3 35.1 %all-to-all-start = ((bf16[4,1056,256]{2,1,0:T(8,128)(2,1)}), bf16[4,1056,256]{2,1,0:T(8,128)(2,1)}, u32[]{:S(2)}, u32[]{:S(2)}) async-start(bf16[4,1056,256]{2,1,0:T(8,128)(2,1)} %pad_maximum_fusion.2), calls=%async_computation | async-start | bytes 4325376 | tf_op jit(solution)/shard_map/all_to_all | solution.py:426
  92.7 165.3 %all-gather.8.cloned.1.call-start = ((), (), s32[]{:S(2)}) async-start(), calls=%async_computation.6 | async-start | bytes 8912896 | tf_op jit(solution)/shard_map/all_gather | solution.py:491
  127.6 52.6 %collective-permute-start.6 = (bf16[4,1056,256]{2,1,0:T(8,128)(2,1)}, bf16[4,1056,256]{2,1,0:T(8,128)(2,1)}, u32[]{:S(2)}, u32[]{:S(2)}) collective-permute-start(bf16[4,1056,256]{2,1,0:T(8,128)(2,1)} %all-to-all-done), channel_id=1, source_target_pairs={{0,16},{16,0},{1,17},{17,1},{2,18},{18,2},{3,19},{19,3},{4,20},{20... | collective-permute-start | bytes 6488072 | tf_op jit(solution)/shard_map/ppermute | solution.py:113
  132.4 47.9 %collective-permute-start.10 = (bf16[512,2048]{1,0:T(8,128)(2,1)S(1)}, bf16[512,2048]{1,0:T(8,128)(2,1)}, u32[]{:S(2)}, u32[]{:S(2)}) collective-permute-start(bf16[512,2048]{1,0:T(8,128)(2,1)S(1)} %constant_dynamic-update-slice_fusion.refs_0_), channel_id=1, source_target_pairs={{0,8},{4,12},{8,0},{12,4},{1,9},{5,13},{9,1},{13,5},{2,10},{6,14},... | collective-permute-start | bytes 6291464 | tf_op jit(solution)/shard_map/ppermute | solution.py:113
  133.0 14.9 %collective-permute-start.3 = (bf16[128,2048]{1,0:T(8,128)(2,1)}, bf16[128,2048]{1,0:T(8,128)(2,1)S(1)}, u32[]{:S(2)}, u32[]{:S(2)}) collective-permute-start(bf16[128,2048]{1,0:T(8,128)(2,1)} %get-tuple-element.271), channel_id=1, source_target_pairs={{0,3},{1,0},{2,1},{3,2},{4,7},{5,4},{6,5},{7,6},{8,11},{9,8},{10,9... | collective-permute-start | bytes 1572872 | tf_op jit(solution)/shard_map/ppermute | solution.py:63
  134.6 45.6 %collective-permute-start.4 = (bf16[128,2048]{1,0:T(8,128)(2,1)}, bf16[128,2048]{1,0:T(8,128)(2,1)S(1)}, u32[]{:S(2)}, u32[]{:S(2)}) collective-permute-start(bf16[128,2048]{1,0:T(8,128)(2,1)} %get-tuple-element.270), channel_id=1, source_target_pairs={{0,2},{1,3},{2,0},{3,1},{4,6},{5,7},{6,4},{7,5},{8,10},{9,11},{10,... | collective-permute-start | bytes 1572872 | tf_op jit(solution)/shard_map/ppermute | solution.py:63
  135.2 45.1 %collective-permute-start.5 = (bf16[128,2048]{1,0:T(8,128)(2,1)}, bf16[128,2048]{1,0:T(8,128)(2,1)}, u32[]{:S(2)}, u32[]{:S(2)}) collective-permute-start(bf16[128,2048]{1,0:T(8,128)(2,1)} %get-tuple-element.269), channel_id=1, source_target_pairs={{0,1},{1,2},{2,3},{3,0},{4,5},{5,6},{6,7},{7,4},{8,9},{9,10},{10,1... | collective-permute-start | bytes 1572872 | tf_op jit(solution)/shard_map/ppermute | solution.py:63
  138.8 163.3 %copy-start.63 = (f32[128]{0:T(128)}, f32[128]{0:T(128)S(1)}, u32[]{:S(2)}) copy-start(f32[128]{0:T(128)S(1)} %compare_convert_fusion) | copy-start | bytes 1540
  204.1 15.0 %collective-permute-start.11 = (bf16[512,2048]{1,0:T(8,128)(2,1)S(1)}, bf16[512,2048]{1,0:T(8,128)(2,1)S(1)}, u32[]{:S(2)}, u32[]{:S(2)}) collective-permute-start(bf16[512,2048]{1,0:T(8,128)(2,1)S(1)} %constant_dynamic-update-slice_fusion.refs_0_), channel_id=1, source_target_pairs={{0,4},{4,0},{8,12},{12,8},{1,5},{5,1},{9,13},{13,9},{2,6},{6,2},{1... | collective-permute-start | bytes 6291464 | tf_op jit(solution)/shard_map/ppermute | solution.py:113
  204.1 15.0 %collective-permute-start.12 = (bf16[512,2048]{1,0:T(8,128)(2,1)}, bf16[512,2048]{1,0:T(8,128)(2,1)S(1)}, u32[]{:S(2)}, u32[]{:S(2)}) collective-permute-start(bf16[512,2048]{1,0:T(8,128)(2,1)} %collective-permute-done.10.refs_2_), channel_id=1, source_target_pairs={{0,4},{4,0},{8,12},{12,8},{1,5},{5,1},{9,13},{13,9},{2,6},{6,2},{1... | collective-permute-start | bytes 6291464 | tf_op jit(solution)/shard_map/ppermute | solution.py:113
  301.2 4.6 collective-permute-start.13
  309.3 63.5 %collective-permute-start.18 = (bf16[512,2176]{1,0:T(8,128)(2,1)}, bf16[512,2176]{1,0:T(8,128)(2,1)S(1)}, u32[]{:S(2)}, u32[]{:S(2)}) collective-permute-start(bf16[512,2176]{1,0:T(8,128)(2,1)} %add_convert_fusion), channel_id=1, source_target_pairs={{0,8},{4,12},{8,0},{12,4},{1,9},{5,13},{9,1},{13,5},{2,10},{6,14},... | collective-permute-start | bytes 6684680 | tf_op jit(solution)/shard_map/ppermute | solution.py:113
  354.9 16.2 %collective-permute-start.14 = (bf16[128,2176]{1,0:T(8,128)(2,1)S(1)}, bf16[128,2176]{1,0:T(8,128)(2,1)S(1)}, u32[]{:S(2)}, u32[]{:S(2)}) collective-permute-start(bf16[128,2176]{1,0:T(8,128)(2,1)S(1)} %get-tuple-element.260), channel_id=1, source_target_pairs={{0,4},{4,0},{8,12},{12,8},{1,5},{5,1},{9,13},{13,9},{2,6},{6,2},{1... | collective-permute-start | bytes 1671176 | tf_op jit(solution)/shard_map/ppermute | solution.py:113
  355.0 17.7 %collective-permute-start.15 = (bf16[128,2176]{1,0:T(8,128)(2,1)S(1)}, bf16[128,2176]{1,0:T(8,128)(2,1)S(1)}, u32[]{:S(2)}, u32[]{:S(2)}) collective-permute-start(bf16[128,2176]{1,0:T(8,128)(2,1)S(1)} %get-tuple-element.259), channel_id=1, source_target_pairs={{0,4},{4,0},{8,12},{12,8},{1,5},{5,1},{9,13},{13,9},{2,6},{6,2},{1... | collective-permute-start | bytes 1671176 | tf_op jit(solution)/shard_map/ppermute | solution.py:113
  355.5 17.2 %collective-permute-start.16 = (bf16[128,2176]{1,0:T(8,128)(2,1)S(1)}, bf16[128,2176]{1,0:T(8,128)(2,1)S(1)}, u32[]{:S(2)}, u32[]{:S(2)}) collective-permute-start(bf16[128,2176]{1,0:T(8,128)(2,1)S(1)} %get-tuple-element.258), channel_id=1, source_target_pairs={{0,4},{4,0},{8,12},{12,8},{1,5},{5,1},{9,13},{13,9},{2,6},{6,2},{1... | collective-permute-start | bytes 1671176 | tf_op jit(solution)/shard_map/ppermute | solution.py:113
  355.6 17.1 %collective-permute-start.17 = (bf16[128,2176]{1,0:T(8,128)(2,1)S(1)}, bf16[128,2176]{1,0:T(8,128)(2,1)S(1)}, u32[]{:S(2)}, u32[]{:S(2)}) collective-permute-start(bf16[128,2176]{1,0:T(8,128)(2,1)S(1)} %get-tuple-element.257), channel_id=1, source_target_pairs={{0,4},{4,0},{8,12},{12,8},{1,5},{5,1},{9,13},{13,9},{2,6},{6,2},{1... | collective-permute-start | bytes 1671176 | tf_op jit(solution)/shard_map/ppermute | solution.py:113
  371.2 65.4 %collective-permute-start.22 = (bf16[704,2048]{1,0:T(8,128)(2,1)S(1)}, bf16[704,2048]{1,0:T(8,128)(2,1)S(1)}, u32[]{:S(2)}, u32[]{:S(2)}) collective-permute-start(bf16[704,2048]{1,0:T(8,128)(2,1)S(1)} %down_rows.1), channel_id=1, source_target_pairs={{0,16},{16,0},{1,17},{17,1},{2,18},{18,2},{3,19},{19,3},{4,20},{20... | collective-permute-start | bytes 8650760 | tf_op jit(solution)/shard_map/ppermute | solution.py:113
  374.6 54.5 %collective-permute-start.19 = (bf16[128,2176]{1,0:T(8,128)(2,1)}, bf16[128,2176]{1,0:T(8,128)(2,1)S(1)}, u32[]{:S(2)}, u32[]{:S(2)}) collective-permute-start(bf16[128,2176]{1,0:T(8,128)(2,1)} %get-tuple-element.240), channel_id=1, source_target_pairs={{0,3},{1,0},{2,1},{3,2},{4,7},{5,4},{6,5},{7,6},{8,11},{9,8},{10,9... | collective-permute-start | bytes 1671176 | tf_op jit(solution)/shard_map/ppermute | solution.py:63
  376.1 53.0 %collective-permute-start.20 = (bf16[128,2176]{1,0:T(8,128)(2,1)}, bf16[128,2176]{1,0:T(8,128)(2,1)S(1)}, u32[]{:S(2)}, u32[]{:S(2)}) collective-permute-start(bf16[128,2176]{1,0:T(8,128)(2,1)} %get-tuple-element.239), channel_id=1, source_target_pairs={{0,2},{1,3},{2,0},{3,1},{4,6},{5,7},{6,4},{7,5},{8,10},{9,11},{10,... | collective-permute-start | bytes 1671176 | tf_op jit(solution)/shard_map/ppermute | solution.py:63
  376.9 52.2 %collective-permute-start.21 = (bf16[128,2176]{1,0:T(8,128)(2,1)}, bf16[128,2176]{1,0:T(8,128)(2,1)S(1)}, u32[]{:S(2)}, u32[]{:S(2)}) collective-permute-start(bf16[128,2176]{1,0:T(8,128)(2,1)} %get-tuple-element.238), channel_id=1, source_target_pairs={{0,1},{1,2},{2,3},{3,0},{4,5},{5,6},{6,7},{7,4},{8,9},{9,10},{10,1... | collective-permute-start | bytes 1671176 | tf_op jit(solution)/shard_map/ppermute | solution.py:63
  412.3 86.2 %collective-permute-start.26 = (bf16[704,2048]{1,0:T(8,128)(2,1)}, bf16[704,2048]{1,0:T(8,128)(2,1)}, u32[]{:S(2)}, u32[]{:S(2)}) collective-permute-start(bf16[704,2048]{1,0:T(8,128)(2,1)} %get-tuple-element.103), channel_id=1, source_target_pairs={{0,16},{16,0},{1,17},{17,1},{2,18},{18,2},{3,19},{19,3},{4,20},{20... | collective-permute-start | bytes 8650760 | tf_op jit(solution)/shard_map/ppermute | solution.py:113
  452.1 17.1 %collective-permute-start.23 = (bf16[128,2048]{1,0:T(8,128)(2,1)}, bf16[128,2048]{1,0:T(8,128)(2,1)}, u32[]{:S(2)}, u32[]{:S(2)}) collective-permute-start(bf16[128,2048]{1,0:T(8,128)(2,1)} %multiply_convert_fusion.2), channel_id=1, source_target_pairs={{0,1},{1,2},{2,3},{3,0},{4,5},{5,6},{6,7},{7,4},{8,9},{9,10},{10,1... | collective-permute-start | bytes 1572872 | tf_op jit(solution)/shard_map/ppermute | solution.py:63
  452.9 36.1 %collective-permute-start.24 = (bf16[128,2048]{1,0:T(8,128)(2,1)}, bf16[128,2048]{1,0:T(8,128)(2,1)}, u32[]{:S(2)}, u32[]{:S(2)}) collective-permute-start(bf16[128,2048]{1,0:T(8,128)(2,1)} %multiply_convert_fusion.2), channel_id=1, source_target_pairs={{0,2},{1,3},{2,0},{3,1},{4,6},{5,7},{6,4},{7,5},{8,10},{9,11},{10,... | collective-permute-start | bytes 1572872 | tf_op jit(solution)/shard_map/ppermute | solution.py:63
  454.3 34.8 %collective-permute-start.25 = (bf16[128,2048]{1,0:T(8,128)(2,1)}, bf16[128,2048]{1,0:T(8,128)(2,1)}, u32[]{:S(2)}, u32[]{:S(2)}) collective-permute-start(bf16[128,2048]{1,0:T(8,128)(2,1)} %multiply_convert_fusion.2), channel_id=1, source_target_pairs={{0,3},{1,0},{2,1},{3,2},{4,7},{5,4},{6,5},{7,6},{8,11},{9,8},{10,9... | collective-permute-start | bytes 1572872 | tf_op jit(solution)/shard_map/ppermute | solution.py:63
  456.6 102.9 %collective-permute-start.33 = (bf16[704,2048]{1,0:T(8,128)(2,1)}, bf16[704,2048]{1,0:T(8,128)(2,1)}, u32[]{:S(2)}, u32[]{:S(2)}) collective-permute-start(bf16[704,2048]{1,0:T(8,128)(2,1)} %get-tuple-element.104), channel_id=1, source_target_pairs={{0,16},{16,0},{1,17},{17,1},{2,18},{18,2},{3,19},{19,3},{4,20},{20... | collective-permute-start | bytes 8650760 | tf_op jit(solution)/shard_map/ppermute | solution.py:113
  458.0 101.4 %all-to-all-start.1 = ((bf16[4,512,2048]{2,1,0:T(8,128)(2,1)}), bf16[4,512,2048]{2,1,0:T(8,128)(2,1)}, u32[]{:S(2)}, u32[]{:S(2)}) async-start(bf16[4,512,2048]{2,1,0:T(8,128)(2,1)} %bitcast.170), calls=%async_computation.1 | async-start | bytes 16777216 | tf_op jit(solution)/shard_map/all_to_all | solution.py:598
  463.7 231.8 %reduce-scatter.2.cloned.1.call-start = ((), (), s32[]{:S(2)}) async-start(), calls=%async_computation.7 | async-start | bytes 10027008 | tf_op jit(solution)/shard_map/reduce_scatter | solution.py:698
  559.5 71.8 %collective-permute-start.37 = (bf16[1056,1024]{1,0:T(8,128)(2,1)}, bf16[1056,1024]{1,0:T(8,128)(2,1)S(1)}, u32[]{:S(2)}, u32[]{:S(2)}) collective-permute-start(bf16[1056,1024]{1,0:T(8,128)(2,1)} %copy-done.6), channel_id=1, source_target_pairs={{0,16},{16,0},{1,17},{17,1},{2,18},{18,2},{3,19},{19,3},{4,20},{20... | collective-permute-start | bytes 6488072 | tf_op jit(solution)/shard_map/ppermute | solution.py:113
  562.5 68.8 %collective-permute-start.32 = (bf16[128,2048]{1,0:T(8,128)(2,1)S(1)}, bf16[128,2048]{1,0:T(8,128)(2,1)S(1)}, u32[]{:S(2)}, u32[]{:S(2)}) collective-permute-start(bf16[128,2048]{1,0:T(8,128)(2,1)S(1)} %get-tuple-element.265), channel_id=1, source_target_pairs={{0,1},{1,2},{2,3},{3,0},{4,5},{5,6},{6,7},{7,4},{8,9},{9,10},{10,1... | collective-permute-start | bytes 1572872 | tf_op jit(solution)/shard_map/ppermute | solution.py:63
  563.4 67.8 %collective-permute-start.31 = (bf16[128,2048]{1,0:T(8,128)(2,1)S(1)}, bf16[128,2048]{1,0:T(8,128)(2,1)S(1)}, u32[]{:S(2)}, u32[]{:S(2)}) collective-permute-start(bf16[128,2048]{1,0:T(8,128)(2,1)S(1)} %get-tuple-element.266), channel_id=1, source_target_pairs={{0,2},{1,3},{2,0},{3,1},{4,6},{5,7},{6,4},{7,5},{8,10},{9,11},{10,... | collective-permute-start | bytes 1572872 | tf_op jit(solution)/shard_map/ppermute | solution.py:63
  564.6 67.5 %collective-permute-start.30 = (bf16[128,2048]{1,0:T(8,128)(2,1)S(1)}, bf16[128,2048]{1,0:T(8,128)(2,1)}, u32[]{:S(2)}, u32[]{:S(2)}) collective-permute-start(bf16[128,2048]{1,0:T(8,128)(2,1)S(1)} %get-tuple-element.267), channel_id=1, source_target_pairs={{0,3},{1,0},{2,1},{3,2},{4,7},{5,4},{6,5},{7,6},{8,11},{9,8},{10,9... | collective-permute-start | bytes 1572872 | tf_op jit(solution)/shard_map/ppermute | solution.py:63
  634.6 40.4 %all-to-all-start.2 = ((bf16[4,1056,256]{2,1,0:T(8,128)(2,1)}), bf16[4,1056,256]{2,1,0:T(8,128)(2,1)}, u32[]{:S(2)}, u32[]{:S(2)}) async-start(bf16[4,1056,256]{2,1,0:T(8,128)(2,1)} %bitcast.169), calls=%async_computation.3 | async-start | bytes 4325376 | tf_op jit(solution)/shard_map/all_to_all | solution.py:664
  652.3 31.0 %collective-permute-start.29 = (bf16[128,2048]{1,0:T(8,128)(2,1)}, bf16[128,2048]{1,0:T(8,128)(2,1)}, u32[]{:S(2)}, u32[]{:S(2)}) collective-permute-start(bf16[128,2048]{1,0:T(8,128)(2,1)} %get-tuple-element.226), channel_id=1, source_target_pairs={{0,1},{1,2},{2,3},{3,0},{4,5},{5,6},{6,7},{7,4},{8,9},{9,10},{10,1... | collective-permute-start | bytes 1572872 | tf_op jit(solution)/shard_map/ppermute | solution.py:63
  652.8 38.4 %collective-permute-start.28 = (bf16[128,2048]{1,0:T(8,128)(2,1)}, bf16[128,2048]{1,0:T(8,128)(2,1)}, u32[]{:S(2)}, u32[]{:S(2)}) collective-permute-start(bf16[128,2048]{1,0:T(8,128)(2,1)} %get-tuple-element.227), channel_id=1, source_target_pairs={{0,2},{1,3},{2,0},{3,1},{4,6},{5,7},{6,4},{7,5},{8,10},{9,11},{10,... | collective-permute-start | bytes 1572872 | tf_op jit(solution)/shard_map/ppermute | solution.py:63
  653.7 37.6 %collective-permute-start.27 = (bf16[128,2048]{1,0:T(8,128)(2,1)}, bf16[128,2048]{1,0:T(8,128)(2,1)}, u32[]{:S(2)}, u32[]{:S(2)}) collective-permute-start(bf16[128,2048]{1,0:T(8,128)(2,1)} %get-tuple-element.225), channel_id=1, source_target_pairs={{0,3},{1,0},{2,1},{3,2},{4,7},{5,4},{6,5},{7,6},{8,11},{9,8},{10,9... | collective-permute-start | bytes 1572872 | tf_op jit(solution)/shard_map/ppermute | solution.py:63
  697.9 16.5 %collective-permute-start.34 = (f32[11,256]{1,0:T(8,128)S(1)}, f32[11,256]{1,0:T(8,128)S(1)}, u32[]{:S(2)}, u32[]{:S(2)}) collective-permute-start(f32[11,256]{1,0:T(8,128)S(1)} %slice_bitcast_fusion.9), channel_id=1, source_target_pairs={{0,3},{1,0},{2,1},{3,2},{4,7},{5,4},{6,5},{7,6},{8,11},{9,8},{10,9... | collective-permute-start | bytes 33800 | tf_op jit(solution)/shard_map/ppermute | solution.py:63
  709.3 5.1 collective-permute-start.35
  710.3 5.7 collective-permute-start.36
  (75 other events, 744.6 us)
Sparse Core Ops, SparseCore 0:
  16.4 51.6 all-gather.3
  75.6 30.4 all-gather.5
  184.0 74.0 all-gather.7
  559.6 103.1 reduce-scatter.1

commit v3 on v2

--- a/solution.py
+++ b/solution.py
@@ -26,12 +26,6 @@
     return lax.dot_general(left, right, (((0,), (0,)), ((), ())), preferred_element_type=F32)
 
 
-def dot_exact(left, right, dims):
-    return lax.dot_general(
-        left, right, (dims, ((), ())), precision=lax.Precision.HIGHEST, preferred_element_type=F32
-    )
-
-
 def norm_parts(values):
     inverse = lax.rsqrt(jnp.mean(values * values, axis=-1, keepdims=True) + EPS)
     return (values * inverse, inverse)
@@ -84,10 +78,10 @@
     return total
 
 
-def ordered_sum(values, axis):
+def ordered_sum(values, axis, beside):
     count = lax.axis_size(axis)
     place = lax.axis_index(axis)
-    blocks = gather_blocks(values, axis)
+    blocks = after(gather_blocks(values, axis), beside)
     total = None
     for j in range(count):
         steps = (place - j) % count
@@ -244,6 +238,66 @@
         store(columns, dot_nn(grad_ref[...], first_ref[:, columns]))
 
     store(pl.ds(width, LANES), extra_scratch[...])
+
+
+def own_kernel(expert_count, *refs):
+    (first_ref, *part_refs) = refs[:-14]
+    (
+        probs_ref, mask_ref, switch_ref, keep_ref, small_ref, unit_ref, inverse_ref, normed_ref,
+        upstream_ref, state_ref, low_ref, router_ref, middle_ref, total_ref,
+    ) = refs[-14:]
+    width = unit_ref.shape[1]
+    total_ref[...] = first_ref[...]
+    for part_ref in part_refs:
+        total_ref[...] += part_ref[...].astype(F32)
+    sums = total_ref[:, width:]
+    sums = sums + pltpu.roll(sums, LANES // 2, axis=1)
+    probs, mask = probs_ref[...], mask_ref[...]
+    keep, switch = keep_ref[:, :1], switch_ref[:, :1]
+    lane = lax.broadcasted_iota(jnp.int32, sums.shape, 1)
+    prob_grad = jnp.where(lane < expert_count, keep * mask * sums, 0.0)
+    mean = jnp.sum(probs * prob_grad, axis=1, keepdims=True)
+    score = jnp.where(lane < expert_count, probs * (prob_grad - mean), 0.0)
+    score = jnp.where(lane == expert_count, keep * sums * switch * (1.0 - switch), score)
+    high = score.astype(BF16)
+    low = (score - high.astype(F32)).astype(BF16)
+    small = small_ref[...]
+    normed_total = total_ref[:, :width] + dot_nn(high, small) + dot_nn(low, small)
+    normed = normed_ref[...]
+    router_ref[...] = dot_tn(high, normed) + dot_tn(low, normed)
+    unit = unit_ref[...]
+    middle_ref[...] = jnp.sum(normed_total * unit, axis=0, keepdims=True)
+    gain = small[expert_count + 2 : expert_count + 3, :].astype(F32)
+    state = upstream_ref[...].astype(F32) + norm_back(normed_total, gain, unit, inverse_ref[:, :1])
+    state_ref[...] = state
+    low_ref[...] = (keep * state).astype(BF16)
+
+
+def run_own(expert_count, blocks, scores, small, unit, inverse, normed, upstream):
+    rows, width = unit.shape
+    wide = lambda column: jnp.broadcast_to(column, (rows, LANES))
+    probs, mask, switch, keep = scores
+    pad = lambda values: jnp.pad(values, ((0, 0), (0, LANES - values.shape[1])))
+    operands = [
+        *blocks, pad(probs), pad(mask), wide(switch), wide(keep), small, unit, wide(inverse), normed, upstream,
+    ]
+    return pl.pallas_call(
+        lambda *refs: own_kernel(expert_count, *refs),
+        in_specs=[pl.BlockSpec(memory_space=pltpu.VMEM)] * len(operands),
+        out_specs=[pl.BlockSpec(memory_space=pltpu.VMEM)] * 4,
+        out_shape=[
+            jax.ShapeDtypeStruct((rows, width), F32),
+            jax.ShapeDtypeStruct((rows, width), BF16),
+            jax.ShapeDtypeStruct((LANES, width), F32),
+            jax.ShapeDtypeStruct((1, width), F32),
+        ],
+        scratch_shapes=[pltpu.VMEM((rows, width + LANES), F32)],
+        compiler_params=pltpu.CompilerParams(vmem_limit_bytes=24 << 20),
+        cost_estimate=pl.CostEstimate(
+            flops=60 * 8 * rows * width * LANES, bytes_accessed=24 * rows * width, transcendentals=0
+        ),
+        name="own_rows",
+    )(*operands)
 
 
 def run_experts(
@@ -451,14 +505,12 @@
     attn_probs = jnp.exp(scores - log_total).astype(BF16)
     context = jnp.einsum("hqk,khd->qhd", attn_probs, value_heads, preferred_element_type=F32)
     context_low = context.astype(BF16).reshape(group_rows, head_cols)
-    context_low = after(context_low, shared_span)
     head_blocks = split_rows(dot_nn(context_low, out_weight).astype(BF16), tp_count)
     attention_parts = send_blocks(head_blocks, "tp")
 
     shared_span = after(shared_span, head_blocks)
     if dp_count == 2:
         shared_other = swapped(shared_span, "dp", 1)
-        attention_parts = after(attention_parts, shared_other)
         shared_parts = in_order(shared_span, shared_other, lax.axis_index("dp"), 1)
     else:
         shared_parts = lax.all_gather(shared_span, "dp", axis=0, tiled=True)
@@ -483,6 +535,8 @@
     near = swapped(group_upstream, "ep", 2)
 
     attention_parts = after(attention_parts, near)
+    if dp_count == 2:
+        attention_parts = after(attention_parts, shared_other)
     attention_own = add_up([head_blocks[0], *attention_parts])
     hidden_state = input_values[:own_rows] + own_keep * attention_own
     middle_unit, middle_inverse = norm_parts(hidden_state)
@@ -517,7 +571,8 @@
 
     first_weight, down_weight = after((first_weight, down_weight), middle_normed)
     span_mask = after(span_mask, expert_probs, switch_value, route_mask)
-    shared_operands = (span_normed, upstream, span_mask, picks, small_full.T, first_weight, down_weight)
+    small_rows_low = small_full.T
+    shared_operands = (span_normed, upstream, span_mask, picks, small_rows_low, first_weight, down_weight)
     sibling_back, chip_back, *made = run_experts(
         (ep_index ^ 3, ep_index ^ 2), tp_index, tp_count, expert_count, *shared_operands, ()
     )
@@ -601,36 +656,27 @@
     back_parts = after(back_parts, branch, shared_kept, shared_given)
     if dp_count == 2:
         back_parts = after(back_parts, last_other)
-    back_own = add_up([back_blocks[0], *back_parts])
-
-    normed_own = back_own[:, :width]
-    gate_sums = back_own[:, width : width + half] + back_own[:, width + half :]
-    prob_grad = own_keep * route_mask * gate_sums[:, :expert_count]
-    logit_grad = expert_probs * (
-        prob_grad - jnp.sum(expert_probs * prob_grad, axis=-1, keepdims=True)
-    )
-    switch_grad = (
-        own_keep
-        * gate_sums[:, expert_count : expert_count + 1]
-        * switch_value
-        * (1.0 - switch_value)
-    )
-    score_grad = jnp.concatenate([logit_grad, switch_grad], axis=1)
-    normed_total = normed_own + dot_exact(score_grad, small_rows[: expert_count + 1], ((1,), (0,)))
-    router_part = dot_exact(score_grad, middle_normed.astype(F32), ((0,), (0,)))
-    middle_part = jnp.sum(normed_total * middle_unit, axis=0, keepdims=True)
-    state_grad = cotangent.astype(F32) + norm_back(
-        normed_total, middle_full, middle_unit, middle_inverse
-    )
-    attention_grad_own = (own_keep * state_grad).astype(BF16)
+
+    state_grad, attention_grad_own, router_part, middle_part = run_own(
+        expert_count,
+        [back_blocks[0], *back_parts],
+        (expert_probs, route_mask, switch_value, own_keep),
+        small_rows_low,
+        middle_unit,
+        middle_inverse,
+        middle_normed,
+        cotangent,
+    )
+    router_part = router_part[: expert_count + 1]
     attention_grad_blocks = gather_blocks(attention_grad_own, "tp")
 
     if dp_count == 2:
         attention_grad_blocks = after(attention_grad_blocks, first_other[0])
     attention_grad = jnp.concatenate(attention_grad_blocks, axis=0)
-    shared_other = swapped_or_none(shared_given, "dp")
-
-    mixing_grad = dot_tn(attention_grad, context_low).astype(BF16)
+    grads_other = swapped_or_none(shared_given, "dp")
+
+    mixing_grad = dot_tn(context_low, attention_grad).astype(BF16)
+    mixing_sum = lax.psum_scatter(mixing_grad, ("dp", "ep"), scatter_dimension=1, tiled=True)
     context_grad = dot_nt(attention_grad, out_weight)
     context_grad = context_grad.astype(BF16).reshape(group_rows, head_count, HD)
     probs_again = jnp.exp(score_matrix() - log_total)
@@ -648,28 +694,46 @@
     )
     query_grad = (query_rot_grad * cosine + unrotate(query_rot_grad * sine)).astype(BF16)
     key_grad = (key_rot_grad * cosine + unrotate(key_rot_grad * sine)).astype(BF16)
+    query_grad = after(query_grad, mixing_grad)
     in_grad = jnp.concatenate(
         [query_grad.reshape(group_rows, head_cols), key_grad.reshape(group_rows, head_cols), value_grad],
         axis=1,
     )
+    in_grad = after(in_grad, branch_terms)
     bias_grad = jnp.sum(in_grad.astype(F32), axis=0)
     entry_part = dot_nt(in_grad, in_weight)
     entry_blocks = split_rows(entry_part.astype(BF16), tp_count)
     entry_parts = send_blocks(entry_blocks, "tp")
     if dp_count == 2:
-        shared_mine = add_up([shared_kept, after(shared_other, entry_parts)]).astype(BF16)
+        shared_mine = add_up([shared_kept, grads_other]).astype(BF16)
     else:
         shared_mine = lax.psum_scatter(shared_kept, "dp", scatter_dimension=1, tiled=True)
     shared_mine = shared_mine.reshape(3 * shared_hidden, ep_count, slice_rows).transpose(1, 0, 2)
     shared_back = lax.all_to_all(shared_mine, "ep", split_axis=0, concat_axis=0, tiled=True)
     shared_back = shared_back.reshape(ep_count, 3, shared_hidden, slice_rows).astype(F32)
+    branch_blocks = []
+    for j in range(tp_count):
+        start = ((tp_index - j) % tp_count) * own_rows
+        rows = lax.dynamic_slice_in_dim(branch_terms, start, own_rows, 1)
+        branch_blocks.append(jnp.sum(rows.astype(F32), axis=0))
+    branch_blocks = [branch_blocks[0]] + [block.astype(BF16) for block in branch_blocks[1:]]
+    branch_parts = send_blocks(branch_blocks, "tp")
+    last_sum = whole_sum(last_own, last_other, "dp").reshape(local_experts, hidden, width)
+    first_sum = [whole_sum(first_own[0], first_other[0], "dp")]
+    entry_parts = after(entry_parts, branch_parts, shared_mine, last_sum, first_sum)
+    if dp_count == 2:
+        first_other[1] = after(first_other[1], entry_parts)
+    first_sum.append(whole_sum(first_own[1], first_other[1], "dp"))
+    first_sum = [part.reshape(local_experts, hidden, width) for part in first_sum]
     entry_own = add_up([entry_blocks[0], *entry_parts])
     input_gradient = state_grad + norm_back(
         entry_own, entry_full, entry_unit[:own_rows], entry_inverse[:own_rows]
     )
 
     entry_gain_part = jnp.sum(entry_part * entry_unit, axis=0, keepdims=True)
-    small_part = jnp.concatenate([router_part, middle_part, entry_gain_part], axis=0)
+    small_part = ordered_sum(
+        jnp.concatenate([router_part, middle_part, entry_gain_part], axis=0), "tp", branch_blocks
+    )
     bias_part = bias_grad.reshape(3, head_count, part_count, -1).transpose(2, 0, 1, 3)
     bias_part = bias_part.reshape(part_count, bias_rows)
     bias_part = jnp.pad(bias_part, ((0, 0), (0, bias_depth * slice_rows - bias_rows)))
@@ -688,38 +752,20 @@
     dense_grad = jnp.concatenate(
         [
             dot_tn(entry_normed, in_grad).astype(BF16),
-            mixing_grad,
             small_cols,
         ],
         axis=1,
     )
     if dp_count == 2:
-        dense_grad = after(dense_grad, first_other[1], branch_terms)
+        dense_grad = after(dense_grad, grads_other)
     dense_sum = lax.psum_scatter(
         dense_grad, ("dp", "ep"), scatter_dimension=0, tiled=True
     ).astype(F32)
-    small_sum = dense_sum[:, 4 * head_cols : 4 * head_cols + half] + dense_sum[:, 4 * head_cols + half :]
-    tp_sum = ordered_sum(small_sum[:, : expert_count + 3].T, "tp")
+    small_sum = dense_sum[:, 3 * head_cols : 3 * head_cols + half] + dense_sum[:, 3 * head_cols + half :]
     bias_sum = small_sum[:, expert_count + 3 : expert_count + 3 + bias_depth]
     bias_sum = bias_sum.T.reshape(-1)[:bias_rows].reshape(heads_bias.shape)
 
-    branch_terms = after(branch_terms, entry_blocks)
-    branch_blocks = []
-    for j in range(tp_count):
-        start = ((tp_index - j) % tp_count) * own_rows
-        rows = lax.dynamic_slice_in_dim(branch_terms, start, own_rows, 1)
-        branch_blocks.append(jnp.sum(rows.astype(F32), axis=0))
-    branch_blocks = [branch_blocks[0]] + [block.astype(BF16) for block in branch_blocks[1:]]
-    branch_parts = send_blocks(branch_blocks, "tp")
     layer_output = (hidden_state + add_up([branch_blocks[0], *branch_parts])).astype(BF16)
-    if dp_count == 2:
-        first_other = after(first_other, entry_parts, tp_sum)
-    first_sum = [
-        whole_sum(own, other, "dp").reshape(local_experts, hidden, width)
-        for own, other in zip(first_own, first_other)
-    ]
-    last_sum = whole_sum(last_own, last_other, "dp").reshape(local_experts, hidden, width)
-
     def by_columns(rows):
         return rows.transpose(2, 0, 1).reshape(slice_rows, ep_count * shared_hidden)
 
@@ -729,12 +775,12 @@
         dense_sum[:, :head_cols],
         dense_sum[:, head_cols : 2 * head_cols],
         dense_sum[:, 2 * head_cols : 3 * head_cols],
-        dense_sum[:, 3 * head_cols : 4 * head_cols].T,
+        mixing_sum.astype(F32),
         bias_sum,
-        tp_sum[expert_count + 2],
-        tp_sum[expert_count + 1],
-        tp_sum[:expert_count].T,
-        tp_sum[expert_count],
+        small_sum[:, expert_count + 2],
+        small_sum[:, expert_count + 1],
+        small_sum[:, :expert_count],
+        small_sum[:, expert_count],
         by_columns(shared_back[:, 0]),
         by_columns(shared_back[:, 1]),
         shared_back[:, 2].reshape(ep_count * shared_hidden, slice_rows),

time: 748 us -> 709 us (0.948)
  waiting for transfers between devices: 288 us -> 220 us
  starting transfers between devices: 69.9 us -> 90 us
  Pallas kernels: 93.5 us -> 105 us
    ppermute x14, waiting for transfers between devices: 102 us -> 25.4 us  [swapped(): return lax.ppermute(values, axis, [(i, i ^ bit) for i in range(count)])]
    ppermute x24, waiting for transfers between devices: 110 us -> 141 us  [shifted(): lax.ppermute(block, axis, [(i, (i + step) % count) for i in range(count)])]
    ppermute x24, starting transfers between devices: 45.1 us -> 65.3 us  [shifted(): lax.ppermute(block, axis, [(i, (i + step) % count) for i in range(count)])]
    all_to_all x1, waiting for transfers between devices: 17.9 us -> 0.01 us  [body(): lax.all_to_all(shared_mine, 'ep', split_axis=0, concat_axis=0, tiled=True)]
    all_to_all x1, waiting for transfers between devices: 24.1 us -> 11.2 us  [body(): lax.all_to_all(shared_own, 'ep', split_axis=0, concat_axis=0, tiled=True)]
    all_gather x1, waiting for transfers between devices: 0.01 us -> 8.51 us  [body(): lax.all_gather(after(mixing_weight, dense_full), ('dp', 'ep'), axis=1, ti...]
    pallas_call x2, Pallas kernels: 85.9 us -> 93.6 us  [run_experts(): pl.pallas_call(lambda *refs: expert_kernel(tp_count, expert_count, *refs)...]
    unnamed x181 -> x154, local copies, waits for them, and re-layouts: 39.9 us -> 43.6 us
  transfers between devices with their start and end apart: 45 -> 46, of which waited for: 16 -> 16; matrix products, arithmetic and copies ran while one was open for 30% -> 32% of each run, Pallas kernels for 7% -> 9%
where the time goes in v3:
time: 709 us; the launch traced here: 697 us
  waiting for transfers between devices  220 us (31%)
  Pallas kernels  105 us (15%)
  matrix products  94.2 us (13%)
  starting transfers between devices  90 us (13%)
  other arithmetic  87.6 us (12%)
  local copies, waits for them, and re-layouts  84.3 us (12%)
  between operations  15.3 us (2%)
    ppermute x24, waiting for transfers between devices, shifted(): lax.ppermute(block, axis, [(i, (i + step) % count) for i in range(count)])  141 us
    pallas_call x2, Pallas kernels, run_experts(): pl.pallas_call(lambda *refs: expert_kernel(tp_count, expert_count, *refs)...  93.6 us
    ppermute x24, starting transfers between devices, shifted(): lax.ppermute(block, axis, [(i, (i + step) % count) for i in range(count)])  65.3 us
    dot_general x4, matrix products, dot_tn(): lax.dot_general(left, right, (((0,), (0,)), ((), ())), preferred_element_...  46.7 us
    unnamed x154, local copies, waits for them, and re-layouts  43.6 us
    all_gather x1, waiting for transfers between devices, body(): lax.all_gather(middle_normed, ('ep', 'tp'), axis=0, tiled=True)  30.8 us
    ppermute x14, waiting for transfers between devices, swapped(): return lax.ppermute(values, axis, [(i, i ^ bit) for i in range(count)])  25.4 us
    dot_general x4, matrix products, dot_nn(): lax.dot_general(left, right, (((1,), (0,)), ((), ())), preferred_element_...  23.1 us
  transfers between devices with their start and end apart: 46, of which 16 were waited for; matrix products, arithmetic and copies ran while one was open for 32% of the time, Pallas kernels for 9%

profile of v3, /device:TPU:0, one launch (start us, length us, event | category | flops | bytes accessed | tf_op | source)
XLA Modules:
  0.0 696.7 jit_solution(6918693970494400197)
XLA Ops:
  16.3 3.1 collective-permute-start
  29.5 5.2 collective-permute-done
  34.7 21.6 %collective-permute-done.1 = bf16[128,2048]{1,0:T(8,128)(2,1)} collective-permute-done((bf16[128,2048]{1,0:T(8,128)(2,1)}, bf16[128,2048]{1,0:T(8,128)(2,1)}, u32[]{:S(2)}, u32[]{:S(2)}) %collective-permute-start.1) | collective-permute-done | bytes 524320 | tf_op jit(solution)/shard_map/ppermute | solution.py:57
  56.3 11.7 %collective-permute-start.6 = (bf16[128,2048]{1,0:T(8,128)(2,1)S(1)}, bf16[128,2048]{1,0:T(8,128)(2,1)}, u32[]{:S(2)}, u32[]{:S(2)}) collective-permute-start(bf16[128,2048]{1,0:T(8,128)(2,1)S(1)} %copy-done.12), channel_id=1, source_target_pairs={{0,1},{1,2},{2,3},{3,0},{4,5},{5,6},{6,7},{7,4},{8,9},{9,10},{10,1... | collective-permute-start | bytes 1572872 | tf_op jit(solution)/shard_map/ppermute | solution.py:57
  74.6 5.9 fusion.10
  86.0 4.5 all-to-all-start
  95.2 3.3 convolution_convert_fusion.8
  98.5 8.5 %all-gather.6.cloned.1.call-done = bf16[512,2048]{1,0:T(8,128)(2,1)} async-done(((bf16[512,256]{1,0:T(8,128)(2,1)}), bf16[512,2048]{1,0:T(8,128)(2,1)}) %all-gather.6.cloned.1.call-update) | async-done | bytes 2097168 | tf_op jit(solution)/shard_map/all_gather | solution.py:443
  111.4 11.2 %all-to-all-done = bf16[4,1056,256]{2,1,0:T(8,128)(2,1)} async-done(((bf16[4,1056,256]{2,1,0:T(8,128)(2,1)}), bf16[4,1056,256]{2,1,0:T(8,128)(2,1)}, u32[]{:S(2)}, u32[]{:S(2)}) %all-to-all-start) | async-done | bytes 2162720 | tf_op jit(solution)/shard_map/all_to_all | solution.py:480
  135.2 7.8 %collective-permute-done.3 = bf16[128,2048]{1,0:T(8,128)(2,1)S(1)} collective-permute-done((bf16[128,2048]{1,0:T(8,128)(2,1)}, bf16[128,2048]{1,0:T(8,128)(2,1)S(1)}, u32[]{:S(2)}, u32[]{:S(2)}) %collective-permute-start.3) | collective-permute-done | bytes 524320 | tf_op jit(solution)/shard_map/ppermute | solution.py:57
  143.0 33.0 %collective-permute-done.4 = bf16[128,2048]{1,0:T(8,128)(2,1)S(1)} collective-permute-done((bf16[128,2048]{1,0:T(8,128)(2,1)}, bf16[128,2048]{1,0:T(8,128)(2,1)S(1)}, u32[]{:S(2)}, u32[]{:S(2)}) %collective-permute-start.4) | collective-permute-done | bytes 524320 | tf_op jit(solution)/shard_map/ppermute | solution.py:57
  195.4 4.0 fusion.27.refs_3_
  215.8 3.3 order_rows.1.refs_2_
  219.1 3.3 copy-done.3
  222.4 30.8 %all-gather.8.cloned.1.call-done.refs_1_ = bf16[2048,2048]{1,0:T(8,128)(2,1)} async-done(((bf16[128,2048]{1,0:T(8,128)(2,1)}), bf16[2048,2048]{1,0:T(8,128)(2,1)}) %all-gather.8.cloned.1.call-update) | async-done | bytes 8388624 | tf_op jit(solution)/shard_map/all_gather | solution.py:545
  253.2 42.4 %experts.2 = (bf16[512,2176]{1,0:T(8,128)(2,1)}, bf16[512,2176]{1,0:T(8,128)(2,1)}, bf16[2048,2304]{1,0:T(8,128)(2,1)}, bf16[2048,1152]{1,0:T(8,128)(2,1)}) custom-call(s32[3]{0:T(128)} %add_add_fusion.1.refs_0_, bf16[2048,2048]{1,0:T(8,128)(2,1)} %all-gather.8.cloned.1.call-done.refs_1_, bf16[2048,2048]{1,0:T(8,128)(2,1)} %copy-done.3, ...), custom_call_target="tpu_custom_call" | custom-call | flops 24159191040 | bytes 33816576 | tf_op jit(solution)/shard_map/experts/pallas_call | solution.py:327
  295.9 4.3 collective-permute-done.13
  300.2 3.5 add_convert_fusion
  304.8 51.2 %experts.3 = (bf16[512,2176]{1,0:T(8,128)(2,1)}, bf16[512,2176]{1,0:T(8,128)(2,1)}, bf16[2048,2304]{1,0:T(8,128)(2,1)}, bf16[2048,1152]{1,0:T(8,128)(2,1)}) custom-call(s32[3]{0:T(128)} %add_add_fusion.2.refs_0_, bf16[2048,2048]{1,0:T(8,128)(2,1)} %all-gather.8.cloned.1.call-done.refs_1_, ...), custom_call_target="tpu_custom_call", output_to_operand_aliasing={{2}: (8, {}), {3}: (9, {})} | custom-call | flops 24159191040 | bytes 33816576 | tf_op jit(solution)/shard_map/experts/pallas_call | solution.py:327
  359.0 14.0 %convolution_convert_fusion.3.refs_0_.refs_1_ = bf16[1152,2048]{1,0:T(8,128)(2,1)S(1)} fusion(bf16[2048,1152]{1,0:T(8,128)(2,1)} %get-tuple-element.113, bf16[2048,2048]{1,0:T(8,128)(2,1)} %copy-done.3), kind=kOutput, calls=%fused_computation.12 | convolution fusion | flops 9666035712 | bytes 17825792 | tf_op jit(solution)/shard_map/dot_general | solution.py:26
  381.7 24.6 %convolution_convert_fusion.refs_0_ = bf16[2304,2048]{1,0:T(8,128)(2,1)} fusion(bf16[2048,2304]{1,0:T(8,128)(2,1)} %get-tuple-element.110, bf16[2048,2048]{1,0:T(8,128)(2,1)S(1)} %bitcast.202), kind=kOutput, calls=%fused_computation.3 | convolution fusion | flops 19332071424 | bytes 27262976 | tf_op jit(solution)/shard_map/dot_general | solution.py:26
  406.3 3.7 copy-done.2
  410.0 3.9 first_rows.1
  414.6 12.9 %convolution_convert_fusion.2 = bf16[2048,2048]{1,0:T(8,128)(2,1)} fusion(bf16[2048,1152]{1,0:T(8,128)(2,1)S(1)} %bitcast.206, bf16[1152,2048]{1,0:T(8,128)(2,1)S(1)} %bitcast.175), kind=kOutput, calls=%fused_computation.11 | convolution fusion | flops 9667870720 | bytes 17825792 | tf_op jit(solution)/shard_map/dot_general | solution.py:18
  427.5 5.6 all-to-all-start.1
  433.2 6.4 collective-permute-done.25
  444.4 3.4 own_rows.1
  456.6 10.1 %collective-permute-done.26 = bf16[128,2048]{1,0:T(8,128)(2,1)S(1)} collective-permute-done((bf16[128,2048]{1,0:T(8,128)(2,1)}, bf16[128,2048]{1,0:T(8,128)(2,1)S(1)}, u32[]{:S(2)}, u32[]{:S(2)}) %collective-permute-start.26) | collective-permute-done | bytes 524320 | tf_op jit(solution)/shard_map/ppermute | solution.py:57
  466.7 20.0 %collective-permute-done.27 = bf16[128,2048]{1,0:T(8,128)(2,1)} collective-permute-done((bf16[128,2048]{1,0:T(8,128)(2,1)}, bf16[128,2048]{1,0:T(8,128)(2,1)}, u32[]{:S(2)}, u32[]{:S(2)}) %collective-permute-start.27) | collective-permute-done | bytes 524320 | tf_op jit(solution)/shard_map/ppermute | solution.py:57
  486.7 14.7 %collective-permute-done.29 = bf16[704,2048]{1,0:T(8,128)(2,1)} collective-permute-done((bf16[704,2048]{1,0:T(8,128)(2,1)}, bf16[704,2048]{1,0:T(8,128)(2,1)}, u32[]{:S(2)}, u32[]{:S(2)}) %collective-permute-start.29) | collective-permute-done | bytes 2883616 | tf_op jit(solution)/shard_map/ppermute | solution.py:107
  509.1 3.7 convolution_convert_fusion.6
  522.8 3.5 all-to-all-done.1
  526.3 10.8 %multiply_reduce_fusion = (f32[2048]{0:T(1024)S(1)}, bf16[512,2048]{1,0:T(8,128)(2,1)}, f32[512,2048]{1,0:T(8,128)}) fusion(f32[512]{0:T(512)S(1)} %copy-done.52, bf16[512,2048]{1,0:T(8,128)(2,1)} %copy-done.19, bf16[512,1536]{0,1:T(8,128)(2,1)} %pad_maximum_fusion.4, bf16[2048,1664]{0,1:T(8,128)(2,1)} %all-gather.4.cloned.1.call-done), kind=kOutput, calls=%fused_computation.27 | convolution fusion | flops 3226466304 | bytes 16263168 | tf_op jit(solution)/shard_map/dot_general | solution.py:22
  541.3 5.6 convolution_convert_fusion.1
  547.4 5.8 dynamic-slice_reduce_fusion.2
  553.2 3.1 convert_reduce_fusion
  556.5 6.8 pad_maximum_fusion
  564.8 3.3 add_convert_fusion.1
  569.6 4.6 all-to-all-start.2
  579.1 5.6 convert_add_fusion.2
  587.7 4.2 collective-permute-done.30
  592.4 22.0 %collective-permute-done.31 = bf16[128,2048]{1,0:T(8,128)(2,1)} collective-permute-done((bf16[128,2048]{1,0:T(8,128)(2,1)S(1)}, bf16[128,2048]{1,0:T(8,128)(2,1)}, u32[]{:S(2)}, u32[]{:S(2)}) %collective-permute-start.31) | collective-permute-done | bytes 524320 | tf_op jit(solution)/shard_map/ppermute | solution.py:57
  614.4 22.6 %collective-permute-start.32 = (bf16[128,2048]{1,0:T(8,128)(2,1)}, bf16[128,2048]{1,0:T(8,128)(2,1)S(1)}, u32[]{:S(2)}, u32[]{:S(2)}) collective-permute-start(bf16[128,2048]{1,0:T(8,128)(2,1)} %get-tuple-element.247), channel_id=1, source_target_pairs={{0,1},{1,2},{2,3},{3,0},{4,5},{5,6},{6,7},{7,4},{8,9},{9,10},{10,1... | collective-permute-start | bytes 1572872 | tf_op jit(solution)/shard_map/ppermute | solution.py:57
  637.0 6.4 convert_add_fusion.1
  643.4 3.6 fusion.70
  653.3 16.8 %collective-permute-done.20 = bf16[128,2048]{1,0:T(8,128)(2,1)} collective-permute-done((bf16[128,2048]{1,0:T(8,128)(2,1)}, bf16[128,2048]{1,0:T(8,128)(2,1)}, u32[]{:S(2)}, u32[]{:S(2)}) %collective-permute-start.20) | collective-permute-done | bytes 524320 | tf_op jit(solution)/shard_map/ppermute | solution.py:57
  675.0 3.1 multiply_add_fusion
  678.1 5.4 convert_add_fusion
  (355 shorter events, 167.0 us)
Async XLA Ops:
  7.2 123.9 %copy-start = (s32[8]{0:T(128)S(1)}, s32[8]{0:T(128)}, u32[]{:S(2)}) copy-start(s32[8]{0:T(128)} %param.23) | copy-start | bytes 100
  7.2 65.4 %all-gather.4.cloned.1.call-start = ((), (), s32[]{:S(2)}) async-start(), calls=%async_computation.5 | async-start | bytes 7667712 | tf_op jit(solution)/shard_map/all_gather | solution.py:440
  16.3 90.7 %all-gather.6.cloned.1.call-start = ((), (), s32[]{:S(2)}) async-start(), calls=%async_computation.6 | async-start | bytes 2359296 | tf_op jit(solution)/shard_map/all_gather | solution.py:443
  16.3 18.3 %collective-permute-start = (bf16[128,2048]{1,0:T(8,128)(2,1)}, bf16[128,2048]{1,0:T(8,128)(2,1)}, u32[]{:S(2)}, u32[]{:S(2)}) collective-permute-start(bf16[128,2048]{1,0:T(8,128)(2,1)} %param.21), channel_id=1, source_target_pairs={{0,1},{1,2},{2,3},{3,0},{4,5},{5,6},{6,7},{7,4},{8,9},{9,10},{10,1... | collective-permute-start | bytes 1572872 | tf_op jit(solution)/shard_map/ppermute | solution.py:57
  19.4 36.9 %collective-permute-start.1 = (bf16[128,2048]{1,0:T(8,128)(2,1)}, bf16[128,2048]{1,0:T(8,128)(2,1)}, u32[]{:S(2)}, u32[]{:S(2)}) collective-permute-start(bf16[128,2048]{1,0:T(8,128)(2,1)} %param.21), channel_id=1, source_target_pairs={{0,2},{1,3},{2,0},{3,1},{4,6},{5,7},{6,4},{7,5},{8,10},{9,11},{10,... | collective-permute-start | bytes 1572872 | tf_op jit(solution)/shard_map/ppermute | solution.py:57
  22.0 34.3 %collective-permute-start.2 = (bf16[128,2048]{1,0:T(8,128)(2,1)}, bf16[128,2048]{1,0:T(8,128)(2,1)}, u32[]{:S(2)}, u32[]{:S(2)}) collective-permute-start(bf16[128,2048]{1,0:T(8,128)(2,1)} %param.21), channel_id=1, source_target_pairs={{0,3},{1,0},{2,1},{3,2},{4,7},{5,4},{6,5},{7,6},{8,11},{9,8},{10,9... | collective-permute-start | bytes 1572872 | tf_op jit(solution)/shard_map/ppermute | solution.py:57
  26.2 67.9 %copy-start.24 = (pred[512,512]{0,1:T(8,128)(4,1)}, pred[512,512]{0,1:T(8,128)(4,1)S(1)}, u32[]{:S(2)}) copy-start(pred[512,512]{0,1:T(8,128)(4,1)S(1)} %broadcast_compare_fusion) | copy-start | bytes 786436
  56.3 67.8 %collective-permute-start.6 = (bf16[128,2048]{1,0:T(8,128)(2,1)S(1)}, bf16[128,2048]{1,0:T(8,128)(2,1)}, u32[]{:S(2)}, u32[]{:S(2)}) collective-permute-start(bf16[128,2048]{1,0:T(8,128)(2,1)S(1)} %copy-done.12), channel_id=1, source_target_pairs={{0,1},{1,2},{2,3},{3,0},{4,5},{5,6},{6,7},{7,4},{8,9},{9,10},{10,1... | collective-permute-start | bytes 1572872 | tf_op jit(solution)/shard_map/ppermute | solution.py:57
  68.0 56.1 %collective-permute-start.7 = (bf16[128,2048]{1,0:T(8,128)(2,1)S(1)}, bf16[128,2048]{1,0:T(8,128)(2,1)}, u32[]{:S(2)}, u32[]{:S(2)}) collective-permute-start(bf16[128,2048]{1,0:T(8,128)(2,1)S(1)} %copy-done.12), channel_id=1, source_target_pairs={{0,2},{1,3},{2,0},{3,1},{4,6},{5,7},{6,4},{7,5},{8,10},{9,11},{10,... | collective-permute-start | bytes 1572872 | tf_op jit(solution)/shard_map/ppermute | solution.py:57
  69.6 54.5 %collective-permute-start.8 = (bf16[128,2048]{1,0:T(8,128)(2,1)S(1)}, bf16[128,2048]{1,0:T(8,128)(2,1)}, u32[]{:S(2)}, u32[]{:S(2)}) collective-permute-start(bf16[128,2048]{1,0:T(8,128)(2,1)S(1)} %copy-done.12), channel_id=1, source_target_pairs={{0,3},{1,0},{2,1},{3,2},{4,7},{5,4},{6,5},{7,6},{8,11},{9,8},{10,9... | collective-permute-start | bytes 1572872 | tf_op jit(solution)/shard_map/ppermute | solution.py:57
  86.0 36.6 %all-to-all-start = ((bf16[4,1056,256]{2,1,0:T(8,128)(2,1)}), bf16[4,1056,256]{2,1,0:T(8,128)(2,1)}, u32[]{:S(2)}, u32[]{:S(2)}) async-start(bf16[4,1056,256]{2,1,0:T(8,128)(2,1)} %pad_maximum_fusion.2), calls=%async_computation | async-start | bytes 4325376 | tf_op jit(solution)/shard_map/all_to_all | solution.py:480
  90.5 162.7 %all-gather.8.cloned.1.call-start = ((), (), s32[]{:S(2)}) async-start(), calls=%async_computation.7 | async-start | bytes 8912896 | tf_op jit(solution)/shard_map/all_gather | solution.py:545
  122.6 53.3 %collective-permute-start.10 = (bf16[4,1056,256]{2,1,0:T(8,128)(2,1)}, bf16[4,1056,256]{2,1,0:T(8,128)(2,1)}, u32[]{:S(2)}, u32[]{:S(2)}) collective-permute-start(bf16[4,1056,256]{2,1,0:T(8,128)(2,1)} %all-to-all-done), channel_id=1, source_target_pairs={{0,16},{16,0},{1,17},{17,1},{2,18},{18,2},{3,19},{19,3},{4,20},{20... | collective-permute-start | bytes 6488072 | tf_op jit(solution)/shard_map/ppermute | solution.py:107
  127.5 48.5 %collective-permute-start.9 = (bf16[512,2048]{1,0:T(8,128)(2,1)S(1)}, bf16[512,2048]{1,0:T(8,128)(2,1)}, u32[]{:S(2)}, u32[]{:S(2)}) collective-permute-start(bf16[512,2048]{1,0:T(8,128)(2,1)S(1)} %constant_dynamic-update-slice_fusion.refs_0_), channel_id=1, source_target_pairs={{0,8},{4,12},{8,0},{12,4},{1,9},{5,13},{9,1},{13,5},{2,10},{6,14},... | collective-permute-start | bytes 6291464 | tf_op jit(solution)/shard_map/ppermute | solution.py:107
  127.9 15.1 %collective-permute-start.3 = (bf16[128,2048]{1,0:T(8,128)(2,1)}, bf16[128,2048]{1,0:T(8,128)(2,1)S(1)}, u32[]{:S(2)}, u32[]{:S(2)}) collective-permute-start(bf16[128,2048]{1,0:T(8,128)(2,1)} %get-tuple-element.253), channel_id=1, source_target_pairs={{0,3},{1,0},{2,1},{3,2},{4,7},{5,4},{6,5},{7,6},{8,11},{9,8},{10,9... | collective-permute-start | bytes 1572872 | tf_op jit(solution)/shard_map/ppermute | solution.py:57
  130.2 45.7 %collective-permute-start.4 = (bf16[128,2048]{1,0:T(8,128)(2,1)}, bf16[128,2048]{1,0:T(8,128)(2,1)S(1)}, u32[]{:S(2)}, u32[]{:S(2)}) collective-permute-start(bf16[128,2048]{1,0:T(8,128)(2,1)} %get-tuple-element.252), channel_id=1, source_target_pairs={{0,2},{1,3},{2,0},{3,1},{4,6},{5,7},{6,4},{7,5},{8,10},{9,11},{10,... | collective-permute-start | bytes 1572872 | tf_op jit(solution)/shard_map/ppermute | solution.py:57
  130.9 45.1 %collective-permute-start.5 = (bf16[128,2048]{1,0:T(8,128)(2,1)}, bf16[128,2048]{1,0:T(8,128)(2,1)}, u32[]{:S(2)}, u32[]{:S(2)}) collective-permute-start(bf16[128,2048]{1,0:T(8,128)(2,1)} %get-tuple-element.251), channel_id=1, source_target_pairs={{0,1},{1,2},{2,3},{3,0},{4,5},{5,6},{6,7},{7,4},{8,9},{9,10},{10,1... | collective-permute-start | bytes 1572872 | tf_op jit(solution)/shard_map/ppermute | solution.py:57
  201.2 14.5 %collective-permute-start.11 = (bf16[512,2048]{1,0:T(8,128)(2,1)S(1)}, bf16[512,2048]{1,0:T(8,128)(2,1)}, u32[]{:S(2)}, u32[]{:S(2)}) collective-permute-start(bf16[512,2048]{1,0:T(8,128)(2,1)S(1)} %constant_dynamic-update-slice_fusion.refs_0_), channel_id=1, source_target_pairs={{0,4},{4,0},{8,12},{12,8},{1,5},{5,1},{9,13},{13,9},{2,6},{6,2},{1... | collective-permute-start | bytes 6291464 | tf_op jit(solution)/shard_map/ppermute | solution.py:107
  201.2 14.5 %collective-permute-start.12 = (bf16[512,2048]{1,0:T(8,128)(2,1)}, bf16[512,2048]{1,0:T(8,128)(2,1)}, u32[]{:S(2)}, u32[]{:S(2)}) collective-permute-start(bf16[512,2048]{1,0:T(8,128)(2,1)} %collective-permute-done.9.refs_2_), channel_id=1, source_target_pairs={{0,4},{4,0},{8,12},{12,8},{1,5},{5,1},{9,13},{13,9},{2,6},{6,2},{1... | collective-permute-start | bytes 6291464 | tf_op jit(solution)/shard_map/ppermute | solution.py:107
  295.6 4.6 collective-permute-start.13
  303.7 71.9 %collective-permute-start.18 = (bf16[512,2176]{1,0:T(8,128)(2,1)}, bf16[512,2176]{1,0:T(8,128)(2,1)S(1)}, u32[]{:S(2)}, u32[]{:S(2)}) collective-permute-start(bf16[512,2176]{1,0:T(8,128)(2,1)} %add_convert_fusion), channel_id=1, source_target_pairs={{0,8},{4,12},{8,0},{12,4},{1,9},{5,13},{9,1},{13,5},{2,10},{6,14},... | collective-permute-start | bytes 6684680 | tf_op jit(solution)/shard_map/ppermute | solution.py:107
  357.9 16.2 %collective-permute-start.14 = (bf16[128,2176]{1,0:T(8,128)(2,1)S(1)}, bf16[128,2176]{1,0:T(8,128)(2,1)S(1)}, u32[]{:S(2)}, u32[]{:S(2)}) collective-permute-start(bf16[128,2176]{1,0:T(8,128)(2,1)S(1)} %get-tuple-element.242), channel_id=1, source_target_pairs={{0,4},{4,0},{8,12},{12,8},{1,5},{5,1},{9,13},{13,9},{2,6},{6,2},{1... | collective-permute-start | bytes 1671176 | tf_op jit(solution)/shard_map/ppermute | solution.py:107
  358.0 17.6 %collective-permute-start.15 = (bf16[128,2176]{1,0:T(8,128)(2,1)S(1)}, bf16[128,2176]{1,0:T(8,128)(2,1)S(1)}, u32[]{:S(2)}, u32[]{:S(2)}) collective-permute-start(bf16[128,2176]{1,0:T(8,128)(2,1)S(1)} %get-tuple-element.241), channel_id=1, source_target_pairs={{0,4},{4,0},{8,12},{12,8},{1,5},{5,1},{9,13},{13,9},{2,6},{6,2},{1... | collective-permute-start | bytes 1671176 | tf_op jit(solution)/shard_map/ppermute | solution.py:107
  358.5 17.1 %collective-permute-start.16 = (bf16[128,2176]{1,0:T(8,128)(2,1)S(1)}, bf16[128,2176]{1,0:T(8,128)(2,1)S(1)}, u32[]{:S(2)}, u32[]{:S(2)}) collective-permute-start(bf16[128,2176]{1,0:T(8,128)(2,1)S(1)} %get-tuple-element.240), channel_id=1, source_target_pairs={{0,4},{4,0},{8,12},{12,8},{1,5},{5,1},{9,13},{13,9},{2,6},{6,2},{1... | collective-permute-start | bytes 1671176 | tf_op jit(solution)/shard_map/ppermute | solution.py:107
  358.6 17.1 %collective-permute-start.17 = (bf16[128,2176]{1,0:T(8,128)(2,1)S(1)}, bf16[128,2176]{1,0:T(8,128)(2,1)S(1)}, u32[]{:S(2)}, u32[]{:S(2)}) collective-permute-start(bf16[128,2176]{1,0:T(8,128)(2,1)S(1)} %get-tuple-element.239), channel_id=1, source_target_pairs={{0,4},{4,0},{8,12},{12,8},{1,5},{5,1},{9,13},{13,9},{2,6},{6,2},{1... | collective-permute-start | bytes 1671176 | tf_op jit(solution)/shard_map/ppermute | solution.py:107
  374.1 65.5 %collective-permute-start.25 = (bf16[704,2048]{1,0:T(8,128)(2,1)S(1)}, bf16[704,2048]{1,0:T(8,128)(2,1)}, u32[]{:S(2)}, u32[]{:S(2)}) collective-permute-start(bf16[704,2048]{1,0:T(8,128)(2,1)S(1)} %down_rows.1), channel_id=1, source_target_pairs={{0,16},{16,0},{1,17},{17,1},{2,18},{18,2},{3,19},{19,3},{4,20},{20... | collective-permute-start | bytes 8650760 | tf_op jit(solution)/shard_map/ppermute | solution.py:107
  377.9 55.3 %collective-permute-start.22 = (bf16[128,2176]{1,0:T(8,128)(2,1)}, bf16[128,2176]{1,0:T(8,128)(2,1)}, u32[]{:S(2)}, u32[]{:S(2)}) collective-permute-start(bf16[128,2176]{1,0:T(8,128)(2,1)} %get-tuple-element.222), channel_id=1, source_target_pairs={{0,3},{1,0},{2,1},{3,2},{4,7},{5,4},{6,5},{7,6},{8,11},{9,8},{10,9... | collective-permute-start | bytes 1671176 | tf_op jit(solution)/shard_map/ppermute | solution.py:57
  379.7 53.5 %collective-permute-start.23 = (bf16[128,2176]{1,0:T(8,128)(2,1)}, bf16[128,2176]{1,0:T(8,128)(2,1)}, u32[]{:S(2)}, u32[]{:S(2)}) collective-permute-start(bf16[128,2176]{1,0:T(8,128)(2,1)} %get-tuple-element.221), channel_id=1, source_target_pairs={{0,2},{1,3},{2,0},{3,1},{4,6},{5,7},{6,4},{7,5},{8,10},{9,11},{10,... | collective-permute-start | bytes 1671176 | tf_op jit(solution)/shard_map/ppermute | solution.py:57
  380.4 52.7 %collective-permute-start.24 = (bf16[128,2176]{1,0:T(8,128)(2,1)}, bf16[128,2176]{1,0:T(8,128)(2,1)}, u32[]{:S(2)}, u32[]{:S(2)}) collective-permute-start(bf16[128,2176]{1,0:T(8,128)(2,1)} %get-tuple-element.220), channel_id=1, source_target_pairs={{0,1},{1,2},{2,3},{3,0},{4,5},{5,6},{6,7},{7,4},{8,9},{9,10},{10,1... | collective-permute-start | bytes 1671176 | tf_op jit(solution)/shard_map/ppermute | solution.py:57
  413.9 87.5 %collective-permute-start.29 = (bf16[704,2048]{1,0:T(8,128)(2,1)}, bf16[704,2048]{1,0:T(8,128)(2,1)}, u32[]{:S(2)}, u32[]{:S(2)}) collective-permute-start(bf16[704,2048]{1,0:T(8,128)(2,1)} %get-tuple-element.111), channel_id=1, source_target_pairs={{0,16},{16,0},{1,17},{17,1},{2,18},{18,2},{3,19},{19,3},{4,20},{20... | collective-permute-start | bytes 8650760 | tf_op jit(solution)/shard_map/ppermute | solution.py:107
  427.5 98.8 %all-to-all-start.1 = ((bf16[4,512,2048]{2,1,0:T(8,128)(2,1)}), bf16[4,512,2048]{2,1,0:T(8,128)(2,1)}, u32[]{:S(2)}, u32[]{:S(2)}) async-start(bf16[4,512,2048]{2,1,0:T(8,128)(2,1)} %bitcast.162), calls=%async_computation.1 | async-start | bytes 16777216 | tf_op jit(solution)/shard_map/all_to_all | solution.py:653
  433.1 218.4 %reduce-scatter.5.cloned.1.call-start = ((), (), s32[]{:S(2)}) async-start(), calls=%async_computation.9 | async-start | bytes 2359296 | tf_op jit(solution)/shard_map/reduce_scatter | solution.py:679
  449.7 17.0 %collective-permute-start.26 = (bf16[128,2048]{1,0:T(8,128)(2,1)}, bf16[128,2048]{1,0:T(8,128)(2,1)S(1)}, u32[]{:S(2)}, u32[]{:S(2)}) collective-permute-start(bf16[128,2048]{1,0:T(8,128)(2,1)} %get-tuple-element.124), channel_id=1, source_target_pairs={{0,1},{1,2},{2,3},{3,0},{4,5},{5,6},{6,7},{7,4},{8,9},{9,10},{10,1... | collective-permute-start | bytes 1572872 | tf_op jit(solution)/shard_map/ppermute | solution.py:57
  450.6 36.1 %collective-permute-start.27 = (bf16[128,2048]{1,0:T(8,128)(2,1)}, bf16[128,2048]{1,0:T(8,128)(2,1)}, u32[]{:S(2)}, u32[]{:S(2)}) collective-permute-start(bf16[128,2048]{1,0:T(8,128)(2,1)} %get-tuple-element.124), channel_id=1, source_target_pairs={{0,2},{1,3},{2,0},{3,1},{4,6},{5,7},{6,4},{7,5},{8,10},{9,11},{10,... | collective-permute-start | bytes 1572872 | tf_op jit(solution)/shard_map/ppermute | solution.py:57
  451.9 34.8 %collective-permute-start.28 = (bf16[128,2048]{1,0:T(8,128)(2,1)}, bf16[128,2048]{1,0:T(8,128)(2,1)}, u32[]{:S(2)}, u32[]{:S(2)}) collective-permute-start(bf16[128,2048]{1,0:T(8,128)(2,1)} %get-tuple-element.124), channel_id=1, source_target_pairs={{0,3},{1,0},{2,1},{3,2},{4,7},{5,4},{6,5},{7,6},{8,11},{9,8},{10,9... | collective-permute-start | bytes 1572872 | tf_op jit(solution)/shard_map/ppermute | solution.py:57
  454.2 109.1 %collective-permute-start.33 = (bf16[1056,1024]{1,0:T(8,128)(2,1)}, bf16[1056,1024]{1,0:T(8,128)(2,1)}, u32[]{:S(2)}, u32[]{:S(2)}) collective-permute-start(bf16[1056,1024]{1,0:T(8,128)(2,1)} %copy-done.16), channel_id=1, source_target_pairs={{0,16},{16,0},{1,17},{17,1},{2,18},{18,2},{3,19},{19,3},{4,20},{20... | collective-permute-start | bytes 6488072 | tf_op jit(solution)/shard_map/ppermute | solution.py:107
  508.6 174.9 %reduce-scatter.3.cloned.1.call-start = ((), (), s32[]{:S(2)}) async-start(), calls=%async_computation.8 | async-start | bytes 7667712 | tf_op jit(solution)/shard_map/reduce_scatter | solution.py:761
  537.1 19.2 %collective-permute-start.34 = (f32[11,2048]{1,0:T(8,128)S(1)}, f32[11,2048]{1,0:T(8,128)S(1)}, u32[]{:S(2)}, u32[]{:S(2)}) collective-permute-start(f32[11,2048]{1,0:T(8,128)S(1)} %pad_maximum_fusion.6), channel_id=1, source_target_pairs={{0,1},{1,2},{2,3},{3,0},{4,5},{5,6},{6,7},{7,4},{8,9},{9,10},{10,1... | collective-permute-start | bytes 270344 | tf_op jit(solution)/shard_map/ppermute | solution.py:57
  538.7 17.6 %collective-permute-start.35 = (f32[11,2048]{1,0:T(8,128)S(1)}, f32[11,2048]{1,0:T(8,128)S(1)}, u32[]{:S(2)}, u32[]{:S(2)}) collective-permute-start(f32[11,2048]{1,0:T(8,128)S(1)} %pad_maximum_fusion.6), channel_id=1, source_target_pairs={{0,2},{1,3},{2,0},{3,1},{4,6},{5,7},{6,4},{7,5},{8,10},{9,11},{10,... | collective-permute-start | bytes 270344 | tf_op jit(solution)/shard_map/ppermute | solution.py:57
  540.0 16.4 %collective-permute-start.36 = (f32[11,2048]{1,0:T(8,128)S(1)}, f32[11,2048]{1,0:T(8,128)S(1)}, u32[]{:S(2)}, u32[]{:S(2)}) collective-permute-start(f32[11,2048]{1,0:T(8,128)S(1)} %pad_maximum_fusion.6), channel_id=1, source_target_pairs={{0,3},{1,0},{2,1},{3,2},{4,7},{5,4},{6,5},{7,6},{8,11},{9,8},{10,9... | collective-permute-start | bytes 270344 | tf_op jit(solution)/shard_map/ppermute | solution.py:57
  563.3 106.8 %collective-permute-start.37 = (bf16[704,2048]{1,0:T(8,128)(2,1)}, bf16[704,2048]{1,0:T(8,128)(2,1)}, u32[]{:S(2)}, u32[]{:S(2)}) collective-permute-start(bf16[704,2048]{1,0:T(8,128)(2,1)} %copy-done.5), channel_id=1, source_target_pairs={{0,16},{16,0},{1,17},{17,1},{2,18},{18,2},{3,19},{19,3},{4,20},{20... | collective-permute-start | bytes 8650760 | tf_op jit(solution)/shard_map/ppermute | solution.py:107
  569.6 73.8 %all-to-all-start.2 = ((bf16[4,1056,256]{2,1,0:T(8,128)(2,1)}), bf16[4,1056,256]{2,1,0:T(8,128)(2,1)}, u32[]{:S(2)}, u32[]{:S(2)}) async-start(bf16[4,1056,256]{2,1,0:T(8,128)(2,1)} %bitcast.161), calls=%async_computation.4 | async-start | bytes 4325376 | tf_op jit(solution)/shard_map/all_to_all | solution.py:712
  576.7 15.2 %collective-permute-start.30 = (bf16[128,2048]{1,0:T(8,128)(2,1)S(1)}, bf16[128,2048]{1,0:T(8,128)(2,1)S(1)}, u32[]{:S(2)}, u32[]{:S(2)}) collective-permute-start(bf16[128,2048]{1,0:T(8,128)(2,1)S(1)} %get-tuple-element.249), channel_id=1, source_target_pairs={{0,3},{1,0},{2,1},{3,2},{4,7},{5,4},{6,5},{7,6},{8,11},{9,8},{10,9... | collective-permute-start | bytes 1572872 | tf_op jit(solution)/shard_map/ppermute | solution.py:57
  578.5 35.9 %collective-permute-start.31 = (bf16[128,2048]{1,0:T(8,128)(2,1)S(1)}, bf16[128,2048]{1,0:T(8,128)(2,1)}, u32[]{:S(2)}, u32[]{:S(2)}) collective-permute-start(bf16[128,2048]{1,0:T(8,128)(2,1)S(1)} %get-tuple-element.248), channel_id=1, source_target_pairs={{0,2},{1,3},{2,0},{3,1},{4,6},{5,7},{6,4},{7,5},{8,10},{9,11},{10,... | collective-permute-start | bytes 1572872 | tf_op jit(solution)/shard_map/ppermute | solution.py:57
  584.6 68.7 %collective-permute-start.19 = (bf16[128,2048]{1,0:T(8,128)(2,1)}, bf16[128,2048]{1,0:T(8,128)(2,1)}, u32[]{:S(2)}, u32[]{:S(2)}) collective-permute-start(bf16[128,2048]{1,0:T(8,128)(2,1)} %get-tuple-element.209), channel_id=1, source_target_pairs={{0,3},{1,0},{2,1},{3,2},{4,7},{5,4},{6,5},{7,6},{8,11},{9,8},{10,9... | collective-permute-start | bytes 1572872 | tf_op jit(solution)/shard_map/ppermute | solution.py:57
  586.7 83.4 %collective-permute-start.20 = (bf16[128,2048]{1,0:T(8,128)(2,1)}, bf16[128,2048]{1,0:T(8,128)(2,1)}, u32[]{:S(2)}, u32[]{:S(2)}) collective-permute-start(bf16[128,2048]{1,0:T(8,128)(2,1)} %get-tuple-element.211), channel_id=1, source_target_pairs={{0,2},{1,3},{2,0},{3,1},{4,6},{5,7},{6,4},{7,5},{8,10},{9,11},{10,... | collective-permute-start | bytes 1572872 | tf_op jit(solution)/shard_map/ppermute | solution.py:57
  591.8 78.3 %collective-permute-start.21 = (bf16[128,2048]{1,0:T(8,128)(2,1)}, bf16[128,2048]{1,0:T(8,128)(2,1)}, u32[]{:S(2)}, u32[]{:S(2)}) collective-permute-start(bf16[128,2048]{1,0:T(8,128)(2,1)} %get-tuple-element.210), channel_id=1, source_target_pairs={{0,1},{1,2},{2,3},{3,0},{4,5},{5,6},{6,7},{7,4},{8,9},{9,10},{10,1... | collective-permute-start | bytes 1572872 | tf_op jit(solution)/shard_map/ppermute | solution.py:57
  614.4 39.0 %collective-permute-start.32 = (bf16[128,2048]{1,0:T(8,128)(2,1)}, bf16[128,2048]{1,0:T(8,128)(2,1)S(1)}, u32[]{:S(2)}, u32[]{:S(2)}) collective-permute-start(bf16[128,2048]{1,0:T(8,128)(2,1)} %get-tuple-element.247), channel_id=1, source_target_pairs={{0,1},{1,2},{2,3},{3,0},{4,5},{5,6},{6,7},{7,4},{8,9},{9,10},{10,1... | collective-permute-start | bytes 1572872 | tf_op jit(solution)/shard_map/ppermute | solution.py:57
  (62 other events, 631.0 us)
Sparse Core Ops, SparseCore 0:
  16.4 51.6 all-gather.3
  73.9 33.0 all-gather.5
  180.1 73.0 all-gather.7
  508.7 47.4 reduce-scatter.4
  563.5 90.3 reduce-scatter.2

commit v4 on v3

--- a/solution.py
+++ b/solution.py
@@ -78,10 +78,10 @@
     return total
 
 
-def ordered_sum(values, axis, beside):
+def ordered_sum(values, axis):
     count = lax.axis_size(axis)
     place = lax.axis_index(axis)
-    blocks = after(gather_blocks(values, axis), beside)
+    blocks = gather_blocks(values, axis)
     total = None
     for j in range(count):
         steps = (place - j) % count
@@ -699,7 +699,14 @@
         [query_grad.reshape(group_rows, head_cols), key_grad.reshape(group_rows, head_cols), value_grad],
         axis=1,
     )
-    in_grad = after(in_grad, branch_terms)
+    branch_blocks = []
+    for j in range(tp_count):
+        start = ((tp_index - j) % tp_count) * own_rows
+        rows = lax.dynamic_slice_in_dim(branch_terms, start, own_rows, 1)
+        branch_blocks.append(jnp.sum(rows.astype(F32), axis=0))
+    branch_blocks = [branch_blocks[0]] + [block.astype(BF16) for block in branch_blocks[1:]]
+    branch_parts = send_blocks(branch_blocks, "tp")
+    in_grad = after(in_grad, branch_blocks)
     bias_grad = jnp.sum(in_grad.astype(F32), axis=0)
     entry_part = dot_nt(in_grad, in_weight)
     entry_blocks = split_rows(entry_part.astype(BF16), tp_count)
@@ -711,13 +718,6 @@
     shared_mine = shared_mine.reshape(3 * shared_hidden, ep_count, slice_rows).transpose(1, 0, 2)
     shared_back = lax.all_to_all(shared_mine, "ep", split_axis=0, concat_axis=0, tiled=True)
     shared_back = shared_back.reshape(ep_count, 3, shared_hidden, slice_rows).astype(F32)
-    branch_blocks = []
-    for j in range(tp_count):
-        start = ((tp_index - j) % tp_count) * own_rows
-        rows = lax.dynamic_slice_in_dim(branch_terms, start, own_rows, 1)
-        branch_blocks.append(jnp.sum(rows.astype(F32), axis=0))
-    branch_blocks = [branch_blocks[0]] + [block.astype(BF16) for block in branch_blocks[1:]]
-    branch_parts = send_blocks(branch_blocks, "tp")
     last_sum = whole_sum(last_own, last_other, "dp").reshape(local_experts, hidden, width)
     first_sum = [whole_sum(first_own[0], first_other[0], "dp")]
     entry_parts = after(entry_parts, branch_parts, shared_mine, last_sum, first_sum)
@@ -731,9 +731,7 @@
     )
 
     entry_gain_part = jnp.sum(entry_part * entry_unit, axis=0, keepdims=True)
-    small_part = ordered_sum(
-        jnp.concatenate([router_part, middle_part, entry_gain_part], axis=0), "tp", branch_blocks
-    )
+    small_part = jnp.concatenate([router_part, middle_part, entry_gain_part], axis=0)
     bias_part = bias_grad.reshape(3, head_count, part_count, -1).transpose(2, 0, 1, 3)
     bias_part = bias_part.reshape(part_count, bias_rows)
     bias_part = jnp.pad(bias_part, ((0, 0), (0, bias_depth * slice_rows - bias_rows)))
@@ -758,10 +756,12 @@
     )
     if dp_count == 2:
         dense_grad = after(dense_grad, grads_other)
+    dense_grad = after(dense_grad, branch_parts[0], branch_parts[-1])
     dense_sum = lax.psum_scatter(
         dense_grad, ("dp", "ep"), scatter_dimension=0, tiled=True
     ).astype(F32)
     small_sum = dense_sum[:, 3 * head_cols : 3 * head_cols + half] + dense_sum[:, 3 * head_cols + half :]
+    tp_sum = ordered_sum(small_sum[:, : expert_count + 3].T, "tp")
     bias_sum = small_sum[:, expert_count + 3 : expert_count + 3 + bias_depth]
     bias_sum = bias_sum.T.reshape(-1)[:bias_rows].reshape(heads_bias.shape)
 
@@ -777,10 +777,10 @@
         dense_sum[:, 2 * head_cols : 3 * head_cols],
         mixing_sum.astype(F32),
         bias_sum,
-        small_sum[:, expert_count + 2],
-        small_sum[:, expert_count + 1],
-        small_sum[:, :expert_count],
-        small_sum[:, expert_count],
+        tp_sum[expert_count + 2],
+        tp_sum[expert_count + 1],
+        tp_sum[:expert_count].T,
+        tp_sum[expert_count],
         by_columns(shared_back[:, 0]),
         by_columns(shared_back[:, 1]),
         shared_back[:, 2].reshape(ep_count * shared_hidden, slice_rows),

time: 709 us -> 689 us (0.972)
  starting transfers between devices: 90 us -> 70.2 us
  Pallas kernels: 105 us -> 97.7 us
    ppermute x24, starting transfers between devices: 65.3 us -> 45.6 us  [shifted(): lax.ppermute(block, axis, [(i, (i + step) % count) for i in range(count)])]
    all_to_all x1, waiting for transfers between devices: 0.01 us -> 16.6 us  [body(): lax.all_to_all(shared_mine, 'ep', split_axis=0, concat_axis=0, tiled=True)]
    ppermute x24, waiting for transfers between devices: 141 us -> 129 us  [shifted(): lax.ppermute(block, axis, [(i, (i + step) % count) for i in range(count)])]
    pallas_call x2, Pallas kernels: 93.6 us -> 85.8 us  [run_experts(): pl.pallas_call(lambda *refs: expert_kernel(tp_count, expert_count, *refs)...]
    unnamed x154 -> x156, local copies, waits for them, and re-layouts: 43.6 us -> 45.8 us
  transfers between devices with their start and end apart: 46 -> 46, of which waited for: 16 -> 18; matrix products, arithmetic and copies ran while one was open for 32% -> 33% of each run, Pallas kernels for 9% -> 8%
where the time goes in v4:
time: 689 us; the launch traced here: 678 us
  waiting for transfers between devices  226 us (33%)
  Pallas kernels  97.7 us (14%)
  matrix products  94.4 us (14%)
  other arithmetic  89.3 us (13%)
  local copies, waits for them, and re-layouts  84.9 us (12%)
  starting transfers between devices  70.2 us (10%)
  between operations  15.4 us (2%)
    ppermute x24, waiting for transfers between devices, shifted(): lax.ppermute(block, axis, [(i, (i + step) % count) for i in range(count)])  129 us
    pallas_call x2, Pallas kernels, run_experts(): pl.pallas_call(lambda *refs: expert_kernel(tp_count, expert_count, *refs)...  85.8 us
    dot_general x4, matrix products, dot_tn(): lax.dot_general(left, right, (((0,), (0,)), ((), ())), preferred_element_...  50.6 us
    unnamed x156, local copies, waits for them, and re-layouts  45.8 us
    ppermute x24, starting transfers between devices, shifted(): lax.ppermute(block, axis, [(i, (i + step) % count) for i in range(count)])  45.6 us
    all_gather x1, waiting for transfers between devices, body(): lax.all_gather(middle_normed, ('ep', 'tp'), axis=0, tiled=True)  30.9 us
    ppermute x14, waiting for transfers between devices, swapped(): return lax.ppermute(values, axis, [(i, i ^ bit) for i in range(count)])  28.2 us
    dot_general x4, matrix products, dot_nn(): lax.dot_general(left, right, (((1,), (0,)), ((), ())), preferred_element_...  22.8 us
  transfers between devices with their start and end apart: 46, of which 18 were waited for; matrix products, arithmetic and copies ran while one was open for 33% of the time, Pallas kernels for 8%

profile of v4, /device:TPU:0, one launch (start us, length us, event | category | flops | bytes accessed | tf_op | source)
XLA Modules:
  0.0 677.8 jit_solution(11342400402390048492)
XLA Ops:
  16.3 3.1 collective-permute-start
  29.5 5.2 collective-permute-done
  34.6 21.6 %collective-permute-done.1 = bf16[128,2048]{1,0:T(8,128)(2,1)} collective-permute-done((bf16[128,2048]{1,0:T(8,128)(2,1)}, bf16[128,2048]{1,0:T(8,128)(2,1)}, u32[]{:S(2)}, u32[]{:S(2)}) %collective-permute-start.1) | collective-permute-done | bytes 524320 | tf_op jit(solution)/shard_map/ppermute | solution.py:57
  56.3 11.7 %collective-permute-start.6 = (bf16[128,2048]{1,0:T(8,128)(2,1)S(1)}, bf16[128,2048]{1,0:T(8,128)(2,1)}, u32[]{:S(2)}, u32[]{:S(2)}) collective-permute-start(bf16[128,2048]{1,0:T(8,128)(2,1)S(1)} %copy-done.12), channel_id=1, source_target_pairs={{0,1},{1,2},{2,3},{3,0},{4,5},{5,6},{6,7},{7,4},{8,9},{9,10},{10,1... | collective-permute-start | bytes 1572872 | tf_op jit(solution)/shard_map/ppermute | solution.py:57
  74.5 5.7 fusion.10
  85.7 4.5 all-to-all-start
  97.4 9.5 %all-gather.6.cloned.1.call-done = bf16[512,2048]{1,0:T(8,128)(2,1)} async-done(((bf16[512,256]{1,0:T(8,128)(2,1)}), bf16[512,2048]{1,0:T(8,128)(2,1)}) %all-gather.6.cloned.1.call-update) | async-done | bytes 2097168 | tf_op jit(solution)/shard_map/all_gather | solution.py:443
  112.3 10.0 %all-to-all-done = bf16[4,1056,256]{2,1,0:T(8,128)(2,1)} async-done(((bf16[4,1056,256]{2,1,0:T(8,128)(2,1)}), bf16[4,1056,256]{2,1,0:T(8,128)(2,1)}, u32[]{:S(2)}, u32[]{:S(2)}) %all-to-all-start) | async-done | bytes 2162720 | tf_op jit(solution)/shard_map/all_to_all | solution.py:480
  134.8 7.8 %collective-permute-done.3 = bf16[128,2048]{1,0:T(8,128)(2,1)S(1)} collective-permute-done((bf16[128,2048]{1,0:T(8,128)(2,1)}, bf16[128,2048]{1,0:T(8,128)(2,1)S(1)}, u32[]{:S(2)}, u32[]{:S(2)}) %collective-permute-start.3) | collective-permute-done | bytes 524320 | tf_op jit(solution)/shard_map/ppermute | solution.py:57
  142.6 33.0 %collective-permute-done.4 = bf16[128,2048]{1,0:T(8,128)(2,1)S(1)} collective-permute-done((bf16[128,2048]{1,0:T(8,128)(2,1)}, bf16[128,2048]{1,0:T(8,128)(2,1)S(1)}, u32[]{:S(2)}, u32[]{:S(2)}) %collective-permute-start.4) | collective-permute-done | bytes 524320 | tf_op jit(solution)/shard_map/ppermute | solution.py:57
  194.9 4.0 fusion.27.refs_3_
  215.4 3.3 order_rows.1.refs_2_
  218.7 3.3 copy-done.3
  222.0 30.9 %all-gather.8.cloned.1.call-done.refs_1_ = bf16[2048,2048]{1,0:T(8,128)(2,1)} async-done(((bf16[128,2048]{1,0:T(8,128)(2,1)}), bf16[2048,2048]{1,0:T(8,128)(2,1)}) %all-gather.8.cloned.1.call-update) | async-done | bytes 8388624 | tf_op jit(solution)/shard_map/all_gather | solution.py:545
  252.8 43.0 %experts.2 = (bf16[512,2176]{1,0:T(8,128)(2,1)}, bf16[512,2176]{1,0:T(8,128)(2,1)}, bf16[2048,2304]{1,0:T(8,128)(2,1)}, bf16[2048,1152]{1,0:T(8,128)(2,1)}) custom-call(s32[3]{0:T(128)} %add_add_fusion.1.refs_0_, bf16[2048,2048]{1,0:T(8,128)(2,1)} %all-gather.8.cloned.1.call-done.refs_1_, bf16[2048,2048]{1,0:T(8,128)(2,1)} %copy-done.3, ...), custom_call_target="tpu_custom_call" | custom-call | flops 24159191040 | bytes 33816576 | tf_op jit(solution)/shard_map/experts/pallas_call | solution.py:327
  296.1 4.3 collective-permute-done.13
  300.4 3.6 add_convert_fusion
  305.1 42.8 %experts.3 = (bf16[512,2176]{1,0:T(8,128)(2,1)}, bf16[512,2176]{1,0:T(8,128)(2,1)}, bf16[2048,2304]{1,0:T(8,128)(2,1)}, bf16[2048,1152]{1,0:T(8,128)(2,1)}) custom-call(s32[3]{0:T(128)} %add_add_fusion.2.refs_0_, bf16[2048,2048]{1,0:T(8,128)(2,1)} %all-gather.8.cloned.1.call-done.refs_1_, ...), custom_call_target="tpu_custom_call", output_to_operand_aliasing={{2}: (8, {}), {3}: (9, {})} | custom-call | flops 24159191040 | bytes 33816576 | tf_op jit(solution)/shard_map/experts/pallas_call | solution.py:327
  350.8 14.0 %convolution_convert_fusion.3.refs_0_.refs_1_ = bf16[1152,2048]{1,0:T(8,128)(2,1)S(1)} fusion(bf16[2048,1152]{1,0:T(8,128)(2,1)} %get-tuple-element.110, bf16[2048,2048]{1,0:T(8,128)(2,1)} %copy-done.3), kind=kOutput, calls=%fused_computation.12 | convolution fusion | flops 9666035712 | bytes 17825792 | tf_op jit(solution)/shard_map/dot_general | solution.py:26
  373.7 24.6 %convolution_convert_fusion.refs_0_ = bf16[2304,2048]{1,0:T(8,128)(2,1)} fusion(bf16[2048,2304]{1,0:T(8,128)(2,1)} %get-tuple-element.107, bf16[2048,2048]{1,0:T(8,128)(2,1)S(1)} %bitcast.209), kind=kOutput, calls=%fused_computation.3 | convolution fusion | flops 19332071424 | bytes 27262976 | tf_op jit(solution)/shard_map/dot_general | solution.py:26
  398.3 3.7 copy-done.2
  402.0 3.9 first_rows.1
  406.4 12.9 %convolution_convert_fusion.2 = bf16[2048,2048]{1,0:T(8,128)(2,1)} fusion(bf16[2048,1152]{1,0:T(8,128)(2,1)S(1)} %bitcast.213, bf16[1152,2048]{1,0:T(8,128)(2,1)S(1)} %bitcast.181), kind=kOutput, calls=%fused_computation.11 | convolution fusion | flops 9667870720 | bytes 17825792 | tf_op jit(solution)/shard_map/dot_general | solution.py:18
  419.3 5.6 all-to-all-start.1
  425.0 6.6 collective-permute-done.25
  436.5 3.4 own_rows.1
  449.3 9.7 %collective-permute-done.26 = bf16[128,2048]{1,0:T(8,128)(2,1)} collective-permute-done((bf16[128,2048]{1,0:T(8,128)(2,1)}, bf16[128,2048]{1,0:T(8,128)(2,1)}, u32[]{:S(2)}, u32[]{:S(2)}) %collective-permute-start.26) | collective-permute-done | bytes 524320 | tf_op jit(solution)/shard_map/ppermute | solution.py:57
  458.9 19.9 %collective-permute-done.27 = bf16[128,2048]{1,0:T(8,128)(2,1)} collective-permute-done((bf16[128,2048]{1,0:T(8,128)(2,1)}, bf16[128,2048]{1,0:T(8,128)(2,1)}, u32[]{:S(2)}, u32[]{:S(2)}) %collective-permute-start.27) | collective-permute-done | bytes 524320 | tf_op jit(solution)/shard_map/ppermute | solution.py:57
  478.8 14.6 %collective-permute-done.29 = bf16[704,2048]{1,0:T(8,128)(2,1)} collective-permute-done((bf16[704,2048]{1,0:T(8,128)(2,1)}, bf16[704,2048]{1,0:T(8,128)(2,1)}, u32[]{:S(2)}, u32[]{:S(2)}) %collective-permute-start.29) | collective-permute-done | bytes 2883616 | tf_op jit(solution)/shard_map/ppermute | solution.py:107
  499.1 3.6 convolution_convert_fusion.4
  502.9 3.7 convolution_convert_fusion.6
  506.5 2.9 multiply_reduce_fusion.1
  518.1 5.7 dynamic-slice_reduce_fusion.2
  526.6 3.1 convert_reduce_fusion
  529.7 8.3 %multiply_reduce_fusion = (f32[2048]{0:T(1024)S(1)}, bf16[512,2048]{1,0:T(8,128)(2,1)}, f32[512,2048]{1,0:T(8,128)}) fusion(f32[512]{0:T(512)S(1)} %copy-done.53, bf16[512,2048]{1,0:T(8,128)(2,1)S(1)} %copy-done.20, bf16[512,1536]{0,1:T(8,128)(2,1)S(1)} %copy-done.26, bf16[2048,1664]{0,1:T(8,128)(2,1)} %all-gather.4.cloned.1.call-done), kind=kOutput, calls=%fused_computation.27 | convolution fusion | flops 3226466304 | bytes 16263168 | tf_op jit(solution)/shard_map/dot_general | solution.py:22
  538.7 8.4 %convolution_convert_fusion.1 = bf16[2048,1536]{0,1:T(8,128)(2,1)} fusion(bf16[512,1536]{0,1:T(8,128)(2,1)} %pad_maximum_fusion.4, f32[2048]{0:T(1024)S(1)} %bitcast.194, f32[512]{0:T(512)S(1)} %copy-done.53, bf16[512,2048]{1,0:T(8,128)(2,1)} %copy-done.19), kind=kOutput, calls=%fused_computation.10 | convolution fusion | flops 3228565504 | bytes 9971712 | tf_op jit(solution)/shard_map/dot_general | solution.py:26
  547.0 6.9 %pad_maximum_fusion = bf16[2048,1664]{0,1:T(8,128)(2,1)} fusion(bf16[2048,128]{0,1:T(8,128)(2,1)S(1)} %fusion.32, bf16[2048,1536]{0,1:T(8,128)(2,1)} %convolution_convert_fusion.1), kind=kLoop, calls=%fused_computation.13 | loop fusion | flops 13631488 | bytes 13631488 | tf_op jit(solution)/shard_map/concatenate | solution.py:750
  555.7 3.3 add_convert_fusion.1
  560.4 4.6 all-to-all-start.2
  565.0 6.1 convert_add_fusion.2
  578.3 7.4 %convert_add_fusion.1 = f32[704,2048]{1,0:T(8,128)} fusion(bf16[704,2048]{1,0:T(8,128)(2,1)} %collective-permute-done.29, bf16[704,2048]{1,0:T(8,128)(2,1)} %get-tuple-element.108), kind=kLoop, calls=%fused_computation.15 | loop fusion | flops 4325376 | bytes 11534336 | tf_op jit(solution)/shard_map/add | solution.py:101
  585.7 16.6 %all-to-all-done.2 = bf16[4,1056,256]{2,1,0:T(8,128)(2,1)} async-done(((bf16[4,1056,256]{2,1,0:T(8,128)(2,1)}), bf16[4,1056,256]{2,1,0:T(8,128)(2,1)}, u32[]{:S(2)}, u32[]{:S(2)}) %all-to-all-start.2) | async-done | bytes 2162720 | tf_op jit(solution)/shard_map/all_to_all | solution.py:719
  602.2 3.5 fusion.70
  605.8 2.9 copy.161
  612.0 30.9 %collective-permute-done.31 = bf16[128,2048]{1,0:T(8,128)(2,1)} collective-permute-done((bf16[128,2048]{1,0:T(8,128)(2,1)}, bf16[128,2048]{1,0:T(8,128)(2,1)}, u32[]{:S(2)}, u32[]{:S(2)}) %collective-permute-start.31) | collective-permute-done | bytes 524320 | tf_op jit(solution)/shard_map/ppermute | solution.py:57
  650.6 3.5 multiply_add_fusion
  654.0 5.3 convert_add_fusion
  660.7 3.6 collective-permute-start.34
  (357 shorter events, 166.3 us)
Async XLA Ops:
  7.2 123.5 %copy-start = (s32[8]{0:T(128)S(1)}, s32[8]{0:T(128)}, u32[]{:S(2)}) copy-start(s32[8]{0:T(128)} %param.23) | copy-start | bytes 100
  7.2 65.3 %all-gather.4.cloned.1.call-start = ((), (), s32[]{:S(2)}) async-start(), calls=%async_computation.5 | async-start | bytes 7667712 | tf_op jit(solution)/shard_map/all_gather | solution.py:440
  16.3 90.6 %all-gather.6.cloned.1.call-start = ((), (), s32[]{:S(2)}) async-start(), calls=%async_computation.6 | async-start | bytes 2359296 | tf_op jit(solution)/shard_map/all_gather | solution.py:443
  16.3 18.3 %collective-permute-start = (bf16[128,2048]{1,0:T(8,128)(2,1)}, bf16[128,2048]{1,0:T(8,128)(2,1)}, u32[]{:S(2)}, u32[]{:S(2)}) collective-permute-start(bf16[128,2048]{1,0:T(8,128)(2,1)} %param.21), channel_id=1, source_target_pairs={{0,1},{1,2},{2,3},{3,0},{4,5},{5,6},{6,7},{7,4},{8,9},{9,10},{10,1... | collective-permute-start | bytes 1572872 | tf_op jit(solution)/shard_map/ppermute | solution.py:57
  19.4 36.9 %collective-permute-start.1 = (bf16[128,2048]{1,0:T(8,128)(2,1)}, bf16[128,2048]{1,0:T(8,128)(2,1)}, u32[]{:S(2)}, u32[]{:S(2)}) collective-permute-start(bf16[128,2048]{1,0:T(8,128)(2,1)} %param.21), channel_id=1, source_target_pairs={{0,2},{1,3},{2,0},{3,1},{4,6},{5,7},{6,4},{7,5},{8,10},{9,11},{10,... | collective-permute-start | bytes 1572872 | tf_op jit(solution)/shard_map/ppermute | solution.py:57
  22.0 34.3 %collective-permute-start.2 = (bf16[128,2048]{1,0:T(8,128)(2,1)}, bf16[128,2048]{1,0:T(8,128)(2,1)}, u32[]{:S(2)}, u32[]{:S(2)}) collective-permute-start(bf16[128,2048]{1,0:T(8,128)(2,1)} %param.21), channel_id=1, source_target_pairs={{0,3},{1,0},{2,1},{3,2},{4,7},{5,4},{6,5},{7,6},{8,11},{9,8},{10,9... | collective-permute-start | bytes 1572872 | tf_op jit(solution)/shard_map/ppermute | solution.py:57
  26.2 67.0 %copy-start.24 = (pred[512,512]{0,1:T(8,128)(4,1)}, pred[512,512]{0,1:T(8,128)(4,1)S(1)}, u32[]{:S(2)}) copy-start(pred[512,512]{0,1:T(8,128)(4,1)S(1)} %broadcast_compare_fusion) | copy-start | bytes 786436
  56.3 67.5 %collective-permute-start.6 = (bf16[128,2048]{1,0:T(8,128)(2,1)S(1)}, bf16[128,2048]{1,0:T(8,128)(2,1)}, u32[]{:S(2)}, u32[]{:S(2)}) collective-permute-start(bf16[128,2048]{1,0:T(8,128)(2,1)S(1)} %copy-done.12), channel_id=1, source_target_pairs={{0,1},{1,2},{2,3},{3,0},{4,5},{5,6},{6,7},{7,4},{8,9},{9,10},{10,1... | collective-permute-start | bytes 1572872 | tf_op jit(solution)/shard_map/ppermute | solution.py:57
  68.0 55.8 %collective-permute-start.7 = (bf16[128,2048]{1,0:T(8,128)(2,1)S(1)}, bf16[128,2048]{1,0:T(8,128)(2,1)}, u32[]{:S(2)}, u32[]{:S(2)}) collective-permute-start(bf16[128,2048]{1,0:T(8,128)(2,1)S(1)} %copy-done.12), channel_id=1, source_target_pairs={{0,2},{1,3},{2,0},{3,1},{4,6},{5,7},{6,4},{7,5},{8,10},{9,11},{10,... | collective-permute-start | bytes 1572872 | tf_op jit(solution)/shard_map/ppermute | solution.py:57
  69.6 54.3 %collective-permute-start.8 = (bf16[128,2048]{1,0:T(8,128)(2,1)S(1)}, bf16[128,2048]{1,0:T(8,128)(2,1)}, u32[]{:S(2)}, u32[]{:S(2)}) collective-permute-start(bf16[128,2048]{1,0:T(8,128)(2,1)S(1)} %copy-done.12), channel_id=1, source_target_pairs={{0,3},{1,0},{2,1},{3,2},{4,7},{5,4},{6,5},{7,6},{8,11},{9,8},{10,9... | collective-permute-start | bytes 1572872 | tf_op jit(solution)/shard_map/ppermute | solution.py:57
  85.7 36.6 %all-to-all-start = ((bf16[4,1056,256]{2,1,0:T(8,128)(2,1)}), bf16[4,1056,256]{2,1,0:T(8,128)(2,1)}, u32[]{:S(2)}, u32[]{:S(2)}) async-start(bf16[4,1056,256]{2,1,0:T(8,128)(2,1)} %pad_maximum_fusion.2), calls=%async_computation | async-start | bytes 4325376 | tf_op jit(solution)/shard_map/all_to_all | solution.py:480
  90.2 162.6 %all-gather.8.cloned.1.call-start = ((), (), s32[]{:S(2)}) async-start(), calls=%async_computation.7 | async-start | bytes 8912896 | tf_op jit(solution)/shard_map/all_gather | solution.py:545
  122.3 53.3 %collective-permute-start.10 = (bf16[4,1056,256]{2,1,0:T(8,128)(2,1)}, bf16[4,1056,256]{2,1,0:T(8,128)(2,1)}, u32[]{:S(2)}, u32[]{:S(2)}) collective-permute-start(bf16[4,1056,256]{2,1,0:T(8,128)(2,1)} %all-to-all-done), channel_id=1, source_target_pairs={{0,16},{16,0},{1,17},{17,1},{2,18},{18,2},{3,19},{19,3},{4,20},{20... | collective-permute-start | bytes 6488072 | tf_op jit(solution)/shard_map/ppermute | solution.py:107
  127.1 48.4 %collective-permute-start.9 = (bf16[512,2048]{1,0:T(8,128)(2,1)S(1)}, bf16[512,2048]{1,0:T(8,128)(2,1)}, u32[]{:S(2)}, u32[]{:S(2)}) collective-permute-start(bf16[512,2048]{1,0:T(8,128)(2,1)S(1)} %constant_dynamic-update-slice_fusion.refs_0_), channel_id=1, source_target_pairs={{0,8},{4,12},{8,0},{12,4},{1,9},{5,13},{9,1},{13,5},{2,10},{6,14},... | collective-permute-start | bytes 6291464 | tf_op jit(solution)/shard_map/ppermute | solution.py:107
  127.6 15.0 %collective-permute-start.3 = (bf16[128,2048]{1,0:T(8,128)(2,1)}, bf16[128,2048]{1,0:T(8,128)(2,1)S(1)}, u32[]{:S(2)}, u32[]{:S(2)}) collective-permute-start(bf16[128,2048]{1,0:T(8,128)(2,1)} %get-tuple-element.247), channel_id=1, source_target_pairs={{0,3},{1,0},{2,1},{3,2},{4,7},{5,4},{6,5},{7,6},{8,11},{9,8},{10,9... | collective-permute-start | bytes 1572872 | tf_op jit(solution)/shard_map/ppermute | solution.py:57
  129.9 45.7 %collective-permute-start.4 = (bf16[128,2048]{1,0:T(8,128)(2,1)}, bf16[128,2048]{1,0:T(8,128)(2,1)S(1)}, u32[]{:S(2)}, u32[]{:S(2)}) collective-permute-start(bf16[128,2048]{1,0:T(8,128)(2,1)} %get-tuple-element.246), channel_id=1, source_target_pairs={{0,2},{1,3},{2,0},{3,1},{4,6},{5,7},{6,4},{7,5},{8,10},{9,11},{10,... | collective-permute-start | bytes 1572872 | tf_op jit(solution)/shard_map/ppermute | solution.py:57
  130.5 45.1 %collective-permute-start.5 = (bf16[128,2048]{1,0:T(8,128)(2,1)}, bf16[128,2048]{1,0:T(8,128)(2,1)}, u32[]{:S(2)}, u32[]{:S(2)}) collective-permute-start(bf16[128,2048]{1,0:T(8,128)(2,1)} %get-tuple-element.245), channel_id=1, source_target_pairs={{0,1},{1,2},{2,3},{3,0},{4,5},{5,6},{6,7},{7,4},{8,9},{9,10},{10,1... | collective-permute-start | bytes 1572872 | tf_op jit(solution)/shard_map/ppermute | solution.py:57
  200.8 14.6 %collective-permute-start.11 = (bf16[512,2048]{1,0:T(8,128)(2,1)S(1)}, bf16[512,2048]{1,0:T(8,128)(2,1)}, u32[]{:S(2)}, u32[]{:S(2)}) collective-permute-start(bf16[512,2048]{1,0:T(8,128)(2,1)S(1)} %constant_dynamic-update-slice_fusion.refs_0_), channel_id=1, source_target_pairs={{0,4},{4,0},{8,12},{12,8},{1,5},{5,1},{9,13},{13,9},{2,6},{6,2},{1... | collective-permute-start | bytes 6291464 | tf_op jit(solution)/shard_map/ppermute | solution.py:107
  200.8 14.6 %collective-permute-start.12 = (bf16[512,2048]{1,0:T(8,128)(2,1)}, bf16[512,2048]{1,0:T(8,128)(2,1)}, u32[]{:S(2)}, u32[]{:S(2)}) collective-permute-start(bf16[512,2048]{1,0:T(8,128)(2,1)} %collective-permute-done.9.refs_2_), channel_id=1, source_target_pairs={{0,4},{4,0},{8,12},{12,8},{1,5},{5,1},{9,13},{13,9},{2,6},{6,2},{1... | collective-permute-start | bytes 6291464 | tf_op jit(solution)/shard_map/ppermute | solution.py:107
  295.8 4.6 collective-permute-start.13
  304.0 63.8 %collective-permute-start.18 = (bf16[512,2176]{1,0:T(8,128)(2,1)}, bf16[512,2176]{1,0:T(8,128)(2,1)S(1)}, u32[]{:S(2)}, u32[]{:S(2)}) collective-permute-start(bf16[512,2176]{1,0:T(8,128)(2,1)} %add_convert_fusion), channel_id=1, source_target_pairs={{0,8},{4,12},{8,0},{12,4},{1,9},{5,13},{9,1},{13,5},{2,10},{6,14},... | collective-permute-start | bytes 6684680 | tf_op jit(solution)/shard_map/ppermute | solution.py:107
  349.8 16.4 %collective-permute-start.14 = (bf16[128,2176]{1,0:T(8,128)(2,1)S(1)}, bf16[128,2176]{1,0:T(8,128)(2,1)S(1)}, u32[]{:S(2)}, u32[]{:S(2)}) collective-permute-start(bf16[128,2176]{1,0:T(8,128)(2,1)S(1)} %get-tuple-element.236), channel_id=1, source_target_pairs={{0,4},{4,0},{8,12},{12,8},{1,5},{5,1},{9,13},{13,9},{2,6},{6,2},{1... | collective-permute-start | bytes 1671176 | tf_op jit(solution)/shard_map/ppermute | solution.py:107
  349.8 17.9 %collective-permute-start.15 = (bf16[128,2176]{1,0:T(8,128)(2,1)S(1)}, bf16[128,2176]{1,0:T(8,128)(2,1)S(1)}, u32[]{:S(2)}, u32[]{:S(2)}) collective-permute-start(bf16[128,2176]{1,0:T(8,128)(2,1)S(1)} %get-tuple-element.235), channel_id=1, source_target_pairs={{0,4},{4,0},{8,12},{12,8},{1,5},{5,1},{9,13},{13,9},{2,6},{6,2},{1... | collective-permute-start | bytes 1671176 | tf_op jit(solution)/shard_map/ppermute | solution.py:107
  350.3 17.4 %collective-permute-start.16 = (bf16[128,2176]{1,0:T(8,128)(2,1)S(1)}, bf16[128,2176]{1,0:T(8,128)(2,1)S(1)}, u32[]{:S(2)}, u32[]{:S(2)}) collective-permute-start(bf16[128,2176]{1,0:T(8,128)(2,1)S(1)} %get-tuple-element.234), channel_id=1, source_target_pairs={{0,4},{4,0},{8,12},{12,8},{1,5},{5,1},{9,13},{13,9},{2,6},{6,2},{1... | collective-permute-start | bytes 1671176 | tf_op jit(solution)/shard_map/ppermute | solution.py:107
  350.4 17.3 %collective-permute-start.17 = (bf16[128,2176]{1,0:T(8,128)(2,1)S(1)}, bf16[128,2176]{1,0:T(8,128)(2,1)S(1)}, u32[]{:S(2)}, u32[]{:S(2)}) collective-permute-start(bf16[128,2176]{1,0:T(8,128)(2,1)S(1)} %get-tuple-element.233), channel_id=1, source_target_pairs={{0,4},{4,0},{8,12},{12,8},{1,5},{5,1},{9,13},{13,9},{2,6},{6,2},{1... | collective-permute-start | bytes 1671176 | tf_op jit(solution)/shard_map/ppermute | solution.py:107
  366.1 65.5 %collective-permute-start.25 = (bf16[704,2048]{1,0:T(8,128)(2,1)S(1)}, bf16[704,2048]{1,0:T(8,128)(2,1)}, u32[]{:S(2)}, u32[]{:S(2)}) collective-permute-start(bf16[704,2048]{1,0:T(8,128)(2,1)S(1)} %down_rows.1), channel_id=1, source_target_pairs={{0,16},{16,0},{1,17},{17,1},{2,18},{18,2},{3,19},{19,3},{4,20},{20... | collective-permute-start | bytes 8650760 | tf_op jit(solution)/shard_map/ppermute | solution.py:107
  370.0 55.0 %collective-permute-start.22 = (bf16[128,2176]{1,0:T(8,128)(2,1)}, bf16[128,2176]{1,0:T(8,128)(2,1)}, u32[]{:S(2)}, u32[]{:S(2)}) collective-permute-start(bf16[128,2176]{1,0:T(8,128)(2,1)} %get-tuple-element.216), channel_id=1, source_target_pairs={{0,3},{1,0},{2,1},{3,2},{4,7},{5,4},{6,5},{7,6},{8,11},{9,8},{10,9... | collective-permute-start | bytes 1671176 | tf_op jit(solution)/shard_map/ppermute | solution.py:57
  371.5 53.5 %collective-permute-start.23 = (bf16[128,2176]{1,0:T(8,128)(2,1)}, bf16[128,2176]{1,0:T(8,128)(2,1)}, u32[]{:S(2)}, u32[]{:S(2)}) collective-permute-start(bf16[128,2176]{1,0:T(8,128)(2,1)} %get-tuple-element.215), channel_id=1, source_target_pairs={{0,2},{1,3},{2,0},{3,1},{4,6},{5,7},{6,4},{7,5},{8,10},{9,11},{10,... | collective-permute-start | bytes 1671176 | tf_op jit(solution)/shard_map/ppermute | solution.py:57
  372.3 52.7 %collective-permute-start.24 = (bf16[128,2176]{1,0:T(8,128)(2,1)}, bf16[128,2176]{1,0:T(8,128)(2,1)}, u32[]{:S(2)}, u32[]{:S(2)}) collective-permute-start(bf16[128,2176]{1,0:T(8,128)(2,1)} %get-tuple-element.214), channel_id=1, source_target_pairs={{0,1},{1,2},{2,3},{3,0},{4,5},{5,6},{6,7},{7,4},{8,9},{9,10},{10,1... | collective-permute-start | bytes 1671176 | tf_op jit(solution)/shard_map/ppermute | solution.py:57
  405.9 87.6 %collective-permute-start.29 = (bf16[704,2048]{1,0:T(8,128)(2,1)}, bf16[704,2048]{1,0:T(8,128)(2,1)}, u32[]{:S(2)}, u32[]{:S(2)}) collective-permute-start(bf16[704,2048]{1,0:T(8,128)(2,1)} %get-tuple-element.108), channel_id=1, source_target_pairs={{0,16},{16,0},{1,17},{17,1},{2,18},{18,2},{3,19},{19,3},{4,20},{20... | collective-permute-start | bytes 8650760 | tf_op jit(solution)/shard_map/ppermute | solution.py:107
  419.3 98.8 %all-to-all-start.1 = ((bf16[4,512,2048]{2,1,0:T(8,128)(2,1)}), bf16[4,512,2048]{2,1,0:T(8,128)(2,1)}, u32[]{:S(2)}, u32[]{:S(2)}) async-start(bf16[4,512,2048]{2,1,0:T(8,128)(2,1)} %bitcast.168), calls=%async_computation.1 | async-start | bytes 16777216 | tf_op jit(solution)/shard_map/all_to_all | solution.py:653
  424.9 185.3 %reduce-scatter.5.cloned.1.call-start = ((), (), s32[]{:S(2)}) async-start(), calls=%async_computation.9 | async-start | bytes 2359296 | tf_op jit(solution)/shard_map/reduce_scatter | solution.py:679
  441.8 17.1 %collective-permute-start.26 = (bf16[128,2048]{1,0:T(8,128)(2,1)}, bf16[128,2048]{1,0:T(8,128)(2,1)}, u32[]{:S(2)}, u32[]{:S(2)}) collective-permute-start(bf16[128,2048]{1,0:T(8,128)(2,1)} %get-tuple-element.121), channel_id=1, source_target_pairs={{0,1},{1,2},{2,3},{3,0},{4,5},{5,6},{6,7},{7,4},{8,9},{9,10},{10,1... | collective-permute-start | bytes 1572872 | tf_op jit(solution)/shard_map/ppermute | solution.py:57
  442.7 36.1 %collective-permute-start.27 = (bf16[128,2048]{1,0:T(8,128)(2,1)}, bf16[128,2048]{1,0:T(8,128)(2,1)}, u32[]{:S(2)}, u32[]{:S(2)}) collective-permute-start(bf16[128,2048]{1,0:T(8,128)(2,1)} %get-tuple-element.121), channel_id=1, source_target_pairs={{0,2},{1,3},{2,0},{3,1},{4,6},{5,7},{6,4},{7,5},{8,10},{9,11},{10,... | collective-permute-start | bytes 1572872 | tf_op jit(solution)/shard_map/ppermute | solution.py:57
  444.1 34.8 %collective-permute-start.28 = (bf16[128,2048]{1,0:T(8,128)(2,1)}, bf16[128,2048]{1,0:T(8,128)(2,1)}, u32[]{:S(2)}, u32[]{:S(2)}) collective-permute-start(bf16[128,2048]{1,0:T(8,128)(2,1)} %get-tuple-element.121), channel_id=1, source_target_pairs={{0,3},{1,0},{2,1},{3,2},{4,7},{5,4},{6,5},{7,6},{8,11},{9,8},{10,9... | collective-permute-start | bytes 1572872 | tf_op jit(solution)/shard_map/ppermute | solution.py:57
  446.7 107.2 %collective-permute-start.33 = (bf16[1056,1024]{1,0:T(8,128)(2,1)}, bf16[1056,1024]{1,0:T(8,128)(2,1)}, u32[]{:S(2)}, u32[]{:S(2)}) collective-permute-start(bf16[1056,1024]{1,0:T(8,128)(2,1)} %copy-done.16), channel_id=1, source_target_pairs={{0,16},{16,0},{1,17},{17,1},{2,18},{18,2},{3,19},{19,3},{4,20},{20... | collective-permute-start | bytes 6488072 | tf_op jit(solution)/shard_map/ppermute | solution.py:107
  502.8 156.5 %reduce-scatter.3.cloned.1.call-start = ((), (), s32[]{:S(2)}) async-start(), calls=%async_computation.8 | async-start | bytes 7667712 | tf_op jit(solution)/shard_map/reduce_scatter | solution.py:760
  523.9 30.1 %collective-permute-start.19 = (bf16[128,2048]{1,0:T(8,128)(2,1)}, bf16[128,2048]{1,0:T(8,128)(2,1)}, u32[]{:S(2)}, u32[]{:S(2)}) collective-permute-start(bf16[128,2048]{1,0:T(8,128)(2,1)} %get-tuple-element.203), channel_id=1, source_target_pairs={{0,3},{1,0},{2,1},{3,2},{4,7},{5,4},{6,5},{7,6},{8,11},{9,8},{10,9... | collective-permute-start | bytes 1572872 | tf_op jit(solution)/shard_map/ppermute | solution.py:57
  526.4 27.5 %collective-permute-start.21 = (bf16[128,2048]{1,0:T(8,128)(2,1)}, bf16[128,2048]{1,0:T(8,128)(2,1)}, u32[]{:S(2)}, u32[]{:S(2)}) collective-permute-start(bf16[128,2048]{1,0:T(8,128)(2,1)} %get-tuple-element.204), channel_id=1, source_target_pairs={{0,1},{1,2},{2,3},{3,0},{4,5},{5,6},{6,7},{7,4},{8,9},{9,10},{10,1... | collective-permute-start | bytes 1572872 | tf_op jit(solution)/shard_map/ppermute | solution.py:57
  554.0 91.5 %collective-permute-start.37 = (bf16[704,2048]{1,0:T(8,128)(2,1)}, bf16[704,2048]{1,0:T(8,128)(2,1)}, u32[]{:S(2)}, u32[]{:S(2)}) collective-permute-start(bf16[704,2048]{1,0:T(8,128)(2,1)} %copy-done.5), channel_id=1, source_target_pairs={{0,16},{16,0},{1,17},{17,1},{2,18},{18,2},{3,19},{19,3},{4,20},{20... | collective-permute-start | bytes 8650760 | tf_op jit(solution)/shard_map/ppermute | solution.py:107
  560.4 41.8 %all-to-all-start.2 = ((bf16[4,1056,256]{2,1,0:T(8,128)(2,1)}), bf16[4,1056,256]{2,1,0:T(8,128)(2,1)}, u32[]{:S(2)}, u32[]{:S(2)}) async-start(bf16[4,1056,256]{2,1,0:T(8,128)(2,1)} %bitcast.167), calls=%async_computation.4 | async-start | bytes 4325376 | tf_op jit(solution)/shard_map/all_to_all | solution.py:719
  571.1 71.7 %collective-permute-start.20 = (bf16[128,2048]{1,0:T(8,128)(2,1)}, bf16[128,2048]{1,0:T(8,128)(2,1)}, u32[]{:S(2)}, u32[]{:S(2)}) collective-permute-start(bf16[128,2048]{1,0:T(8,128)(2,1)} %get-tuple-element.205), channel_id=1, source_target_pairs={{0,2},{1,3},{2,0},{3,1},{4,6},{5,7},{6,4},{7,5},{8,10},{9,11},{10,... | collective-permute-start | bytes 1572872 | tf_op jit(solution)/shard_map/ppermute | solution.py:57
  573.2 38.7 %collective-permute-start.30 = (bf16[128,2048]{1,0:T(8,128)(2,1)}, bf16[128,2048]{1,0:T(8,128)(2,1)}, u32[]{:S(2)}, u32[]{:S(2)}) collective-permute-start(bf16[128,2048]{1,0:T(8,128)(2,1)} %get-tuple-element.243), channel_id=1, source_target_pairs={{0,3},{1,0},{2,1},{3,2},{4,7},{5,4},{6,5},{7,6},{8,11},{9,8},{10,9... | collective-permute-start | bytes 1572872 | tf_op jit(solution)/shard_map/ppermute | solution.py:57
  576.1 66.8 %collective-permute-start.31 = (bf16[128,2048]{1,0:T(8,128)(2,1)}, bf16[128,2048]{1,0:T(8,128)(2,1)}, u32[]{:S(2)}, u32[]{:S(2)}) collective-permute-start(bf16[128,2048]{1,0:T(8,128)(2,1)} %get-tuple-element.242), channel_id=1, source_target_pairs={{0,2},{1,3},{2,0},{3,1},{4,6},{5,7},{6,4},{7,5},{8,10},{9,11},{10,... | collective-permute-start | bytes 1572872 | tf_op jit(solution)/shard_map/ppermute | solution.py:57
  578.1 64.8 %collective-permute-start.32 = (bf16[128,2048]{1,0:T(8,128)(2,1)}, bf16[128,2048]{1,0:T(8,128)(2,1)}, u32[]{:S(2)}, u32[]{:S(2)}) collective-permute-start(bf16[128,2048]{1,0:T(8,128)(2,1)} %get-tuple-element.241), channel_id=1, source_target_pairs={{0,1},{1,2},{2,3},{3,0},{4,5},{5,6},{6,7},{7,4},{8,9},{9,10},{10,1... | collective-permute-start | bytes 1572872 | tf_op jit(solution)/shard_map/ppermute | solution.py:57
  660.7 8.0 %collective-permute-start.34 = (f32[11,256]{1,0:T(8,128)S(1)}, f32[11,256]{1,0:T(8,128)S(1)}, u32[]{:S(2)}, u32[]{:S(2)}) collective-permute-start(f32[11,256]{1,0:T(8,128)S(1)} %slice_bitcast_fusion.7), channel_id=1, source_target_pairs={{0,3},{1,0},{2,1},{3,2},{4,7},{5,4},{6,5},{7,6},{8,11},{9,8},{10,9... | collective-permute-start | bytes 33800 | tf_op jit(solution)/shard_map/ppermute | solution.py:57
  664.3 4.6 collective-permute-start.35
  664.3 5.5 collective-permute-start.36
  (63 other events, 613.5 us)
Sparse Core Ops, SparseCore 0:
  16.4 51.6 all-gather.3
  73.8 33.0 all-gather.5
  179.7 73.0 all-gather.7
  502.9 46.1 reduce-scatter.4
  554.1 91.6 reduce-scatter.2

commit v5 on v4

--- a/solution.py
+++ b/solution.py
@@ -437,6 +437,8 @@
     dense_own = jnp.concatenate(
         [query_weight, key_weight, value_weight, small], axis=1
     )
+    input_blocks = gather_blocks(layer_input, "tp")
+    dense_own = after(dense_own, input_blocks[1])
     dense_full = lax.all_gather(dense_own, ("dp", "ep"), axis=0, tiled=True)
     in_weight = dense_full[:, : 3 * head_cols]
     small_full = dense_full[:, 3 * head_cols :]
@@ -466,7 +468,6 @@
         named = named | (lanes == span_routes[:, k : k + 1].astype(jnp.int32))
     span_mask = (named & span_keep).astype(BF16)
 
-    input_blocks = gather_blocks(layer_input, "tp")
     grad_blocks = gather_blocks(after(cotangent, input_blocks), "tp")
     input_values = jnp.concatenate(input_blocks, axis=0)
 

time: 689 us -> 691 us (level)
    all_gather x1, waiting for transfers between devices: 0.02 us -> 7.67 us  [body(): dense_full = lax.all_gather(dense_own, ('dp', 'ep'), axis=0, tiled=True)]
    unnamed x156 -> x160, local copies, waits for them, and re-layouts: 45.8 us -> 45.5 us
  transfers between devices with their start and end apart: 46 -> 46, of which waited for: 18 -> 20; matrix products, arithmetic and copies ran while one was open for 33% -> 34% of each run, Pallas kernels for 8% -> 8%
where the time goes in v5:
time: 691 us; the launch traced here: 680 us
  waiting for transfers between devices  229 us (33%)
  Pallas kernels  97.6 us (14%)
  matrix products  94.6 us (14%)
  other arithmetic  89.3 us (13%)
  local copies, waits for them, and re-layouts  84.6 us (12%)
  starting transfers between devices  68.7 us (10%)
  between operations  15.4 us (2%)
    ppermute x24, waiting for transfers between devices, shifted(): lax.ppermute(block, axis, [(i, (i + step) % count) for i in range(count)])  123 us
    pallas_call x2, Pallas kernels, run_experts(): pl.pallas_call(lambda *refs: expert_kernel(tp_count, expert_count, *refs)...  85.8 us
    dot_general x4, matrix products, dot_tn(): lax.dot_general(left, right, (((0,), (0,)), ((), ())), preferred_element_...  50.5 us
    unnamed x160, local copies, waits for them, and re-layouts  45.5 us
    ppermute x24, starting transfers between devices, shifted(): lax.ppermute(block, axis, [(i, (i + step) % count) for i in range(count)])  45.4 us
    all_gather x1, waiting for transfers between devices, body(): lax.all_gather(middle_normed, ('ep', 'tp'), axis=0, tiled=True)  33 us
    ppermute x14, waiting for transfers between devices, swapped(): return lax.ppermute(values, axis, [(i, i ^ bit) for i in range(count)])  28.3 us
    dot_general x4, matrix products, dot_nn(): lax.dot_general(left, right, (((1,), (0,)), ((), ())), preferred_element_...  23 us
  transfers between devices with their start and end apart: 46, of which 20 were waited for; matrix products, arithmetic and copies ran while one was open for 34% of the time, Pallas kernels for 8%

profile of v5, /device:TPU:0, one launch (start us, length us, event | category | flops | bytes accessed | tf_op | source)
XLA Modules:
  0.0 679.7 jit_solution(4469145431678941628)
XLA Ops:
  7.3 3.1 collective-permute-start
  19.2 5.3 collective-permute-done
  32.9 16.3 %collective-permute-done.1 = bf16[128,2048]{1,0:T(8,128)(2,1)} collective-permute-done((bf16[128,2048]{1,0:T(8,128)(2,1)}, bf16[128,2048]{1,0:T(8,128)(2,1)}, u32[]{:S(2)}, u32[]{:S(2)}) %collective-permute-start.1) | collective-permute-done | bytes 524320 | tf_op jit(solution)/shard_map/ppermute | solution.py:57
  49.4 11.4 %collective-permute-start.6 = (bf16[128,2048]{1,0:T(8,128)(2,1)S(1)}, bf16[128,2048]{1,0:T(8,128)(2,1)}, u32[]{:S(2)}, u32[]{:S(2)}) collective-permute-start(bf16[128,2048]{1,0:T(8,128)(2,1)S(1)} %copy-done.12), channel_id=1, source_target_pairs={{0,1},{1,2},{2,3},{3,0},{4,5},{5,6},{6,7},{7,4},{8,9},{9,10},{10,1... | collective-permute-start | bytes 1572872 | tf_op jit(solution)/shard_map/ppermute | solution.py:57
  65.4 7.7 %all-gather.4.cloned.1.call-done = bf16[2048,1664]{0,1:T(8,128)(2,1)} async-done(((bf16[256,1664]{0,1:T(8,128)(2,1)}), bf16[2048,1664]{0,1:T(8,128)(2,1)}) %all-gather.4.cloned.1.call-update) | async-done | bytes 6815760 | tf_op jit(solution)/shard_map/all_gather | solution.py:442
  75.0 5.7 fusion.10
  86.2 4.5 all-to-all-start
  97.8 10.7 %all-gather.6.cloned.1.call-done = bf16[512,2048]{1,0:T(8,128)(2,1)} async-done(((bf16[512,256]{1,0:T(8,128)(2,1)}), bf16[512,2048]{1,0:T(8,128)(2,1)}) %all-gather.6.cloned.1.call-update) | async-done | bytes 2097168 | tf_op jit(solution)/shard_map/all_gather | solution.py:445
  113.9 8.8 %all-to-all-done = bf16[4,1056,256]{2,1,0:T(8,128)(2,1)} async-done(((bf16[4,1056,256]{2,1,0:T(8,128)(2,1)}), bf16[4,1056,256]{2,1,0:T(8,128)(2,1)}, u32[]{:S(2)}, u32[]{:S(2)}) %all-to-all-start) | async-done | bytes 2162720 | tf_op jit(solution)/shard_map/all_to_all | solution.py:481
  126.9 3.8 collective-permute-start.3
  135.9 7.5 %collective-permute-done.3 = bf16[128,2048]{1,0:T(8,128)(2,1)S(1)} collective-permute-done((bf16[128,2048]{1,0:T(8,128)(2,1)}, bf16[128,2048]{1,0:T(8,128)(2,1)S(1)}, u32[]{:S(2)}, u32[]{:S(2)}) %collective-permute-start.3) | collective-permute-done | bytes 524320 | tf_op jit(solution)/shard_map/ppermute | solution.py:57
  143.4 31.9 %collective-permute-done.4 = bf16[128,2048]{1,0:T(8,128)(2,1)S(1)} collective-permute-done((bf16[128,2048]{1,0:T(8,128)(2,1)}, bf16[128,2048]{1,0:T(8,128)(2,1)S(1)}, u32[]{:S(2)}, u32[]{:S(2)}) %collective-permute-start.4) | collective-permute-done | bytes 524320 | tf_op jit(solution)/shard_map/ppermute | solution.py:57
  194.6 4.0 fusion.27.refs_3_
  215.2 3.3 order_rows.1.refs_2_
  218.5 3.2 copy-done.3
  221.7 33.0 %all-gather.8.cloned.1.call-done.refs_1_ = bf16[2048,2048]{1,0:T(8,128)(2,1)} async-done(((bf16[128,2048]{1,0:T(8,128)(2,1)}), bf16[2048,2048]{1,0:T(8,128)(2,1)}) %all-gather.8.cloned.1.call-update) | async-done | bytes 8388624 | tf_op jit(solution)/shard_map/all_gather | solution.py:546
  254.7 43.0 %experts.2 = (bf16[512,2176]{1,0:T(8,128)(2,1)}, bf16[512,2176]{1,0:T(8,128)(2,1)}, bf16[2048,2304]{1,0:T(8,128)(2,1)}, bf16[2048,1152]{1,0:T(8,128)(2,1)}) custom-call(s32[3]{0:T(128)} %add_add_fusion.1.refs_0_, bf16[2048,2048]{1,0:T(8,128)(2,1)} %all-gather.8.cloned.1.call-done.refs_1_, bf16[2048,2048]{1,0:T(8,128)(2,1)} %copy-done.3, ...), custom_call_target="tpu_custom_call" | custom-call | flops 24159191040 | bytes 33816576 | tf_op jit(solution)/shard_map/experts/pallas_call | solution.py:327
  298.0 4.3 collective-permute-done.13
  302.3 3.6 add_convert_fusion
  307.0 42.8 %experts.3 = (bf16[512,2176]{1,0:T(8,128)(2,1)}, bf16[512,2176]{1,0:T(8,128)(2,1)}, bf16[2048,2304]{1,0:T(8,128)(2,1)}, bf16[2048,1152]{1,0:T(8,128)(2,1)}) custom-call(s32[3]{0:T(128)} %add_add_fusion.2.refs_0_, bf16[2048,2048]{1,0:T(8,128)(2,1)} %all-gather.8.cloned.1.call-done.refs_1_, ...), custom_call_target="tpu_custom_call", output_to_operand_aliasing={{2}: (8, {}), {3}: (9, {})} | custom-call | flops 24159191040 | bytes 33816576 | tf_op jit(solution)/shard_map/experts/pallas_call | solution.py:327
  352.7 14.0 %convolution_convert_fusion.3.refs_0_.refs_1_ = bf16[1152,2048]{1,0:T(8,128)(2,1)S(1)} fusion(bf16[2048,1152]{1,0:T(8,128)(2,1)} %get-tuple-element.112, bf16[2048,2048]{1,0:T(8,128)(2,1)} %copy-done.3), kind=kOutput, calls=%fused_computation.12 | convolution fusion | flops 9666035712 | bytes 17825792 | tf_op jit(solution)/shard_map/dot_general | solution.py:26
  375.4 24.6 %convolution_convert_fusion.refs_0_ = bf16[2304,2048]{1,0:T(8,128)(2,1)} fusion(bf16[2048,2304]{1,0:T(8,128)(2,1)} %get-tuple-element.109, bf16[2048,2048]{1,0:T(8,128)(2,1)S(1)} %bitcast.209), kind=kOutput, calls=%fused_computation.3 | convolution fusion | flops 19332071424 | bytes 27262976 | tf_op jit(solution)/shard_map/dot_general | solution.py:26
  400.0 3.7 copy-done.2
  403.7 3.9 first_rows.1
  408.2 12.9 %convolution_convert_fusion.2 = bf16[2048,2048]{1,0:T(8,128)(2,1)} fusion(bf16[2048,1152]{1,0:T(8,128)(2,1)S(1)} %bitcast.213, bf16[1152,2048]{1,0:T(8,128)(2,1)S(1)} %bitcast.181), kind=kOutput, calls=%fused_computation.11 | convolution fusion | flops 9667870720 | bytes 17825792 | tf_op jit(solution)/shard_map/dot_general | solution.py:18
  421.1 5.6 all-to-all-start.1
  426.8 6.7 collective-permute-done.25
  438.3 3.4 own_rows.1
  451.0 9.8 %collective-permute-done.26 = bf16[128,2048]{1,0:T(8,128)(2,1)} collective-permute-done((bf16[128,2048]{1,0:T(8,128)(2,1)}, bf16[128,2048]{1,0:T(8,128)(2,1)}, u32[]{:S(2)}, u32[]{:S(2)}) %collective-permute-start.26) | collective-permute-done | bytes 524320 | tf_op jit(solution)/shard_map/ppermute | solution.py:57
  460.8 19.9 %collective-permute-done.27 = bf16[128,2048]{1,0:T(8,128)(2,1)} collective-permute-done((bf16[128,2048]{1,0:T(8,128)(2,1)}, bf16[128,2048]{1,0:T(8,128)(2,1)}, u32[]{:S(2)}, u32[]{:S(2)}) %collective-permute-start.27) | collective-permute-done | bytes 524320 | tf_op jit(solution)/shard_map/ppermute | solution.py:57
  480.7 14.6 %collective-permute-done.29 = bf16[704,2048]{1,0:T(8,128)(2,1)} collective-permute-done((bf16[704,2048]{1,0:T(8,128)(2,1)}, bf16[704,2048]{1,0:T(8,128)(2,1)}, u32[]{:S(2)}, u32[]{:S(2)}) %collective-permute-start.29) | collective-permute-done | bytes 2883616 | tf_op jit(solution)/shard_map/ppermute | solution.py:107
  500.9 3.6 convolution_convert_fusion.4
  504.7 3.7 convolution_convert_fusion.6
  519.9 5.7 dynamic-slice_reduce_fusion.2
  528.5 3.1 convert_reduce_fusion
  531.6 8.3 %multiply_reduce_fusion = (f32[2048]{0:T(1024)S(1)}, bf16[512,2048]{1,0:T(8,128)(2,1)}, f32[512,2048]{1,0:T(8,128)}) fusion(f32[512]{0:T(512)S(1)} %copy-done.55, bf16[512,2048]{1,0:T(8,128)(2,1)S(1)} %copy-done.20, bf16[512,1536]{0,1:T(8,128)(2,1)S(1)} %copy-done.26, bf16[2048,1664]{0,1:T(8,128)(2,1)} %all-gather.4.cloned.1.call-done), kind=kOutput, calls=%fused_computation.27 | convolution fusion | flops 3226466304 | bytes 16263168 | tf_op jit(solution)/shard_map/dot_general | solution.py:22
  540.6 8.3 %convolution_convert_fusion.1 = bf16[2048,1536]{0,1:T(8,128)(2,1)} fusion(bf16[512,1536]{0,1:T(8,128)(2,1)} %pad_maximum_fusion.4, f32[2048]{0:T(1024)S(1)} %bitcast.194, f32[512]{0:T(512)S(1)} %copy-done.55, bf16[512,2048]{1,0:T(8,128)(2,1)} %copy-done.19), kind=kOutput, calls=%fused_computation.10 | convolution fusion | flops 3228565504 | bytes 9971712 | tf_op jit(solution)/shard_map/dot_general | solution.py:26
  548.9 6.9 %pad_maximum_fusion = bf16[2048,1664]{0,1:T(8,128)(2,1)} fusion(bf16[2048,128]{0,1:T(8,128)(2,1)S(1)} %fusion.32, bf16[2048,1536]{0,1:T(8,128)(2,1)} %convolution_convert_fusion.1), kind=kLoop, calls=%fused_computation.13 | loop fusion | flops 13631488 | bytes 13631488 | tf_op jit(solution)/shard_map/concatenate | solution.py:751
  557.5 3.3 add_convert_fusion.1
  562.2 4.6 all-to-all-start.2
  566.9 6.1 convert_add_fusion.2
  580.1 7.4 %convert_add_fusion.1 = f32[704,2048]{1,0:T(8,128)} fusion(bf16[704,2048]{1,0:T(8,128)(2,1)} %collective-permute-done.29, bf16[704,2048]{1,0:T(8,128)(2,1)} %get-tuple-element.110), kind=kLoop, calls=%fused_computation.15 | loop fusion | flops 4325376 | bytes 11534336 | tf_op jit(solution)/shard_map/add | solution.py:101
  587.5 16.5 %all-to-all-done.2 = bf16[4,1056,256]{2,1,0:T(8,128)(2,1)} async-done(((bf16[4,1056,256]{2,1,0:T(8,128)(2,1)}), bf16[4,1056,256]{2,1,0:T(8,128)(2,1)}, u32[]{:S(2)}, u32[]{:S(2)}) %all-to-all-start.2) | async-done | bytes 2162720 | tf_op jit(solution)/shard_map/all_to_all | solution.py:720
  604.0 3.5 fusion.70
  613.8 30.9 %collective-permute-done.31 = bf16[128,2048]{1,0:T(8,128)(2,1)} collective-permute-done((bf16[128,2048]{1,0:T(8,128)(2,1)}, bf16[128,2048]{1,0:T(8,128)(2,1)}, u32[]{:S(2)}, u32[]{:S(2)}) %collective-permute-start.31) | collective-permute-done | bytes 524320 | tf_op jit(solution)/shard_map/ppermute | solution.py:57
  652.4 3.5 multiply_add_fusion
  655.9 5.3 convert_add_fusion
  662.6 3.6 collective-permute-start.34
  (361 shorter events, 167.3 us)
Async XLA Ops:
  7.2 124.6 %copy-start = (s32[8]{0:T(128)S(1)}, s32[8]{0:T(128)}, u32[]{:S(2)}) copy-start(s32[8]{0:T(128)} %param.23) | copy-start | bytes 100
  7.2 65.8 %all-gather.4.cloned.1.call-start = ((), (), s32[]{:S(2)}) async-start(), calls=%async_computation.5 | async-start | bytes 7667712 | tf_op jit(solution)/shard_map/all_gather | solution.py:442
  7.3 17.2 %collective-permute-start = (bf16[128,2048]{1,0:T(8,128)(2,1)}, bf16[128,2048]{1,0:T(8,128)(2,1)S(1)}, u32[]{:S(2)}, u32[]{:S(2)}) collective-permute-start(bf16[128,2048]{1,0:T(8,128)(2,1)} %param.21), channel_id=1, source_target_pairs={{0,1},{1,2},{2,3},{3,0},{4,5},{5,6},{6,7},{7,4},{8,9},{9,10},{10,1... | collective-permute-start | bytes 1572872 | tf_op jit(solution)/shard_map/ppermute | solution.py:57
  24.5 84.0 %all-gather.6.cloned.1.call-start = ((), (), s32[]{:S(2)}) async-start(), calls=%async_computation.6 | async-start | bytes 2359296 | tf_op jit(solution)/shard_map/all_gather | solution.py:445
  24.6 24.6 %collective-permute-start.1 = (bf16[128,2048]{1,0:T(8,128)(2,1)}, bf16[128,2048]{1,0:T(8,128)(2,1)}, u32[]{:S(2)}, u32[]{:S(2)}) collective-permute-start(bf16[128,2048]{1,0:T(8,128)(2,1)} %param.21), channel_id=1, source_target_pairs={{0,2},{1,3},{2,0},{3,1},{4,6},{5,7},{6,4},{7,5},{8,10},{9,11},{10,... | collective-permute-start | bytes 1572872 | tf_op jit(solution)/shard_map/ppermute | solution.py:57
  25.4 24.1 %collective-permute-start.2 = (bf16[128,2048]{1,0:T(8,128)(2,1)}, bf16[128,2048]{1,0:T(8,128)(2,1)}, u32[]{:S(2)}, u32[]{:S(2)}) collective-permute-start(bf16[128,2048]{1,0:T(8,128)(2,1)} %param.21), channel_id=1, source_target_pairs={{0,3},{1,0},{2,1},{3,2},{4,7},{5,4},{6,5},{7,6},{8,11},{9,8},{10,9... | collective-permute-start | bytes 1572872 | tf_op jit(solution)/shard_map/ppermute | solution.py:57
  29.6 64.0 %copy-start.24 = (pred[512,512]{0,1:T(8,128)(4,1)}, pred[512,512]{0,1:T(8,128)(4,1)S(1)}, u32[]{:S(2)}) copy-start(pred[512,512]{0,1:T(8,128)(4,1)S(1)} %broadcast_compare_fusion) | copy-start | bytes 786436
  49.4 73.7 %collective-permute-start.6 = (bf16[128,2048]{1,0:T(8,128)(2,1)S(1)}, bf16[128,2048]{1,0:T(8,128)(2,1)}, u32[]{:S(2)}, u32[]{:S(2)}) collective-permute-start(bf16[128,2048]{1,0:T(8,128)(2,1)S(1)} %copy-done.12), channel_id=1, source_target_pairs={{0,1},{1,2},{2,3},{3,0},{4,5},{5,6},{6,7},{7,4},{8,9},{9,10},{10,1... | collective-permute-start | bytes 1572872 | tf_op jit(solution)/shard_map/ppermute | solution.py:57
  60.9 62.2 %collective-permute-start.7 = (bf16[128,2048]{1,0:T(8,128)(2,1)S(1)}, bf16[128,2048]{1,0:T(8,128)(2,1)}, u32[]{:S(2)}, u32[]{:S(2)}) collective-permute-start(bf16[128,2048]{1,0:T(8,128)(2,1)S(1)} %copy-done.12), channel_id=1, source_target_pairs={{0,2},{1,3},{2,0},{3,1},{4,6},{5,7},{6,4},{7,5},{8,10},{9,11},{10,... | collective-permute-start | bytes 1572872 | tf_op jit(solution)/shard_map/ppermute | solution.py:57
  63.3 59.8 %collective-permute-start.8 = (bf16[128,2048]{1,0:T(8,128)(2,1)S(1)}, bf16[128,2048]{1,0:T(8,128)(2,1)}, u32[]{:S(2)}, u32[]{:S(2)}) collective-permute-start(bf16[128,2048]{1,0:T(8,128)(2,1)S(1)} %copy-done.12), channel_id=1, source_target_pairs={{0,3},{1,0},{2,1},{3,2},{4,7},{5,4},{6,5},{7,6},{8,11},{9,8},{10,9... | collective-permute-start | bytes 1572872 | tf_op jit(solution)/shard_map/ppermute | solution.py:57
  86.2 36.6 %all-to-all-start = ((bf16[4,1056,256]{2,1,0:T(8,128)(2,1)}), bf16[4,1056,256]{2,1,0:T(8,128)(2,1)}, u32[]{:S(2)}, u32[]{:S(2)}) async-start(bf16[4,1056,256]{2,1,0:T(8,128)(2,1)} %pad_maximum_fusion.2), calls=%async_computation | async-start | bytes 4325376 | tf_op jit(solution)/shard_map/all_to_all | solution.py:481
  90.7 164.0 %all-gather.8.cloned.1.call-start = ((), (), s32[]{:S(2)}) async-start(), calls=%async_computation.7 | async-start | bytes 8912896 | tf_op jit(solution)/shard_map/all_gather | solution.py:546
  122.8 52.5 %collective-permute-start.10 = (bf16[4,1056,256]{2,1,0:T(8,128)(2,1)}, bf16[4,1056,256]{2,1,0:T(8,128)(2,1)}, u32[]{:S(2)}, u32[]{:S(2)}) collective-permute-start(bf16[4,1056,256]{2,1,0:T(8,128)(2,1)} %all-to-all-done), channel_id=1, source_target_pairs={{0,16},{16,0},{1,17},{17,1},{2,18},{18,2},{3,19},{19,3},{4,20},{20... | collective-permute-start | bytes 6488072 | tf_op jit(solution)/shard_map/ppermute | solution.py:107
  126.4 48.9 %collective-permute-start.9 = (bf16[512,2048]{1,0:T(8,128)(2,1)S(1)}, bf16[512,2048]{1,0:T(8,128)(2,1)}, u32[]{:S(2)}, u32[]{:S(2)}) collective-permute-start(bf16[512,2048]{1,0:T(8,128)(2,1)S(1)} %constant_dynamic-update-slice_fusion.refs_0_), channel_id=1, source_target_pairs={{0,8},{4,12},{8,0},{12,4},{1,9},{5,13},{9,1},{13,5},{2,10},{6,14},... | collective-permute-start | bytes 6291464 | tf_op jit(solution)/shard_map/ppermute | solution.py:107
  126.9 16.5 %collective-permute-start.3 = (bf16[128,2048]{1,0:T(8,128)(2,1)}, bf16[128,2048]{1,0:T(8,128)(2,1)S(1)}, u32[]{:S(2)}, u32[]{:S(2)}) collective-permute-start(bf16[128,2048]{1,0:T(8,128)(2,1)} %get-tuple-element.249), channel_id=1, source_target_pairs={{0,3},{1,0},{2,1},{3,2},{4,7},{5,4},{6,5},{7,6},{8,11},{9,8},{10,9... | collective-permute-start | bytes 1572872 | tf_op jit(solution)/shard_map/ppermute | solution.py:57
  130.6 44.7 %collective-permute-start.4 = (bf16[128,2048]{1,0:T(8,128)(2,1)}, bf16[128,2048]{1,0:T(8,128)(2,1)S(1)}, u32[]{:S(2)}, u32[]{:S(2)}) collective-permute-start(bf16[128,2048]{1,0:T(8,128)(2,1)} %get-tuple-element.248), channel_id=1, source_target_pairs={{0,2},{1,3},{2,0},{3,1},{4,6},{5,7},{6,4},{7,5},{8,10},{9,11},{10,... | collective-permute-start | bytes 1572872 | tf_op jit(solution)/shard_map/ppermute | solution.py:57
  130.6 44.7 %collective-permute-start.5 = (bf16[128,2048]{1,0:T(8,128)(2,1)}, bf16[128,2048]{1,0:T(8,128)(2,1)}, u32[]{:S(2)}, u32[]{:S(2)}) collective-permute-start(bf16[128,2048]{1,0:T(8,128)(2,1)} %get-tuple-element.247), channel_id=1, source_target_pairs={{0,1},{1,2},{2,3},{3,0},{4,5},{5,6},{6,7},{7,4},{8,9},{9,10},{10,1... | collective-permute-start | bytes 1572872 | tf_op jit(solution)/shard_map/ppermute | solution.py:57
  200.4 14.7 %collective-permute-start.11 = (bf16[512,2048]{1,0:T(8,128)(2,1)S(1)}, bf16[512,2048]{1,0:T(8,128)(2,1)}, u32[]{:S(2)}, u32[]{:S(2)}) collective-permute-start(bf16[512,2048]{1,0:T(8,128)(2,1)S(1)} %constant_dynamic-update-slice_fusion.refs_0_), channel_id=1, source_target_pairs={{0,4},{4,0},{8,12},{12,8},{1,5},{5,1},{9,13},{13,9},{2,6},{6,2},{1... | collective-permute-start | bytes 6291464 | tf_op jit(solution)/shard_map/ppermute | solution.py:107
  200.4 14.7 %collective-permute-start.12 = (bf16[512,2048]{1,0:T(8,128)(2,1)}, bf16[512,2048]{1,0:T(8,128)(2,1)}, u32[]{:S(2)}, u32[]{:S(2)}) collective-permute-start(bf16[512,2048]{1,0:T(8,128)(2,1)} %collective-permute-done.9.refs_2_), channel_id=1, source_target_pairs={{0,4},{4,0},{8,12},{12,8},{1,5},{5,1},{9,13},{13,9},{2,6},{6,2},{1... | collective-permute-start | bytes 6291464 | tf_op jit(solution)/shard_map/ppermute | solution.py:107
  297.7 4.6 collective-permute-start.13
  305.8 63.7 %collective-permute-start.18 = (bf16[512,2176]{1,0:T(8,128)(2,1)}, bf16[512,2176]{1,0:T(8,128)(2,1)S(1)}, u32[]{:S(2)}, u32[]{:S(2)}) collective-permute-start(bf16[512,2176]{1,0:T(8,128)(2,1)} %add_convert_fusion), channel_id=1, source_target_pairs={{0,8},{4,12},{8,0},{12,4},{1,9},{5,13},{9,1},{13,5},{2,10},{6,14},... | collective-permute-start | bytes 6684680 | tf_op jit(solution)/shard_map/ppermute | solution.py:107
  351.6 16.4 %collective-permute-start.14 = (bf16[128,2176]{1,0:T(8,128)(2,1)S(1)}, bf16[128,2176]{1,0:T(8,128)(2,1)S(1)}, u32[]{:S(2)}, u32[]{:S(2)}) collective-permute-start(bf16[128,2176]{1,0:T(8,128)(2,1)S(1)} %get-tuple-element.238), channel_id=1, source_target_pairs={{0,4},{4,0},{8,12},{12,8},{1,5},{5,1},{9,13},{13,9},{2,6},{6,2},{1... | collective-permute-start | bytes 1671176 | tf_op jit(solution)/shard_map/ppermute | solution.py:107
  351.7 17.9 %collective-permute-start.15 = (bf16[128,2176]{1,0:T(8,128)(2,1)S(1)}, bf16[128,2176]{1,0:T(8,128)(2,1)S(1)}, u32[]{:S(2)}, u32[]{:S(2)}) collective-permute-start(bf16[128,2176]{1,0:T(8,128)(2,1)S(1)} %get-tuple-element.237), channel_id=1, source_target_pairs={{0,4},{4,0},{8,12},{12,8},{1,5},{5,1},{9,13},{13,9},{2,6},{6,2},{1... | collective-permute-start | bytes 1671176 | tf_op jit(solution)/shard_map/ppermute | solution.py:107
  352.2 17.4 %collective-permute-start.16 = (bf16[128,2176]{1,0:T(8,128)(2,1)S(1)}, bf16[128,2176]{1,0:T(8,128)(2,1)S(1)}, u32[]{:S(2)}, u32[]{:S(2)}) collective-permute-start(bf16[128,2176]{1,0:T(8,128)(2,1)S(1)} %get-tuple-element.236), channel_id=1, source_target_pairs={{0,4},{4,0},{8,12},{12,8},{1,5},{5,1},{9,13},{13,9},{2,6},{6,2},{1... | collective-permute-start | bytes 1671176 | tf_op jit(solution)/shard_map/ppermute | solution.py:107
  352.3 17.3 %collective-permute-start.17 = (bf16[128,2176]{1,0:T(8,128)(2,1)S(1)}, bf16[128,2176]{1,0:T(8,128)(2,1)S(1)}, u32[]{:S(2)}, u32[]{:S(2)}) collective-permute-start(bf16[128,2176]{1,0:T(8,128)(2,1)S(1)} %get-tuple-element.235), channel_id=1, source_target_pairs={{0,4},{4,0},{8,12},{12,8},{1,5},{5,1},{9,13},{13,9},{2,6},{6,2},{1... | collective-permute-start | bytes 1671176 | tf_op jit(solution)/shard_map/ppermute | solution.py:107
  368.0 65.5 %collective-permute-start.25 = (bf16[704,2048]{1,0:T(8,128)(2,1)S(1)}, bf16[704,2048]{1,0:T(8,128)(2,1)}, u32[]{:S(2)}, u32[]{:S(2)}) collective-permute-start(bf16[704,2048]{1,0:T(8,128)(2,1)S(1)} %down_rows.1), channel_id=1, source_target_pairs={{0,16},{16,0},{1,17},{17,1},{2,18},{18,2},{3,19},{19,3},{4,20},{20... | collective-permute-start | bytes 8650760 | tf_op jit(solution)/shard_map/ppermute | solution.py:107
  371.8 55.0 %collective-permute-start.22 = (bf16[128,2176]{1,0:T(8,128)(2,1)}, bf16[128,2176]{1,0:T(8,128)(2,1)}, u32[]{:S(2)}, u32[]{:S(2)}) collective-permute-start(bf16[128,2176]{1,0:T(8,128)(2,1)} %get-tuple-element.218), channel_id=1, source_target_pairs={{0,3},{1,0},{2,1},{3,2},{4,7},{5,4},{6,5},{7,6},{8,11},{9,8},{10,9... | collective-permute-start | bytes 1671176 | tf_op jit(solution)/shard_map/ppermute | solution.py:57
  373.4 53.4 %collective-permute-start.23 = (bf16[128,2176]{1,0:T(8,128)(2,1)}, bf16[128,2176]{1,0:T(8,128)(2,1)}, u32[]{:S(2)}, u32[]{:S(2)}) collective-permute-start(bf16[128,2176]{1,0:T(8,128)(2,1)} %get-tuple-element.217), channel_id=1, source_target_pairs={{0,2},{1,3},{2,0},{3,1},{4,6},{5,7},{6,4},{7,5},{8,10},{9,11},{10,... | collective-permute-start | bytes 1671176 | tf_op jit(solution)/shard_map/ppermute | solution.py:57
  374.2 52.7 %collective-permute-start.24 = (bf16[128,2176]{1,0:T(8,128)(2,1)}, bf16[128,2176]{1,0:T(8,128)(2,1)}, u32[]{:S(2)}, u32[]{:S(2)}) collective-permute-start(bf16[128,2176]{1,0:T(8,128)(2,1)} %get-tuple-element.216), channel_id=1, source_target_pairs={{0,1},{1,2},{2,3},{3,0},{4,5},{5,6},{6,7},{7,4},{8,9},{9,10},{10,1... | collective-permute-start | bytes 1671176 | tf_op jit(solution)/shard_map/ppermute | solution.py:57
  407.6 87.7 %collective-permute-start.29 = (bf16[704,2048]{1,0:T(8,128)(2,1)}, bf16[704,2048]{1,0:T(8,128)(2,1)}, u32[]{:S(2)}, u32[]{:S(2)}) collective-permute-start(bf16[704,2048]{1,0:T(8,128)(2,1)} %get-tuple-element.110), channel_id=1, source_target_pairs={{0,16},{16,0},{1,17},{17,1},{2,18},{18,2},{3,19},{19,3},{4,20},{20... | collective-permute-start | bytes 8650760 | tf_op jit(solution)/shard_map/ppermute | solution.py:107
  421.1 98.8 %all-to-all-start.1 = ((bf16[4,512,2048]{2,1,0:T(8,128)(2,1)}), bf16[4,512,2048]{2,1,0:T(8,128)(2,1)}, u32[]{:S(2)}, u32[]{:S(2)}) async-start(bf16[4,512,2048]{2,1,0:T(8,128)(2,1)} %bitcast.168), calls=%async_computation.1 | async-start | bytes 16777216 | tf_op jit(solution)/shard_map/all_to_all | solution.py:654
  426.7 185.2 %reduce-scatter.5.cloned.1.call-start = ((), (), s32[]{:S(2)}) async-start(), calls=%async_computation.9 | async-start | bytes 2359296 | tf_op jit(solution)/shard_map/reduce_scatter | solution.py:680
  443.7 17.1 %collective-permute-start.26 = (bf16[128,2048]{1,0:T(8,128)(2,1)}, bf16[128,2048]{1,0:T(8,128)(2,1)}, u32[]{:S(2)}, u32[]{:S(2)}) collective-permute-start(bf16[128,2048]{1,0:T(8,128)(2,1)} %get-tuple-element.123), channel_id=1, source_target_pairs={{0,1},{1,2},{2,3},{3,0},{4,5},{5,6},{6,7},{7,4},{8,9},{9,10},{10,1... | collective-permute-start | bytes 1572872 | tf_op jit(solution)/shard_map/ppermute | solution.py:57
  444.6 36.1 %collective-permute-start.27 = (bf16[128,2048]{1,0:T(8,128)(2,1)}, bf16[128,2048]{1,0:T(8,128)(2,1)}, u32[]{:S(2)}, u32[]{:S(2)}) collective-permute-start(bf16[128,2048]{1,0:T(8,128)(2,1)} %get-tuple-element.123), channel_id=1, source_target_pairs={{0,2},{1,3},{2,0},{3,1},{4,6},{5,7},{6,4},{7,5},{8,10},{9,11},{10,... | collective-permute-start | bytes 1572872 | tf_op jit(solution)/shard_map/ppermute | solution.py:57
  445.9 34.8 %collective-permute-start.28 = (bf16[128,2048]{1,0:T(8,128)(2,1)}, bf16[128,2048]{1,0:T(8,128)(2,1)}, u32[]{:S(2)}, u32[]{:S(2)}) collective-permute-start(bf16[128,2048]{1,0:T(8,128)(2,1)} %get-tuple-element.123), channel_id=1, source_target_pairs={{0,3},{1,0},{2,1},{3,2},{4,7},{5,4},{6,5},{7,6},{8,11},{9,8},{10,9... | collective-permute-start | bytes 1572872 | tf_op jit(solution)/shard_map/ppermute | solution.py:57
  448.5 107.3 %collective-permute-start.33 = (bf16[1056,1024]{1,0:T(8,128)(2,1)}, bf16[1056,1024]{1,0:T(8,128)(2,1)}, u32[]{:S(2)}, u32[]{:S(2)}) collective-permute-start(bf16[1056,1024]{1,0:T(8,128)(2,1)} %copy-done.16), channel_id=1, source_target_pairs={{0,16},{16,0},{1,17},{17,1},{2,18},{18,2},{3,19},{19,3},{4,20},{20... | collective-permute-start | bytes 6488072 | tf_op jit(solution)/shard_map/ppermute | solution.py:107
  504.6 156.6 %reduce-scatter.3.cloned.1.call-start = ((), (), s32[]{:S(2)}) async-start(), calls=%async_computation.8 | async-start | bytes 7667712 | tf_op jit(solution)/shard_map/reduce_scatter | solution.py:761
  525.7 30.2 %collective-permute-start.19 = (bf16[128,2048]{1,0:T(8,128)(2,1)}, bf16[128,2048]{1,0:T(8,128)(2,1)}, u32[]{:S(2)}, u32[]{:S(2)}) collective-permute-start(bf16[128,2048]{1,0:T(8,128)(2,1)} %get-tuple-element.205), channel_id=1, source_target_pairs={{0,3},{1,0},{2,1},{3,2},{4,7},{5,4},{6,5},{7,6},{8,11},{9,8},{10,9... | collective-permute-start | bytes 1572872 | tf_op jit(solution)/shard_map/ppermute | solution.py:57
  528.3 27.5 %collective-permute-start.21 = (bf16[128,2048]{1,0:T(8,128)(2,1)}, bf16[128,2048]{1,0:T(8,128)(2,1)}, u32[]{:S(2)}, u32[]{:S(2)}) collective-permute-start(bf16[128,2048]{1,0:T(8,128)(2,1)} %get-tuple-element.206), channel_id=1, source_target_pairs={{0,1},{1,2},{2,3},{3,0},{4,5},{5,6},{6,7},{7,4},{8,9},{9,10},{10,1... | collective-permute-start | bytes 1572872 | tf_op jit(solution)/shard_map/ppermute | solution.py:57
  555.9 91.5 %collective-permute-start.37 = (bf16[704,2048]{1,0:T(8,128)(2,1)}, bf16[704,2048]{1,0:T(8,128)(2,1)}, u32[]{:S(2)}, u32[]{:S(2)}) collective-permute-start(bf16[704,2048]{1,0:T(8,128)(2,1)} %copy-done.5), channel_id=1, source_target_pairs={{0,16},{16,0},{1,17},{17,1},{2,18},{18,2},{3,19},{19,3},{4,20},{20... | collective-permute-start | bytes 8650760 | tf_op jit(solution)/shard_map/ppermute | solution.py:107
  562.2 41.8 %all-to-all-start.2 = ((bf16[4,1056,256]{2,1,0:T(8,128)(2,1)}), bf16[4,1056,256]{2,1,0:T(8,128)(2,1)}, u32[]{:S(2)}, u32[]{:S(2)}) async-start(bf16[4,1056,256]{2,1,0:T(8,128)(2,1)} %bitcast.167), calls=%async_computation.4 | async-start | bytes 4325376 | tf_op jit(solution)/shard_map/all_to_all | solution.py:720
  572.9 71.7 %collective-permute-start.20 = (bf16[128,2048]{1,0:T(8,128)(2,1)}, bf16[128,2048]{1,0:T(8,128)(2,1)}, u32[]{:S(2)}, u32[]{:S(2)}) collective-permute-start(bf16[128,2048]{1,0:T(8,128)(2,1)} %get-tuple-element.207), channel_id=1, source_target_pairs={{0,2},{1,3},{2,0},{3,1},{4,6},{5,7},{6,4},{7,5},{8,10},{9,11},{10,... | collective-permute-start | bytes 1572872 | tf_op jit(solution)/shard_map/ppermute | solution.py:57
  575.0 38.7 %collective-permute-start.30 = (bf16[128,2048]{1,0:T(8,128)(2,1)}, bf16[128,2048]{1,0:T(8,128)(2,1)}, u32[]{:S(2)}, u32[]{:S(2)}) collective-permute-start(bf16[128,2048]{1,0:T(8,128)(2,1)} %get-tuple-element.245), channel_id=1, source_target_pairs={{0,3},{1,0},{2,1},{3,2},{4,7},{5,4},{6,5},{7,6},{8,11},{9,8},{10,9... | collective-permute-start | bytes 1572872 | tf_op jit(solution)/shard_map/ppermute | solution.py:57
  577.9 66.8 %collective-permute-start.31 = (bf16[128,2048]{1,0:T(8,128)(2,1)}, bf16[128,2048]{1,0:T(8,128)(2,1)}, u32[]{:S(2)}, u32[]{:S(2)}) collective-permute-start(bf16[128,2048]{1,0:T(8,128)(2,1)} %get-tuple-element.244), channel_id=1, source_target_pairs={{0,2},{1,3},{2,0},{3,1},{4,6},{5,7},{6,4},{7,5},{8,10},{9,11},{10,... | collective-permute-start | bytes 1572872 | tf_op jit(solution)/shard_map/ppermute | solution.py:57
  579.9 64.7 %collective-permute-start.32 = (bf16[128,2048]{1,0:T(8,128)(2,1)}, bf16[128,2048]{1,0:T(8,128)(2,1)}, u32[]{:S(2)}, u32[]{:S(2)}) collective-permute-start(bf16[128,2048]{1,0:T(8,128)(2,1)} %get-tuple-element.243), channel_id=1, source_target_pairs={{0,1},{1,2},{2,3},{3,0},{4,5},{5,6},{6,7},{7,4},{8,9},{9,10},{10,1... | collective-permute-start | bytes 1572872 | tf_op jit(solution)/shard_map/ppermute | solution.py:57
  662.6 8.0 %collective-permute-start.34 = (f32[11,256]{1,0:T(8,128)S(1)}, f32[11,256]{1,0:T(8,128)S(1)}, u32[]{:S(2)}, u32[]{:S(2)}) collective-permute-start(f32[11,256]{1,0:T(8,128)S(1)} %slice_bitcast_fusion.7), channel_id=1, source_target_pairs={{0,3},{1,0},{2,1},{3,2},{4,7},{5,4},{6,5},{7,6},{8,11},{9,8},{10,9... | collective-permute-start | bytes 33800 | tf_op jit(solution)/shard_map/ppermute | solution.py:57
  666.2 4.6 collective-permute-start.35
  666.2 5.5 collective-permute-start.36
  (65 other events, 663.6 us)
Sparse Core Ops, SparseCore 0:
  24.7 48.3 all-gather.3
  74.9 33.5 all-gather.5
  179.4 75.2 all-gather.7
  504.7 46.1 reduce-scatter.4
  556.0 91.6 reduce-scatter.2
